TPU v7x, 256 devices: a whole 4x4x8 slice. The times are simulated.
256 devices in a mesh: row: 32 (over z, y_lo, core), col: 8 (over y_hi, x).
Axes of the slice: x: 4, y: 4 (y_hi: 2, y_lo: 2; y = y_hi * 2 + y_lo), z: 8, core: 2. Of those that a mesh axis runs over, the one named last changes fastest.
Arguments:
- source: float32 [8192, 8192], P('row', 'col'), may hold values from 0.25 to 4
- boxes_a: float32 [32, 32, 512, 512], P('row', 'col'), may hold values from 0.25 to 4
- shifts_a: int32 [32, 32, 2], P('row', 'col'), may hold values from -128 to -1
- widths_a: int32 [32, 32, 2], P('row', 'col'), may hold values from 256 to 512
- boxes_b: float32 [32, 32, 512, 512], P('row', 'col'), may hold values from 0.25 to 4
- shifts_b: int32 [32, 32, 2], P('row', 'col'), may hold values from -128 to -1
- widths_b: int32 [32, 32, 2], P('row', 'col'), may hold values from 256 to 512
Outputs:
- smoothed: float32 [8192, 8192], P('row', 'col')
Inputs may be any that keep to these rules, and one draw needn't show every extreme that they name: `shifts_a`: first entry: rows, second: columns. `widths_a`: first entry: rows, second: columns. `shifts_b`: first entry: rows, second: columns. `widths_b`: first entry: rows, second: columns.
All inputs are finite; a program needn't handle non-finite values.
Results may differ from a plain program's by a relative error of at most 0.0003.
Values sent between devices are 32-bit elements; how exact they have to be, the bound alone decides.
No kernel may reach another device: no remote copies, remote signals or barrier semaphores. Data moves between devices by JAX's collectives and lax.ppermute only.
A program may use at most 64 MiB of HBM per device.

v0:
```python
import functools
import math

import jax
import jax.numpy as jnp
import numpy as np
from jax import lax
from jax.experimental import pallas as pl
from jax.experimental.pallas import tpu as pltpu
from jax.sharding import PartitionSpec as P

S = 256
HALF = 128
BOX = 512
ITERS = 3
RADIUS = 8
REACH = BOX + HALF
EPS = 0.05
SIGMA = 2.0
F32 = jnp.float32
BF16 = jnp.bfloat16
OWN = S + RADIUS
NEXT = S + 2 * RADIUS
FAR = REACH - 2 * S + RADIUS
BASE = 904
VMEM = pl.BlockSpec(memory_space=pltpu.VMEM)
SMEM = pl.BlockSpec(memory_space=pltpu.SMEM)
ANY = pl.BlockSpec(memory_space=pl.ANY)
HBM = pl.BlockSpec(memory_space=pltpu.HBM)
PARAMS = pltpu.CompilerParams(vmem_limit_bytes=40 << 20)


def dot(a, b):
    return jnp.dot(a, b, preferred_element_type=F32)


def fill_base(ref):
    for c in range(0, BASE, 8 * 28):
        n = min(8 * 28, BASE - c)
        rows = lax.broadcasted_iota(jnp.int32, (n, HALF), 0)
        cols = lax.broadcasted_iota(jnp.int32, (n, HALF), 1)
        dist = (rows - cols + (c - 384)).astype(F32) / S
        ref[c : c + n] = jnp.exp(-dist * dist / EPS)


def window(ref, start):
    base = pl.multiple_of(start // 8 * 8, 8)
    rest = start - base
    tiles = ref[pl.ds(base, REACH + 8), :].reshape(REACH // 8 + 1, 8, HALF)
    tiles = pltpu.roll(tiles, jnp.where(rest == 0, 0, 8 - rest), 1)
    row = lax.broadcasted_iota(jnp.int32, (REACH // 8, 8, HALF), 1)
    return jnp.where(row < 8 - rest, tiles[:-1], tiles[1:]).reshape(REACH, HALF).astype(BF16)


def fill_tables(o_r, o_c, w_r, w_c, base_ref, refs):
    back_r, back_c, fwd_r, fwd_c = refs
    tall_r = window(base_ref, o_r + S)
    tall_c = window(base_ref, o_c + S)
    wide_r = window(base_ref, -o_r)
    wide_c = window(base_ref, -o_c)
    none = jnp.zeros((), BF16)
    lane = lax.broadcasted_iota(jnp.int32, (S, HALF), 1)
    deep = lax.broadcasted_iota(jnp.int32, (BOX, HALF), 0)
    for k in range(BOX // HALF):
        at = slice(k * HALF, (k + 1) * HALF)
        rows = slice(384 - HALF * k, 640 - HALF * k)
        back_c[:, at] = wide_c[rows]
        fwd_r[:, at] = jnp.where(lane + k * HALF < w_r, wide_r[rows], none)
    for k in range(S // HALF):
        at = slice(k * HALF, (k + 1) * HALF)
        rows = slice(HALF - HALF * k, REACH - HALF * k)
        back_r[:, at] = tall_r[rows]
        fwd_c[:, at] = jnp.where(deep < w_c, tall_c[rows], none)


def table_scratch():
    return [
        pltpu.VMEM((BOX, S), BF16),
        pltpu.VMEM((S, BOX), BF16),
        pltpu.VMEM((S, BOX), BF16),
        pltpu.VMEM((BOX, S), BF16),
    ]


def forward(mass, tables, vb_ref):
    inner = dot(tables[2][...], vb_ref[...]).astype(BF16)
    return mass / dot(inner, tables[3][...])


def aligned_kernel(cells, shifts, widths, source, boxes, *refs):
    n = len(cells)
    outs, refs = refs[: 4 if 0 in cells else 2], refs[4 if 0 in cells else 2 :]
    base_ref, box_ref, mass_ref, vb_ref, tables, sems = refs
    copies = []
    for i, j in enumerate(cells):
        copies.append((
            pltpu.make_async_copy(boxes.at[0, j], box_ref.at[i], sems.at[i, 0]),
            pltpu.make_async_copy(
                source.at[:, pl.ds(j * S, S)], mass_ref.at[:, pl.ds(i * S, S)], sems.at[i, 1]),
        ))
    for pair in copies:
        for copy in pair:
            copy.start()
    fill_base(base_ref)
    for i, j in enumerate(cells):
        fill_tables(
            shifts[0, j, 0], shifts[0, j, 1], widths[0, j, 0], widths[0, j, 1], base_ref, tables[i])
    scales = []
    for i in range(n):
        down = dot(tables[i][0][...], jnp.ones((S, HALF), BF16)).astype(BF16).astype(F32)
        across = dot(jnp.ones((8, S), BF16), tables[i][1][...])
        scales.append(((1.0 / down)[:, :1], (1.0 / across)[:1]))
    u = [None] * n
    for step in range(ITERS):
        for i in range(n):
            if step == 0:
                for copy in copies[i]:
                    copy.wait()
                down, across = scales[i]
                for c in range(0, BOX, HALF):
                    v = box_ref[i, c : c + HALF] * down[c : c + HALF] * across
                    vb_ref[i, c : c + HALF] = v.astype(BF16)
            else:
                inner = dot(tables[i][0][...], u[i].astype(BF16)).astype(BF16)
                vb_ref[i] = (box_ref[i] / dot(inner, tables[i][1][...])).astype(BF16)
        for i in range(n):
            u[i] = forward(mass_ref[:, i * S : (i + 1) * S], tables[i], vb_ref.at[i])
    for i, j in enumerate(cells):
        outs[0][:, i * S : (i + 1) * S] = u[i][:HALF]
        outs[1][:, i * S : (i + 1) * S] = u[i][HALF:]
        if j == 0:
            for k in range(2):
                outs[2 + k][:HALF] = u[i][k * HALF : (k + 1) * HALF, :HALF]
                outs[2 + k][HALF:] = mass_ref[k * HALF : (k + 1) * HALF, i * S : i * S + HALF]


def cost(cells, applies):
    return pl.CostEstimate(
        flops=cells * applies * 804_000_000, bytes_accessed=cells << 20, transcendentals=0)


def aligned(cells, source, boxes, shifts, widths):
    n = len(cells)
    half = jax.ShapeDtypeStruct((HALF, n * S), F32)
    corner = jax.ShapeDtypeStruct((S, HALF), F32)
    shapes = [half, half] + ([corner, corner] if 0 in cells else [])
    return pl.pallas_call(
        functools.partial(aligned_kernel, cells),
        in_specs=[SMEM, SMEM, HBM, HBM],
        out_specs=[VMEM] * len(shapes),
        out_shape=shapes,
        scratch_shapes=[
            pltpu.VMEM((BASE, HALF), F32),
            pltpu.VMEM((n, BOX, BOX), F32),
            pltpu.VMEM((S, n * S), F32),
            pltpu.VMEM((n, BOX, BOX), BF16),
            [table_scratch() for _ in cells],
            pltpu.SemaphoreType.DMA((n, 2)),
        ],
        compiler_params=PARAMS,
        cost_estimate=cost(n, 5),
        name="aligned",
    )(shifts, widths, source, boxes)


def place(plan_ref, top, left, canvas_ref, first):
    base = pl.multiple_of(top // 8 * 8, 8)
    rest = top - base
    row = lax.broadcasted_iota(jnp.int32, (HALF // 8 + 1, 8, BOX), 1)
    column = lax.broadcasted_iota(jnp.int32, (HALF + 8, HALF), 1)
    none = jnp.zeros((1, 8, BOX), F32)
    for c in range(0, BOX, HALF):
        turned = pltpu.roll(plan_ref[c : c + HALF].reshape(HALF // 8, 8, BOX), rest, 1)
        rows = jnp.where(
            row < rest,
            jnp.concatenate([none, turned], 0),
            jnp.concatenate([turned, none], 0),
        ).reshape(HALF + 8, BOX)
        before = jnp.zeros((HALF + 8, HALF), F32)
        for k in range(BOX // HALF + 1):
            now = jnp.zeros((HALF + 8, HALF), F32)
            if k < BOX // HALF:
                now = pltpu.roll(rows[:, k * HALF : (k + 1) * HALF], left, 1)
            at = (pl.ds(base + c, HALF + 8), slice(first + k * HALF, first + (k + 1) * HALF))
            canvas_ref[at] = canvas_ref[at] + jnp.where(column < left, before, now)
            before = now


def shifted_kernel(cells, origin, carried, finals, kept, shifts, widths, boxes, *refs):
    n = len(cells)
    quads, refs = refs[: 8 * n], refs[8 * n :]
    upper_ref = None
    if carried:
        carry_ref, refs = refs[0], refs[1:]
        if kept:
            upper_ref, refs = refs[0], refs[1:]
    outs, refs = refs[:4], refs[4:]
    if kept:
        keep_ref, refs = refs[0], refs[1:]
    base_ref, box_ref, mass_ref, ub_ref, vb_ref, v_ref, canvas_ref, tables, sems, out_sems = refs
    copies = [
        pltpu.make_async_copy(boxes.at[0, j], box_ref.at[i], sems.at[i])
        for i, j in enumerate(cells)
    ]
    for copy in copies:
        copy.start()
    fill_base(base_ref)
    canvas_ref[...] = jnp.zeros_like(canvas_ref)
    if carried:
        first, last = carried[0] - origin, carried[1] - origin
        canvas_ref[:REACH, first:last] = carry_ref[...]
    for i, j in enumerate(cells):
        fill_tables(
            shifts[0, j, 0], shifts[0, j, 1], widths[0, j, 0], widths[0, j, 1], base_ref, tables[i])
        for k in range(4):
            rows = slice(k // 2 * HALF, (k // 2 + 1) * HALF)
            cols = slice(k % 2 * HALF, (k % 2 + 1) * HALF)
            ub_ref[i, rows, cols] = quads[8 * i + k][...].astype(BF16)
            mass_ref[i, rows, cols] = quads[8 * i + 4 + k][...]
    u = [ub_ref[i] for i in range(n)]
    for step in range(ITERS):
        for i in range(n):
            inner = dot(tables[i][0][...], u[i]).astype(BF16)
            den = dot(inner, tables[i][1][...])
            if step == 0:
                copies[i].wait()
            v = box_ref[i] / den
            if step == ITERS - 1:
                v_ref[i] = v
            vb_ref[i] = v.astype(BF16)
        for i in range(n):
            u[i] = forward(mass_ref[i], tables[i], vb_ref.at[i]).astype(BF16)
    deep = lax.broadcasted_iota(jnp.int32, (BOX, S), 0)
    lane = lax.broadcasted_iota(jnp.int32, (S, BOX), 1)
    for i, j in enumerate(cells):
        inner = jnp.where(deep < widths[0, j, 0], dot(tables[i][0][...], u[i]), 0.0).astype(BF16)
        used = jnp.where(lane < widths[0, j, 1], tables[i][1][...], jnp.zeros((), BF16))
        v_ref[i] = v_ref[i] * dot(inner, used)
    for i, j in enumerate(cells):
        place(v_ref.at[i], shifts[0, j, 0] + HALF, shifts[0, j, 1] + HALF, canvas_ref,
              j * S - origin)
    writes = []
    at = 0
    for first, last in finals:
        size = last - first
        for ref, row in zip(outs, (0, S - RADIUS, 2 * S - RADIUS, 0)):
            writes.append(pltpu.make_async_copy(
                canvas_ref.at[pl.ds(row, ref.shape[0]), pl.ds(first - origin, size)],
                ref.at[:, pl.ds(at, size)],
                out_sems.at[len(writes)]))
        at += size
    if upper_ref is not None:
        writes.append(pltpu.make_async_copy(
            upper_ref, outs[3].at[:, pl.ds(at, upper_ref.shape[1])], out_sems.at[len(writes)]))
    if kept:
        size = kept[1] - kept[0]
        writes.append(pltpu.make_async_copy(
            canvas_ref.at[pl.ds(0, REACH), pl.ds(kept[0] - origin, size)], keep_ref,
            out_sems.at[len(writes)]))
    for copy in writes:
        copy.start()
    for copy in writes:
        copy.wait()


def shifted(cells, boxes, shifts, widths, quads, carried=None, carry=None, finals=(), kept=None):
    n = len(cells)
    origin = min(j * S for j in cells)
    width = max(j * S + REACH for j in cells) - origin
    total = sum(last - first for first, last in finals)
    shapes = [jax.ShapeDtypeStruct((rows, total), F32) for rows in (OWN, NEXT, FAR, RADIUS)]
    if kept:
        shapes.append(jax.ShapeDtypeStruct((REACH, kept[1] - kept[0]), F32))
    blocks, arrays = [], []
    for j in cells:
        for array, at in quads[j]:
            arrays.append(array)
            blocks.append(pl.BlockSpec((HALF, HALF), lambda g, at=at: at))
    if carried:
        arrays += carry
        blocks += [VMEM] * len(carry)
        if kept:
            shapes[3] = jax.ShapeDtypeStruct((RADIUS, total + carry[1].shape[1]), F32)
    return pl.pallas_call(
        functools.partial(shifted_kernel, cells, origin, carried, finals, kept),
        grid=(1,),
        in_specs=[SMEM, SMEM, HBM] + blocks,
        out_specs=[ANY] * len(shapes),
        out_shape=shapes,
        scratch_shapes=[
            pltpu.VMEM((BASE, HALF), F32),
            pltpu.VMEM((n, BOX, BOX), F32),
            pltpu.VMEM((n, S, S), F32),
            pltpu.VMEM((n, S, S), BF16),
            pltpu.VMEM((n, BOX, BOX), BF16),
            pltpu.VMEM((n, BOX, BOX), F32),
            pltpu.VMEM((REACH + 8, width), F32),
            [table_scratch() for _ in cells],
            pltpu.SemaphoreType.DMA((n,)),
            pltpu.SemaphoreType.DMA((4 * len(finals) + 2,)),
        ],
        compiler_params=PARAMS,
        cost_estimate=cost(n, 7),
        name="shifted",
    )(shifts, widths, boxes, *arrays)


def blur_weights():
    raw = [math.exp(-(d * d) / (2.0 * SIGMA * SIGMA)) for d in range(-RADIUS, RADIUS + 1)]
    total = sum(raw)
    return [w / total for w in raw]


def blurred_rows(own_ref, next_ref, far_ref, back_ref, win_ref, width, put):
    win_ref[:, :width] = next_ref[...]
    win_ref[RADIUS:, :width] = win_ref[RADIUS:, :width] + own_ref[...]
    win_ref[:FAR, :width] = win_ref[:FAR, :width] + far_ref[...]
    win_ref[NEXT - RADIUS :, :width] = win_ref[NEXT - RADIUS :, :width] + back_ref[...]
    weights = blur_weights()
    for c in range(0, width, HALF):
        col = win_ref[:, c : c + HALF]
        out = weights[RADIUS] * col[RADIUS : RADIUS + S]
        for d in range(1, RADIUS + 1):
            out = out + weights[RADIUS + d] * (
                col[RADIUS + d : RADIUS + d + S] + col[RADIUS - d : RADIUS - d + S])
        put(c, out)


def edges_kernel(*refs):
    (own3, next3, far3, own2, next2, far2, back2, main_ref, right_ref, east_ref, west_ref,
     win_ref) = refs

    def outer(c, out):
        east_ref[:S, HALF + c : 2 * HALF + c] = out

    def inner(c, out):
        if c < 3 * HALF:
            main_ref[:, c : c + HALF] = out
        else:
            east_ref[:S, :HALF] = out
            right_ref[...] = out
        if c == 0:
            west_ref[...] = out.T[:RADIUS]
        if c == 2 * HALF:
            east_ref[S:, :S] = out.T[HALF - RADIUS :]
            east_ref[S:, S:] = jnp.zeros((RADIUS, HALF), F32)

    blurred_rows(own3, next3, far3, back2.at[:, 2 * S :], win_ref, S, outer)
    blurred_rows(own2, next2, far2, back2.at[:, : 2 * S], win_ref, 2 * S, inner)


def edges(*arrays):
    return pl.pallas_call(
        edges_kernel,
        in_specs=[VMEM] * 7,
        out_specs=[VMEM] * 4,
        out_shape=[
            jax.ShapeDtypeStruct((S, 3 * HALF), F32),
            jax.ShapeDtypeStruct((S, HALF), F32),
            jax.ShapeDtypeStruct((S + RADIUS, 3 * HALF), F32),
            jax.ShapeDtypeStruct((RADIUS, S), F32),
        ],
        scratch_shapes=[pltpu.VMEM((NEXT, 2 * S), F32)],
        compiler_params=PARAMS,
        name="edges",
    )(*arrays)


def band():
    full = np.zeros((2 * S, S), np.float64)
    for j in range(S):
        for d, w in zip(range(-RADIUS, RADIUS + 1), blur_weights()):
            full[j + HALF + d, j] = w
    high = full.astype(jnp.bfloat16)
    return high, (full - high.astype(np.float64)).astype(jnp.bfloat16)


def final_kernel(own1, next1, far1, back1, main_ref, right_ref, east_ref, west_ref, high_ref,
                 low_ref, out_ref, rows_ref, win_ref):
    span = out_ref.shape[1]
    none = jnp.zeros((HALF - RADIUS, S), F32)
    win_ref[:, :HALF] = jnp.concatenate([none, east_ref[S:, :S]], 0).T
    win_ref[:, HALF : HALF + S] = main_ref[:, :S] + east_ref[:S, :S]
    win_ref[:, HALF + 7 * HALF : HALF + span] = main_ref[:, S:]
    win_ref[:, HALF + span :] = right_ref[...] + jnp.concatenate([west_ref[...], none], 0).T

    def middle(c, out):
        if c == 0:
            out = out + east_ref[:S, S:]
        win_ref[:, HALF + S + c : 2 * HALF + S + c] = out

    blurred_rows(own1, next1, far1, back1, rows_ref, REACH, middle)
    for c in range(0, span, S):
        strip = win_ref[:, c : c + 2 * S]
        high = strip.astype(BF16)
        low = (strip - high.astype(F32)).astype(BF16)
        out_ref[:, c : c + S] = (
            dot(high, high_ref[...]) + dot(high, low_ref[...]) + dot(low, high_ref[...]))


def final(span, *arrays):
    high, low = band()
    return pl.pallas_call(
        final_kernel,
        in_specs=[VMEM] * 10,
        out_specs=VMEM,
        out_shape=jax.ShapeDtypeStruct((S, span), F32),
        scratch_shapes=[
            pltpu.VMEM((NEXT, REACH), F32),
            pltpu.VMEM((S, span + 2 * HALF), F32),
        ],
        compiler_params=PARAMS,
        name="final",
    )(*arrays, jnp.asarray(high), jnp.asarray(low))


def moved(array, by_row, by_col):
    n_row, n_col = lax.axis_size("row"), lax.axis_size("col")
    if by_col == 0:
        return lax.ppermute(array, "row", [(i, (i + by_row) % n_row) for i in range(n_row)])
    if by_row == 0:
        return lax.ppermute(array, "col", [(i, (i + by_col) % n_col) for i in range(n_col)])
    pairs = [
        (r * n_col + c, (r + by_row) % n_row * n_col + (c + by_col) % n_col)
        for r in range(n_row)
        for c in range(n_col)
    ]
    return lax.ppermute(array, ("row", "col"), pairs)


def spilled(parts):
    own, after, far, back = parts
    return own, moved(after, 1, 0), moved(far, 2, 0), moved(back, -1, 0)


def behind(array, *others):
    return lax.optimization_barrier((array, *others))[0]


def on_device(source, boxes_a, shifts_a, widths_a, boxes_b, shifts_b, widths_b):
    mtop = moved(source[:HALF], -1, 0)
    boxes_a = pltpu.with_memory_space_constraint(boxes_a, pltpu.HBM)
    boxes_b = pltpu.with_memory_space_constraint(boxes_b, pltpu.HBM)
    masses = pltpu.with_memory_space_constraint(source, pltpu.HBM)
    top03, bot03, left_top, left_bot = aligned((0, 3), masses, boxes_a, shifts_a, widths_a)
    rtop03 = moved(top03, -1, 0)
    east = moved(left_bot, 0, -1)
    diag = moved(left_top, -1, -1)
    top12, bot12 = aligned(
        (1, 2), masses, boxes_a, behind(shifts_a, bot03), widths_a)
    rtop12 = moved(top12, -1, 0)
    own = [(bot03, 0), (bot03, 1), (bot12, 0), (bot12, 1), (bot12, 2), (bot12, 3), (bot03, 2),
           (bot03, 3), (east, 0)]
    below = [(rtop03, 0), (rtop03, 1), (rtop12, 0), (rtop12, 1), (rtop12, 2), (rtop12, 3),
             (rtop03, 2), (rtop03, 3), (diag, 0)]
    quads = {}
    for j in range(4):
        a, b = 2 * j + 1, 2 * j + 2
        quads[j] = [(array, (0, at)) for array, at in (own[a], own[b], below[a], below[b])]
        quads[j] += [
            (source, (1, a)),
            (source, (1, b)) if j < 3 else (east, (1, 0)),
            (mtop, (0, a)),
            (mtop, (0, b)) if j < 3 else (diag, (1, 0)),
        ]
    own3, next3, far3, back3, carry = shifted(
        (3,), boxes_b, behind(shifts_b, bot12), widths_b, quads,
        finals=((1152, 1408),), kept=(768, 1152))
    next3 = moved(next3, 1, 0)
    far3 = moved(far3, 2, 0)
    own2, next2, far2, back2, carry = shifted(
        (0, 2), boxes_b, shifts_b, widths_b, quads,
        carried=(768, 1152), carry=(carry, back3), finals=((0, 256), (896, 1152)),
        kept=(256, 896))
    next2 = moved(next2, 1, 0)
    far2 = moved(far2, 2, 0)
    rback2 = moved(back2, -1, 0)
    own1, next1, far1, back1 = shifted(
        (1,), boxes_b, shifts_b, widths_b, quads,
        carried=(256, 896), carry=(behind(carry, next3, far3),),
        finals=((256, 896),))
    next1 = moved(behind(next1, next2, far2, rback2), 1, 0)
    far1 = moved(behind(far1, next2, far2, rback2), 2, 0)
    back1 = moved(behind(back1, next2, far2, rback2), -1, 0)
    main, right, east, west = edges(own3, next3, far3, own2, next2, far2, rback2)
    return final(
        source.shape[1], own1, next1, far1, back1, main, right, moved(east, 0, 1),
        moved(west, 0, -1))


def solution(mesh):
    cells = P("row", "col", None)
    boxes = P("row", "col", None, None)
    return jax.shard_map(
        on_device,
        mesh=mesh,
        in_specs=(P("row", "col"), boxes, cells, cells, boxes, cells, cells),
        out_specs=P("row", "col"),
        check_vma=False,
    )
```

profile of v0, /device:TPU:1, one launch (start us, length us, event | category | flops | bytes accessed | tf_op | source)
XLA Modules:
  0.0 89.8 jit_solution(7411128729139624967)
XLA Ops:
  0.0 0.8 copy.11.widths
  0.8 0.8 copy.10.shifts
  1.5 0.0 copy-start.2
  1.5 0.0 copy-start.6
  1.5 5.5 %aligned.2 = (f32[128,512]{1,0:T(8,128)S(1)}, f32[128,512]{1,0:T(8,128)S(1)}, f32[256,128]{1,0:T(8,128)S(1)}, f32[256,128]{1,0:T(8,128)S(1)}) custom-call(s32[1,4,2]{2,1,0:T(4,128)S(1)} %copy.10.shifts, s32[1,4,2]{2,1,0:T(4,128)S(1)} %copy.11.widths, f32[256,1024]{1,0:T(8,128)} %refs_5_.3, f32[1,4,512,512]{3,2,1,0:T(8,128)} %boxes.6), custom_call_target="tpu_custom_call" | custom-call | flops 8040000000 | bytes 2097152 | tf_op jit(solution)/shard_map/aligned/pallas_call | solution.py:147
  7.0 0.0 copy-start.4
  7.1 0.7 copy-done.4
  7.7 3.2 %collective-permute-start.2 = (f32[128,512]{1,0:T(8,128)S(1)}, f32[128,512]{1,0:T(8,128)S(1)}, u32[]{:S(2)}, u32[]{:S(2)}) collective-permute-start(f32[128,512]{1,0:T(8,128)S(1)} %get-tuple-element.39), channel_id=1, source_target_pairs={{0,248},{8,0},{16,8},{24,16},{32,24},{40,32},{48,40},{56,48},{64,5... | collective-permute-start | bytes 786440 | tf_op jit(solution)/shard_map/ppermute | solution.py:420
  11.0 3.4 %collective-permute-start.3 = (f32[256,128]{1,0:T(8,128)S(1)}, f32[256,128]{1,0:T(8,128)S(1)}, u32[]{:S(2)}, u32[]{:S(2)}) collective-permute-start(f32[256,128]{1,0:T(8,128)S(1)} %get-tuple-element.41), channel_id=1, source_target_pairs={{0,7},{1,0},{2,1},{3,2},{4,3},{5,4},{6,5},{7,6},{8,15},{9,8},{10,9... | collective-permute-start | bytes 393224 | tf_op jit(solution)/shard_map/ppermute | solution.py:422
  14.4 6.7 %collective-permute-start.4 = (f32[256,128]{1,0:T(8,128)S(1)}, f32[256,128]{1,0:T(8,128)S(1)}, u32[]{:S(2)}, u32[]{:S(2)}) collective-permute-start(f32[256,128]{1,0:T(8,128)S(1)} %get-tuple-element.42), channel_id=1, source_target_pairs={{0,255},{1,248},{2,249},{3,250},{4,251},{5,252},{6,253},{7,254},{8... | collective-permute-start | bytes 393224 | tf_op jit(solution)/shard_map/ppermute | solution.py:428
  21.1 0.0 copy-done.2
  21.1 0.8 slice.3
  21.9 0.0 collective-permute-start.1
  21.9 0.0 copy-done.6
  21.9 0.1 copy.12.shifts
  22.0 0.0 copy-start.7
  22.0 0.0 copy-start.8
  22.0 0.0 copy-start.3
  22.0 5.5 %aligned.3 = (f32[128,512]{1,0:T(8,128)S(1)}, f32[128,512]{1,0:T(8,128)S(1)}) custom-call(s32[1,4,2]{2,1,0:T(4,128)S(1)} %copy.12.shifts, s32[1,4,2]{2,1,0:T(4,128)S(1)} %copy.11.widths, f32[256,1024]{1,0:T(8,128)} %refs_5_.3, f32[1,4,512,512]{3,2,1,0:T(8,128)} %boxes.6), custom_call_target="tpu_custom_call" | custom-call | flops 8040000000 | bytes 2097152 | tf_op jit(solution)/shard_map/aligned/pallas_call | solution.py:147
  27.6 0.5 collective-permute-start
  28.1 0.0 copy-done.7
  28.1 0.1 copy.18.shifts
  28.2 0.1 copy.14.shifts
  28.3 0.0 copy-done.8
  28.3 0.1 copy.19.widths
  28.4 0.0 collective-permute-done.3.refs_1_.refs_5_
  28.4 0.0 collective-permute-done.4.refs_3_.refs_7_
  28.4 0.0 collective-permute-done.2.refs_2_.refs_11_
  28.4 2.4 %collective-permute-done.1.refs_6_.refs_7_.refs_14_.refs_15_ = f32[128,1024]{1,0:T(8,128)S(1)} collective-permute-done((f32[128,1024]{1,0:T(8,128)}, f32[128,1024]{1,0:T(8,128)S(1)}, u32[]{:S(2)}, u32[]{:S(2)}) %collective-permute-start.1) | collective-permute-done | bytes 524320 | tf_op jit(solution)/shard_map/ppermute | solution.py:420
  30.7 0.0 copy-done.3
  30.7 0.0 copy-start.5
  30.7 0.9 %copy-done.5 = f32[128,512]{1,0:T(8,128)S(1)} copy-done((f32[128,512]{1,0:T(8,128)S(1)}, f32[128,512]{1,0:T(8,128)}, u32[]{:S(2)}) %copy-start.5) | copy-done | bytes 262168
  31.7 5.0 %shifted.3 = (f32[264,256]{1,0:T(8,128)S(1)}, f32[272,256]{1,0:T(8,128)S(1)}, f32[136,256]{1,0:T(8,128)S(1)}, f32[8,256]{1,0:T(8,128)S(1)}, f32[640,384]{1,0:T(8,128)S(1)}) custom-call(s32[1,4,2]{2,1,0:T(4,128)S(1)} %copy.14.shifts, s32[1,4,2]{2,1,0:T(4,128)S(1)} %copy.19.widths, f32[1,4,512,512]{3,2,1,0:T(8,128)} %boxes.9, f32[128,512]{1,0:T(8,128)S(1)} %copy-done.5, ...), custom_call_target="tpu_custom_call" | custom-call | flops 5628000256 | bytes 1048576 | tf_op jit(solution)/shard_map/shifted/pallas_call | solution.py:284
  36.7 0.1 collective-permute-start.5
  36.8 0.1 collective-permute-start.6
  36.9 0.0 collective-permute-done.refs_3_.refs_10_.refs_2_
  36.9 7.1 %shifted.4 = (f32[264,512]{1,0:T(8,128)S(1)}, f32[272,512]{1,0:T(8,128)S(1)}, f32[136,512]{1,0:T(8,128)S(1)}, f32[8,768]{1,0:T(8,128)S(1)}, f32[640,640]{1,0:T(8,128)S(1)}) custom-call(s32[1,4,2]{2,1,0:T(4,128)S(1)} %copy.18.shifts, s32[1,4,2]{2,1,0:T(4,128)S(1)} %copy.19.widths, f32[1,4,512,512]{3,2,1,0:T(8,128)} %boxes.9, f32[128,512]{1,0:T(8,128)S(1)} %copy-done.5, ...), custom_call_target="tpu_custom_call" | custom-call | flops 11256000512 | bytes 2097152 | tf_op jit(solution)/shard_map/shifted/pallas_call | solution.py:284
  44.0 0.1 collective-permute-start.7
  44.1 0.1 collective-permute-start.8
  44.2 0.7 collective-permute-start.9
  44.9 1.1 %collective-permute-done.6.refs_2_ = f32[136,256]{1,0:T(8,128)S(1)} collective-permute-done((f32[136,256]{1,0:T(8,128)S(1)}, f32[136,256]{1,0:T(8,128)S(1)}, u32[]{:S(2)}, u32[]{:S(2)}) %collective-permute-start.6) | collective-permute-done | bytes 139296 | tf_op jit(solution)/shard_map/ppermute | solution.py:420
  46.0 0.0 collective-permute-done.5.refs_1_
  46.0 0.0 copy-start
  46.0 0.0 copy-start.1
  46.0 5.8 %shifted.5 = (f32[264,640]{1,0:T(8,128)S(1)}, f32[272,640]{1,0:T(8,128)S(1)}, f32[136,640]{1,0:T(8,128)S(1)}, f32[8,640]{1,0:T(8,128)S(1)}) custom-call(s32[1,4,2]{2,1,0:T(4,128)S(1)} %copy.18.shifts, s32[1,4,2]{2,1,0:T(4,128)S(1)} %copy.19.widths, f32[1,4,512,512]{3,2,1,0:T(8,128)} %boxes.9, f32[128,512]{1,0:T(8,128)S(1)} %get-tuple-element.37.refs_1_.refs_8_.refs_0_, ...), custom_call_target="tpu_custom_call" | custom-call | flops 5628000256 | bytes 1048576 | tf_op jit(solution)/shard_map/shifted/pallas_call | solution.py:284
  51.8 0.0 collective-permute-done.9.refs_6_
  51.8 9.0 %collective-permute-done.8.refs_5_ = f32[136,512]{1,0:T(8,128)S(1)} collective-permute-done((f32[136,512]{1,0:T(8,128)S(1)}, f32[136,512]{1,0:T(8,128)S(1)}, u32[]{:S(2)}, u32[]{:S(2)}) %collective-permute-start.8) | collective-permute-done | bytes 278560 | tf_op jit(solution)/shard_map/ppermute | solution.py:420
  60.8 0.0 collective-permute-done.7.refs_4_
  60.8 0.0 collective-permute-start.10
  60.8 1.5 %edges.1 = (f32[256,384]{1,0:T(8,128)S(1)}, f32[256,128]{1,0:T(8,128)S(1)}, f32[264,384]{1,0:T(8,128)S(1)}, f32[8,256]{1,0:T(8,128)S(1)}) custom-call(f32[264,256]{1,0:T(8,128)S(1)} %get-tuple-element.59.refs_0_, f32[272,256]{1,0:T(8,128)S(1)} %collective-permute-done.5.refs_1_, f32[136,256]{1,0:T(8,128)S(1)} %collective-permute-done.6.refs_2_, ...), custom_call_target="tpu_custom_call" | custom-call | tf_op jit(solution)/shard_map/edges/pallas_call | solution.py:353
  62.3 1.0 %collective-permute-start.13 = (f32[264,384]{1,0:T(8,128)S(1)}, f32[264,384]{1,0:T(8,128)S(1)}, u32[]{:S(2)}, u32[]{:S(2)}) collective-permute-start(f32[264,384]{1,0:T(8,128)S(1)} %get-tuple-element.63), channel_id=1, source_target_pairs={{0,1},{1,2},{2,3},{3,4},{4,5},{5,6},{6,7},{7,0},{8,9},{9,10},{10,1... | collective-permute-start | bytes 1216520 | tf_op jit(solution)/shard_map/ppermute | solution.py:422
  63.3 0.0 collective-permute-start.11
  63.3 0.8 collective-permute-start.12
  64.1 4.2 %collective-permute-start.14 = (f32[8,256]{1,0:T(8,128)S(1)}, f32[8,256]{1,0:T(8,128)S(1)}, u32[]{:S(2)}, u32[]{:S(2)}) collective-permute-start(f32[8,256]{1,0:T(8,128)S(1)} %get-tuple-element.64), channel_id=1, source_target_pairs={{0,7},{1,0},{2,1},{3,2},{4,3},{5,4},{6,5},{7,6},{8,15},{9,8},{10,9... | collective-permute-start | bytes 24584 | tf_op jit(solution)/shard_map/ppermute | solution.py:422
  68.3 0.8 collective-permute-done.14.west_ref
  69.1 17.9 %collective-permute-done.12.back1 = f32[8,640]{1,0:T(8,128)S(1)} collective-permute-done((f32[8,640]{1,0:T(8,128)S(1)}, f32[8,640]{1,0:T(8,128)S(1)}, u32[]{:S(2)}, u32[]{:S(2)}) %collective-permute-start.12) | collective-permute-done | bytes 20512 | tf_op jit(solution)/shard_map/ppermute | solution.py:420
  86.9 0.0 collective-permute-done.11.far1
  86.9 0.0 collective-permute-done.13.east_ref
  86.9 0.0 collective-permute-done.10.next1
  87.0 0.0 copy-done
  87.0 0.0 copy-done.1
  87.0 2.8 %final.1 = f32[256,1024]{1,0:T(8,128)} custom-call(f32[264,640]{1,0:T(8,128)S(1)} %get-tuple-element.49.own1, f32[272,640]{1,0:T(8,128)S(1)} %collective-permute-done.10.next1, f32[136,640]{1,0:T(8,128)S(1)} %collective-permute-done.11.far1, f32[8,640]{1,0:T(8,128)S(1)} %collective-permute-done.12.back1, f32[256,384]{1,0:T(8,128)S(1)} %get-tuple-element.61.main_ref, ...), custom_call_target="tpu_custom_call" | custom-call | tf_op jit(solution)/shard_map/final/pallas_call | solution.py:403
Async XLA Ops:
  1.5 19.6 %copy-start.2 = (f32[256,1024]{1,0:T(8,128)S(1)}, f32[256,1024]{1,0:T(8,128)}, u32[]{:S(2)}) copy-start(f32[256,1024]{1,0:T(8,128)} %refs_5_.3) | copy-start | bytes 3145732
  1.5 20.4 %copy-start.6 = (s32[1,4,2]{1,2,0:T(2,128)S(1)}, s32[1,4,2]{1,2,0:T(2,128)}, u32[]{:S(2)}) copy-start(s32[1,4,2]{1,2,0:T(2,128)} %param.11) | copy-start | bytes 100
  7.0 0.7 copy-start.4
  7.7 20.6 %collective-permute-start.2 = (f32[128,512]{1,0:T(8,128)S(1)}, f32[128,512]{1,0:T(8,128)S(1)}, u32[]{:S(2)}, u32[]{:S(2)}) collective-permute-start(f32[128,512]{1,0:T(8,128)S(1)} %get-tuple-element.39), channel_id=1, source_target_pairs={{0,248},{8,0},{16,8},{24,16},{32,24},{40,32},{48,40},{56,48},{64,5... | collective-permute-start | bytes 786440 | tf_op jit(solution)/shard_map/ppermute | solution.py:420
  11.0 17.4 %collective-permute-start.3 = (f32[256,128]{1,0:T(8,128)S(1)}, f32[256,128]{1,0:T(8,128)S(1)}, u32[]{:S(2)}, u32[]{:S(2)}) collective-permute-start(f32[256,128]{1,0:T(8,128)S(1)} %get-tuple-element.41), channel_id=1, source_target_pairs={{0,7},{1,0},{2,1},{3,2},{4,3},{5,4},{6,5},{7,6},{8,15},{9,8},{10,9... | collective-permute-start | bytes 393224 | tf_op jit(solution)/shard_map/ppermute | solution.py:422
  14.4 14.0 %collective-permute-start.4 = (f32[256,128]{1,0:T(8,128)S(1)}, f32[256,128]{1,0:T(8,128)S(1)}, u32[]{:S(2)}, u32[]{:S(2)}) collective-permute-start(f32[256,128]{1,0:T(8,128)S(1)} %get-tuple-element.42), channel_id=1, source_target_pairs={{0,255},{1,248},{2,249},{3,250},{4,251},{5,252},{6,253},{7,254},{8... | collective-permute-start | bytes 393224 | tf_op jit(solution)/shard_map/ppermute | solution.py:428
  21.9 8.8 %collective-permute-start.1 = (f32[128,1024]{1,0:T(8,128)}, f32[128,1024]{1,0:T(8,128)S(1)}, u32[]{:S(2)}, u32[]{:S(2)}) collective-permute-start(f32[128,1024]{1,0:T(8,128)} %slice.3), channel_id=1, source_target_pairs={{0,248},{8,0},{16,8},{24,16},{32,24},{40,32},{48,40},{56,48},{64,5... | collective-permute-start | bytes 1572872 | tf_op jit(solution)/shard_map/ppermute | solution.py:420
  22.0 6.1 %copy-start.7 = (s32[1,4,2]{1,2,0:T(2,128)S(1)}, s32[1,4,2]{1,2,0:T(2,128)}, u32[]{:S(2)}) copy-start(s32[1,4,2]{1,2,0:T(2,128)} %param.14) | copy-start | bytes 100
  22.0 6.3 %copy-start.8 = (s32[1,4,2]{1,2,0:T(2,128)S(1)}, s32[1,4,2]{1,2,0:T(2,128)}, u32[]{:S(2)}) copy-start(s32[1,4,2]{1,2,0:T(2,128)} %param.15) | copy-start | bytes 100
  22.0 8.7 %copy-start.3 = (f32[256,1024]{1,0:T(8,128)S(1)}, f32[256,1024]{1,0:T(8,128)}, u32[]{:S(2)}) copy-start(f32[256,1024]{1,0:T(8,128)} %refs_5_.3) | copy-start | bytes 3145732
  27.6 9.3 %collective-permute-start = (f32[128,512]{1,0:T(8,128)S(1)}, f32[128,512]{1,0:T(8,128)S(1)}, u32[]{:S(2)}, u32[]{:S(2)}) collective-permute-start(f32[128,512]{1,0:T(8,128)S(1)} %get-tuple-element.38), channel_id=1, source_target_pairs={{0,248},{8,0},{16,8},{24,16},{32,24},{40,32},{48,40},{56,48},{64,5... | collective-permute-start | bytes 786440 | tf_op jit(solution)/shard_map/ppermute | solution.py:420
  30.7 1.0 %copy-start.5 = (f32[128,512]{1,0:T(8,128)S(1)}, f32[128,512]{1,0:T(8,128)}, u32[]{:S(2)}) copy-start(f32[128,512]{1,0:T(8,128)} %copy-done.4) | copy-start | bytes 786436
  36.7 9.3 %collective-permute-start.5 = (f32[272,256]{1,0:T(8,128)S(1)}, f32[272,256]{1,0:T(8,128)S(1)}, u32[]{:S(2)}, u32[]{:S(2)}) collective-permute-start(f32[272,256]{1,0:T(8,128)S(1)} %get-tuple-element.46), channel_id=1, source_target_pairs={{0,8},{8,16},{16,24},{24,32},{32,40},{40,48},{48,56},{56,64},{64,7... | collective-permute-start | bytes 835592 | tf_op jit(solution)/shard_map/ppermute | solution.py:420
  36.8 9.2 %collective-permute-start.6 = (f32[136,256]{1,0:T(8,128)S(1)}, f32[136,256]{1,0:T(8,128)S(1)}, u32[]{:S(2)}, u32[]{:S(2)}) collective-permute-start(f32[136,256]{1,0:T(8,128)S(1)} %get-tuple-element.47), channel_id=1, source_target_pairs={{0,16},{8,24},{16,32},{24,40},{32,48},{40,56},{48,64},{56,72},{64,... | collective-permute-start | bytes 417800 | tf_op jit(solution)/shard_map/ppermute | solution.py:420
  44.0 16.8 %collective-permute-start.7 = (f32[272,512]{1,0:T(8,128)S(1)}, f32[272,512]{1,0:T(8,128)S(1)}, u32[]{:S(2)}, u32[]{:S(2)}) collective-permute-start(f32[272,512]{1,0:T(8,128)S(1)} %get-tuple-element.51), channel_id=1, source_target_pairs={{0,8},{8,16},{16,24},{24,32},{32,40},{40,48},{48,56},{56,64},{64,7... | collective-permute-start | bytes 1671176 | tf_op jit(solution)/shard_map/ppermute | solution.py:420
  44.1 16.7 %collective-permute-start.8 = (f32[136,512]{1,0:T(8,128)S(1)}, f32[136,512]{1,0:T(8,128)S(1)}, u32[]{:S(2)}, u32[]{:S(2)}) collective-permute-start(f32[136,512]{1,0:T(8,128)S(1)} %get-tuple-element.52), channel_id=1, source_target_pairs={{0,16},{8,24},{16,32},{24,40},{32,48},{40,56},{48,64},{56,72},{64,... | collective-permute-start | bytes 835592 | tf_op jit(solution)/shard_map/ppermute | solution.py:420
  44.2 7.6 %collective-permute-start.9 = (f32[8,768]{1,0:T(8,128)S(1)}, f32[8,768]{1,0:T(8,128)S(1)}, u32[]{:S(2)}, u32[]{:S(2)}) collective-permute-start(f32[8,768]{1,0:T(8,128)S(1)} %get-tuple-element.53), channel_id=1, source_target_pairs={{0,248},{8,0},{16,8},{24,16},{32,24},{40,32},{48,40},{56,48},{64,5... | collective-permute-start | bytes 73736 | tf_op jit(solution)/shard_map/ppermute | solution.py:420
  46.0 41.0 %copy-start = (bf16[512,256]{1,0:T(8,128)(2,1)S(1)}, bf16[512,256]{1,0:T(8,128)(2,1)}, u32[]{:S(2)}) copy-start(bf16[512,256]{1,0:T(8,128)(2,1)} %constant.4.clone.high_ref) | copy-start | bytes 786436
  46.0 41.0 %copy-start.1 = (bf16[512,256]{1,0:T(8,128)(2,1)S(1)}, bf16[512,256]{1,0:T(8,128)(2,1)}, u32[]{:S(2)}) copy-start(bf16[512,256]{1,0:T(8,128)(2,1)} %constant.5.clone.low_ref) | copy-start | bytes 786436
  60.8 26.1 %collective-permute-start.10 = (f32[272,640]{1,0:T(8,128)S(1)}, f32[272,640]{1,0:T(8,128)S(1)}, u32[]{:S(2)}, u32[]{:S(2)}) collective-permute-start(f32[272,640]{1,0:T(8,128)S(1)} %get-tuple-element.54), channel_id=1, source_target_pairs={{0,8},{8,16},{16,24},{24,32},{32,40},{40,48},{48,56},{56,64},{64,7... | collective-permute-start | bytes 2088968 | tf_op jit(solution)/shard_map/ppermute | solution.py:420
  62.3 24.6 %collective-permute-start.13 = (f32[264,384]{1,0:T(8,128)S(1)}, f32[264,384]{1,0:T(8,128)S(1)}, u32[]{:S(2)}, u32[]{:S(2)}) collective-permute-start(f32[264,384]{1,0:T(8,128)S(1)} %get-tuple-element.63), channel_id=1, source_target_pairs={{0,1},{1,2},{2,3},{3,4},{4,5},{5,6},{6,7},{7,0},{8,9},{9,10},{10,1... | collective-permute-start | bytes 1216520 | tf_op jit(solution)/shard_map/ppermute | solution.py:422
  63.3 23.7 %collective-permute-start.11 = (f32[136,640]{1,0:T(8,128)S(1)}, f32[136,640]{1,0:T(8,128)S(1)}, u32[]{:S(2)}, u32[]{:S(2)}) collective-permute-start(f32[136,640]{1,0:T(8,128)S(1)} %get-tuple-element.56), channel_id=1, source_target_pairs={{0,16},{8,24},{16,32},{24,40},{32,48},{40,56},{48,64},{56,72},{64,... | collective-permute-start | bytes 1044488 | tf_op jit(solution)/shard_map/ppermute | solution.py:420
  63.3 23.6 %collective-permute-start.12 = (f32[8,640]{1,0:T(8,128)S(1)}, f32[8,640]{1,0:T(8,128)S(1)}, u32[]{:S(2)}, u32[]{:S(2)}) collective-permute-start(f32[8,640]{1,0:T(8,128)S(1)} %get-tuple-element.58), channel_id=1, source_target_pairs={{0,248},{8,0},{16,8},{24,16},{32,24},{40,32},{48,40},{56,48},{64,5... | collective-permute-start | bytes 61448 | tf_op jit(solution)/shard_map/ppermute | solution.py:420
  64.1 5.0 %collective-permute-start.14 = (f32[8,256]{1,0:T(8,128)S(1)}, f32[8,256]{1,0:T(8,128)S(1)}, u32[]{:S(2)}, u32[]{:S(2)}) collective-permute-start(f32[8,256]{1,0:T(8,128)S(1)} %get-tuple-element.64), channel_id=1, source_target_pairs={{0,7},{1,0},{2,1},{3,2},{4,3},{5,4},{6,5},{7,6},{8,15},{9,8},{10,9... | collective-permute-start | bytes 24584 | tf_op jit(solution)/shard_map/ppermute | solution.py:422
where the time goes:
time: 90.1 us; the launch traced here: 89.8 us
  Pallas kernels  33.3 us (37%)
  waiting for transfers between devices  31.2 us (35%)
  starting transfers between devices  20.8 us (23%)
  local copies, waits for them, and re-layouts  4.39 us (5%)
    ppermute x11, waiting for transfers between devices, moved(): lax.ppermute(array, 'row', [(i, (i + by_row) % n_row) for i in range(n_ro...  30.4 us
    pallas_call x3, Pallas kernels, shifted(): pl.pallas_call(functools.partial(shifted_kernel, cells, origin, carried,...  17.9 us
    pallas_call x2, Pallas kernels, aligned(): pl.pallas_call(functools.partial(aligned_kernel, cells), in_specs=[SMEM,...  11 us
    ppermute x3, starting transfers between devices, moved(): lax.ppermute(array, 'col', [(i, (i + by_col) % n_col) for i in range(n_co...  8.53 us
    ppermute x1, starting transfers between devices, moved(): return lax.ppermute(array, ('row', 'col'), pairs)  6.73 us
    ppermute x11, starting transfers between devices, moved(): lax.ppermute(array, 'row', [(i, (i + by_row) % n_row) for i in range(n_ro...  5.56 us
    unnamed x22, local copies, waits for them, and re-layouts  3.38 us
    pallas_call x1, Pallas kernels, final(): pl.pallas_call(final_kernel, in_specs=[VMEM] * 10, out_specs=VMEM, out_sh...  2.81 us
  transfers between devices with their start and end apart: 15, of which 5 were waited for; matrix products, arithmetic and copies ran while one was open for 1% of the time, Pallas kernels for 28%

commit v1 on v0

--- a/solution.py
+++ b/solution.py
@@ -27,7 +27,7 @@
 SMEM = pl.BlockSpec(memory_space=pltpu.SMEM)
 ANY = pl.BlockSpec(memory_space=pl.ANY)
 HBM = pl.BlockSpec(memory_space=pltpu.HBM)
-PARAMS = pltpu.CompilerParams(vmem_limit_bytes=40 << 20)
+PARAMS = pltpu.CompilerParams(vmem_limit_bytes=24 << 20)
 
 
 def dot(a, b):
@@ -89,8 +89,11 @@
 
 def aligned_kernel(cells, shifts, widths, source, boxes, *refs):
     n = len(cells)
-    outs, refs = refs[: 4 if 0 in cells else 2], refs[4 if 0 in cells else 2 :]
-    base_ref, box_ref, mass_ref, vb_ref, tables, sems = refs
+    if 0 in cells:
+        outs, base_ref, refs = refs[:4], refs[4], refs[5:]
+    else:
+        base_ref, outs, refs = refs[0], refs[1:3], refs[3:]
+    box_ref, mass_ref, vb_ref, tables, sems = refs
     copies = []
     for i, j in enumerate(cells):
         copies.append((
@@ -101,10 +104,11 @@
     for pair in copies:
         for copy in pair:
             copy.start()
-    fill_base(base_ref)
+    if 0 in cells:
+        fill_base(base_ref)
     for i, j in enumerate(cells):
         fill_tables(
-            shifts[0, j, 0], shifts[0, j, 1], widths[0, j, 0], widths[0, j, 1], base_ref, tables[i])
+            shifts[0, 0, j], shifts[0, 1, j], widths[0, 0, j], widths[0, 1, j], base_ref, tables[i])
     scales = []
     for i in range(n):
         down = dot(tables[i][0][...], jnp.ones((S, HALF), BF16)).astype(BF16).astype(F32)
@@ -126,7 +130,8 @@
         for i in range(n):
             u[i] = forward(mass_ref[:, i * S : (i + 1) * S], tables[i], vb_ref.at[i])
     for i, j in enumerate(cells):
-        outs[0][:, i * S : (i + 1) * S] = u[i][:HALF]
+        outs[0][:HALF, i * S : (i + 1) * S] = u[i][:HALF]
+        outs[0][HALF:, i * S : (i + 1) * S] = mass_ref[:HALF, i * S : (i + 1) * S]
         outs[1][:, i * S : (i + 1) * S] = u[i][HALF:]
         if j == 0:
             for k in range(2):
@@ -139,18 +144,18 @@
         flops=cells * applies * 804_000_000, bytes_accessed=cells << 20, transcendentals=0)
 
 
-def aligned(cells, source, boxes, shifts, widths):
+def aligned(cells, source, boxes, shifts, widths, *base):
     n = len(cells)
-    half = jax.ShapeDtypeStruct((HALF, n * S), F32)
     corner = jax.ShapeDtypeStruct((S, HALF), F32)
-    shapes = [half, half] + ([corner, corner] if 0 in cells else [])
+    shapes = [jax.ShapeDtypeStruct((S, n * S), F32), jax.ShapeDtypeStruct((HALF, n * S), F32)]
+    if 0 in cells:
+        shapes += [corner, corner, jax.ShapeDtypeStruct((BASE, HALF), F32)]
     return pl.pallas_call(
         functools.partial(aligned_kernel, cells),
-        in_specs=[SMEM, SMEM, HBM, HBM],
+        in_specs=[SMEM, SMEM, HBM, HBM] + [VMEM] * len(base),
         out_specs=[VMEM] * len(shapes),
         out_shape=shapes,
         scratch_shapes=[
-            pltpu.VMEM((BASE, HALF), F32),
             pltpu.VMEM((n, BOX, BOX), F32),
             pltpu.VMEM((S, n * S), F32),
             pltpu.VMEM((n, BOX, BOX), BF16),
@@ -160,7 +165,7 @@
         compiler_params=PARAMS,
         cost_estimate=cost(n, 5),
         name="aligned",
-    )(shifts, widths, source, boxes)
+    )(shifts, widths, source, boxes, *base)
 
 
 def place(plan_ref, top, left, canvas_ref, first):
@@ -186,7 +191,7 @@
             before = now
 
 
-def shifted_kernel(cells, origin, carried, finals, kept, shifts, widths, boxes, *refs):
+def shifted_kernel(cells, origin, carried, finals, kept, shifts, widths, boxes, base_ref, *refs):
     n = len(cells)
     quads, refs = refs[: 8 * n], refs[8 * n :]
     upper_ref = None
@@ -197,21 +202,20 @@
     outs, refs = refs[:4], refs[4:]
     if kept:
         keep_ref, refs = refs[0], refs[1:]
-    base_ref, box_ref, mass_ref, ub_ref, vb_ref, v_ref, canvas_ref, tables, sems, out_sems = refs
+    box_ref, mass_ref, ub_ref, vb_ref, v_ref, canvas_ref, tables, sems, out_sems = refs
     copies = [
         pltpu.make_async_copy(boxes.at[0, j], box_ref.at[i], sems.at[i])
         for i, j in enumerate(cells)
     ]
     for copy in copies:
         copy.start()
-    fill_base(base_ref)
     canvas_ref[...] = jnp.zeros_like(canvas_ref)
     if carried:
         first, last = carried[0] - origin, carried[1] - origin
         canvas_ref[:REACH, first:last] = carry_ref[...]
     for i, j in enumerate(cells):
         fill_tables(
-            shifts[0, j, 0], shifts[0, j, 1], widths[0, j, 0], widths[0, j, 1], base_ref, tables[i])
+            shifts[0, 0, j], shifts[0, 1, j], widths[0, 0, j], widths[0, 1, j], base_ref, tables[i])
         for k in range(4):
             rows = slice(k // 2 * HALF, (k // 2 + 1) * HALF)
             cols = slice(k % 2 * HALF, (k % 2 + 1) * HALF)
@@ -233,11 +237,11 @@
     deep = lax.broadcasted_iota(jnp.int32, (BOX, S), 0)
     lane = lax.broadcasted_iota(jnp.int32, (S, BOX), 1)
     for i, j in enumerate(cells):
-        inner = jnp.where(deep < widths[0, j, 0], dot(tables[i][0][...], u[i]), 0.0).astype(BF16)
-        used = jnp.where(lane < widths[0, j, 1], tables[i][1][...], jnp.zeros((), BF16))
+        inner = jnp.where(deep < widths[0, 0, j], dot(tables[i][0][...], u[i]), 0.0).astype(BF16)
+        used = jnp.where(lane < widths[0, 1, j], tables[i][1][...], jnp.zeros((), BF16))
         v_ref[i] = v_ref[i] * dot(inner, used)
     for i, j in enumerate(cells):
-        place(v_ref.at[i], shifts[0, j, 0] + HALF, shifts[0, j, 1] + HALF, canvas_ref,
+        place(v_ref.at[i], shifts[0, 0, j] + HALF, shifts[0, 1, j] + HALF, canvas_ref,
               j * S - origin)
     writes = []
     at = 0
@@ -263,7 +267,7 @@
         copy.wait()
 
 
-def shifted(cells, boxes, shifts, widths, quads, carried=None, carry=None, finals=(), kept=None):
+def shifted(cells, boxes, shifts, widths, base, quads, carried=None, carry=None, finals=(), kept=None):
     n = len(cells)
     origin = min(j * S for j in cells)
     width = max(j * S + REACH for j in cells) - origin
@@ -284,11 +288,10 @@
     return pl.pallas_call(
         functools.partial(shifted_kernel, cells, origin, carried, finals, kept),
         grid=(1,),
-        in_specs=[SMEM, SMEM, HBM] + blocks,
+        in_specs=[SMEM, SMEM, HBM, VMEM] + blocks,
         out_specs=[ANY] * len(shapes),
         out_shape=shapes,
         scratch_shapes=[
-            pltpu.VMEM((BASE, HALF), F32),
             pltpu.VMEM((n, BOX, BOX), F32),
             pltpu.VMEM((n, S, S), F32),
             pltpu.VMEM((n, S, S), BF16),
@@ -302,7 +305,7 @@
         compiler_params=PARAMS,
         cost_estimate=cost(n, 7),
         name="shifted",
-    )(shifts, widths, boxes, *arrays)
+    )(shifts, widths, boxes, base, *arrays)
 
 
 def blur_weights():
@@ -327,8 +330,10 @@
 
 
 def edges_kernel(*refs):
-    (own3, next3, far3, own2, next2, far2, back2, main_ref, right_ref, east_ref, west_ref,
-     win_ref) = refs
+    (own3, next3, far3, own2, next2, far2, back2, next1, joined, main_ref, right_ref, east_ref,
+     west_ref, sum_ref, win_ref) = refs
+    sum_ref[:FAR] = next1[:FAR] + joined[...]
+    sum_ref[FAR:] = next1[FAR:]
 
     def outer(c, out):
         east_ref[:S, HALF + c : 2 * HALF + c] = out
@@ -352,13 +357,14 @@
 def edges(*arrays):
     return pl.pallas_call(
         edges_kernel,
-        in_specs=[VMEM] * 7,
-        out_specs=[VMEM] * 4,
+        in_specs=[VMEM] * 9,
+        out_specs=[VMEM] * 5,
         out_shape=[
             jax.ShapeDtypeStruct((S, 3 * HALF), F32),
             jax.ShapeDtypeStruct((S, HALF), F32),
             jax.ShapeDtypeStruct((S + RADIUS, 3 * HALF), F32),
             jax.ShapeDtypeStruct((RADIUS, S), F32),
+            jax.ShapeDtypeStruct((NEXT, REACH), F32),
         ],
         scratch_shapes=[pltpu.VMEM((NEXT, 2 * S), F32)],
         compiler_params=PARAMS,
@@ -438,16 +444,18 @@
 
 
 def on_device(source, boxes_a, shifts_a, widths_a, boxes_b, shifts_b, widths_b):
-    mtop = moved(source[:HALF], -1, 0)
+    shifts_a, widths_a, shifts_b, widths_b = (
+        jnp.swapaxes(array, 1, 2) for array in (shifts_a, widths_a, shifts_b, widths_b))
     boxes_a = pltpu.with_memory_space_constraint(boxes_a, pltpu.HBM)
     boxes_b = pltpu.with_memory_space_constraint(boxes_b, pltpu.HBM)
     masses = pltpu.with_memory_space_constraint(source, pltpu.HBM)
-    top03, bot03, left_top, left_bot = aligned((0, 3), masses, boxes_a, shifts_a, widths_a)
+    top03, bot03, left_top, left_bot, base = aligned(
+        (0, 3), masses, boxes_a, shifts_a, widths_a)
     rtop03 = moved(top03, -1, 0)
     east = moved(left_bot, 0, -1)
     diag = moved(left_top, -1, -1)
     top12, bot12 = aligned(
-        (1, 2), masses, boxes_a, behind(shifts_a, bot03), widths_a)
+        (1, 2), masses, boxes_a, shifts_a, widths_a, behind(base, bot03))
     rtop12 = moved(top12, -1, 0)
     own = [(bot03, 0), (bot03, 1), (bot12, 0), (bot12, 1), (bot12, 2), (bot12, 3), (bot03, 2),
            (bot03, 3), (east, 0)]
@@ -460,29 +468,32 @@
         quads[j] += [
             (source, (1, a)),
             (source, (1, b)) if j < 3 else (east, (1, 0)),
-            (mtop, (0, a)),
-            (mtop, (0, b)) if j < 3 else (diag, (1, 0)),
         ]
+        quads[j] += [(array, (1, at)) for array, at in (below[a], below[b])]
     own3, next3, far3, back3, carry = shifted(
-        (3,), boxes_b, behind(shifts_b, bot12), widths_b, quads,
+        (3,), boxes_b, shifts_b, widths_b, behind(base, bot12), quads,
         finals=((1152, 1408),), kept=(768, 1152))
     next3 = moved(next3, 1, 0)
     far3 = moved(far3, 2, 0)
     own2, next2, far2, back2, carry = shifted(
-        (0, 2), boxes_b, shifts_b, widths_b, quads,
+        (0, 2), boxes_b, shifts_b, widths_b, base, quads,
         carried=(768, 1152), carry=(carry, back3), finals=((0, 256), (896, 1152)),
         kept=(256, 896))
     next2 = moved(next2, 1, 0)
     far2 = moved(far2, 2, 0)
     rback2 = moved(back2, -1, 0)
     own1, next1, far1, back1 = shifted(
-        (1,), boxes_b, shifts_b, widths_b, quads,
+        (1,), boxes_b, shifts_b, widths_b, base, quads,
         carried=(256, 896), carry=(behind(carry, next3, far3),),
         finals=((256, 896),))
-    next1 = moved(behind(next1, next2, far2, rback2), 1, 0)
-    far1 = moved(behind(far1, next2, far2, rback2), 2, 0)
-    back1 = moved(behind(back1, next2, far2, rback2), -1, 0)
-    main, right, east, west = edges(own3, next3, far3, own2, next2, far2, rback2)
+    n_row = lax.axis_size("row")
+    joined = lax.ppermute(
+        behind(far1, far2, rback2), "row", [(i, i + 1) for i in range(0, n_row, 2)])
+    far1 = lax.ppermute(far1, "row", [(i, (i + 2) % n_row) for i in range(1, n_row, 2)])
+    back1 = moved(back1, -1, 0)
+    main, right, east, west, next1 = edges(
+        own3, next3, far3, own2, next2, far2, rback2, next1, joined)
+    next1 = moved(next1, 1, 0)
     return final(
         source.shape[1], own1, next1, far1, back1, main, right, moved(east, 0, 1),
         moved(west, 0, -1))

time: 90.1 us -> 85.6 us (0.950)
  waiting for transfers between devices: 31.2 us -> 26.3 us
  starting transfers between devices: 20.8 us -> 24.7 us
  local copies, waits for them, and re-layouts: 4.39 us -> 1.38 us
    ppermute x11 -> x9, waiting for transfers between devices: 30.4 us -> 20.8 us  [moved(): lax.ppermute(array, 'row', [(i, (i + by_row) % n_row) for i in range(n_ro...]
    ppermute x0 -> x2, waiting for transfers between devices: none -> 5.49 us  [the longest x1 5.49 us: on_device(): lax.ppermute(behind(far1, far2, rback2), 'row', [(i, i + 1) for i in rang...]
    ppermute x1, starting transfers between devices: 6.73 us -> 1.38 us  [moved(): return lax.ppermute(array, ('row', 'col'), pairs)]
    ppermute x11 -> x9, starting transfers between devices: 5.56 us -> 8.83 us  [moved(): lax.ppermute(array, 'row', [(i, (i + by_row) % n_row) for i in range(n_ro...]
    ppermute x0 -> x2, starting transfers between devices: none -> 3.19 us  [the longest x1 1.91 us: on_device(): lax.ppermute(far1, 'row', [(i, (i + 2) % n_row) for i in range(1, n_row,...]
    ppermute x3, starting transfers between devices: 8.53 us -> 11.3 us  [moved(): lax.ppermute(array, 'col', [(i, (i + by_col) % n_col) for i in range(n_co...]
    unnamed x22 -> x14, local copies, waits for them, and re-layouts: 3.38 us -> 1.38 us
  transfers between devices with their start and end apart: 15 -> 15, of which waited for: 5 -> 5; matrix products, arithmetic and copies ran while one was open for 1% -> 0% of each run, Pallas kernels for 28% -> 27%
where the time goes in v1:
time: 85.6 us; the launch traced here: 85.3 us
  Pallas kernels  32.8 us (38%)
  waiting for transfers between devices  26.3 us (31%)
  starting transfers between devices  24.7 us (29%)
  local copies, waits for them, and re-layouts  1.38 us (2%)
    ppermute x9, waiting for transfers between devices, moved(): lax.ppermute(array, 'row', [(i, (i + by_row) % n_row) for i in range(n_ro...  20.8 us
    pallas_call x3, Pallas kernels, shifted(): pl.pallas_call(functools.partial(shifted_kernel, cells, origin, carried,...  17.1 us
    pallas_call x2, Pallas kernels, aligned(): pl.pallas_call(functools.partial(aligned_kernel, cells), in_specs=[SMEM,...  11.3 us
    ppermute x3, starting transfers between devices, moved(): lax.ppermute(array, 'col', [(i, (i + by_col) % n_col) for i in range(n_co...  11.3 us
    ppermute x9, starting transfers between devices, moved(): lax.ppermute(array, 'row', [(i, (i + by_row) % n_row) for i in range(n_ro...  8.83 us
    ppermute x1, waiting for transfers between devices, on_device(): lax.ppermute(behind(far1, far2, rback2), 'row', [(i, i + 1) for i in rang...  5.49 us
    pallas_call x1, Pallas kernels, final(): pl.pallas_call(final_kernel, in_specs=[VMEM] * 10, out_specs=VMEM, out_sh...  2.78 us
    ppermute x1, starting transfers between devices, on_device(): lax.ppermute(far1, 'row', [(i, (i + 2) % n_row) for i in range(1, n_row,...  1.91 us
  transfers between devices with their start and end apart: 15, of which 5 were waited for; matrix products, arithmetic and copies ran while one was open for 0% of the time, Pallas kernels for 27%

profile of v1, /device:TPU:1, one launch (start us, length us, event | category | flops | bytes accessed | tf_op | source)
XLA Modules:
  0.0 85.3 jit_solution(14223010553700871478)
XLA Ops:
  0.0 0.0 copy-start.3
  0.0 0.7 copy-done.3
  0.7 0.0 copy-start.4
  0.7 0.7 copy-done.4
  1.4 5.7 %aligned.2 = (f32[256,512]{1,0:T(8,128)S(1)}, f32[128,512]{1,0:T(8,128)S(1)}, f32[256,128]{1,0:T(8,128)S(1)}, f32[256,128]{1,0:T(8,128)S(1)}, f32[904,128]{1,0:T(8,128)S(1)}) custom-call(s32[1,2,4]{2,1,0:T(2,128)S(1)} %bitcast.4, s32[1,2,4]{2,1,0:T(2,128)S(1)} %bitcast.6, f32[256,1024]{1,0:T(8,128)} %refs_5_.3, f32[1,4,512,512]{3,2,1,0:T(8,128)} %boxes.6), custom_call_target="tpu_custom_call" | custom-call | flops 8040000000 | bytes 2097152 | tf_op jit(solution)/shard_map/aligned/pallas_call | solution.py:153
  7.1 6.0 %collective-permute-start.2 = (f32[256,128]{1,0:T(8,128)S(1)}, f32[256,128]{1,0:T(8,128)S(1)}, u32[]{:S(2)}, u32[]{:S(2)}) collective-permute-start(f32[256,128]{1,0:T(8,128)S(1)} %get-tuple-element.42), channel_id=1, source_target_pairs={{0,7},{1,0},{2,1},{3,2},{4,3},{5,4},{6,5},{7,6},{8,15},{9,8},{10,9... | collective-permute-start | bytes 393224 | tf_op jit(solution)/shard_map/ppermute | solution.py:428
  13.1 1.4 %collective-permute-start.3 = (f32[256,128]{1,0:T(8,128)S(1)}, f32[256,128]{1,0:T(8,128)S(1)}, u32[]{:S(2)}, u32[]{:S(2)}) collective-permute-start(f32[256,128]{1,0:T(8,128)S(1)} %get-tuple-element.43), channel_id=1, source_target_pairs={{0,255},{1,248},{2,249},{3,250},{4,251},{5,252},{6,253},{7,254},{8... | collective-permute-start | bytes 393224 | tf_op jit(solution)/shard_map/ppermute | solution.py:434
  14.5 4.7 %collective-permute-start.1 = (f32[256,512]{1,0:T(8,128)S(1)}, f32[256,512]{1,0:T(8,128)S(1)}, u32[]{:S(2)}, u32[]{:S(2)}) collective-permute-start(f32[256,512]{1,0:T(8,128)S(1)} %get-tuple-element.40), channel_id=1, source_target_pairs={{0,248},{8,0},{16,8},{24,16},{32,24},{40,32},{48,40},{56,48},{64,5... | collective-permute-start | bytes 1572872 | tf_op jit(solution)/shard_map/ppermute | solution.py:426
  19.2 0.0 copy-start.2
  19.2 0.0 copy-start.5
  19.2 0.0 copy-start.6
  19.2 5.6 %aligned.3 = (f32[256,512]{1,0:T(8,128)S(1)}, f32[128,512]{1,0:T(8,128)S(1)}) custom-call(s32[1,2,4]{2,1,0:T(2,128)S(1)} %bitcast.5, s32[1,2,4]{2,1,0:T(2,128)S(1)} %bitcast.7, f32[256,1024]{1,0:T(8,128)} %refs_5_.3, f32[1,4,512,512]{3,2,1,0:T(8,128)} %boxes.6, f32[904,128]{1,0:T(8,128)S(1)} %get-tuple-element.41.refs_0_.base_ref), custom_call_target="tpu_custom_call" | custom-call | flops 8040000000 | bytes 2097152 | tf_op jit(solution)/shard_map/aligned/pallas_call | solution.py:153
  24.8 1.7 %collective-permute-start = (f32[256,512]{1,0:T(8,128)S(1)}, f32[256,512]{1,0:T(8,128)S(1)}, u32[]{:S(2)}, u32[]{:S(2)}) collective-permute-start(f32[256,512]{1,0:T(8,128)S(1)} %get-tuple-element.39), channel_id=1, source_target_pairs={{0,248},{8,0},{16,8},{24,16},{32,24},{40,32},{48,40},{56,48},{64,5... | collective-permute-start | bytes 1572872 | tf_op jit(solution)/shard_map/ppermute | solution.py:426
  26.5 0.0 collective-permute-done.2.refs_1_.refs_5_
  26.5 0.0 collective-permute-done.3.refs_3_.refs_7_
  26.5 0.0 collective-permute-done.1.refs_2_.refs_6_.refs_11_.refs_15_
  26.5 0.0 copy-done.2
  26.5 0.0 copy-done.5
  26.5 0.0 copy-done.6
  26.5 4.9 %shifted.3 = (f32[264,256]{1,0:T(8,128)S(1)}, f32[272,256]{1,0:T(8,128)S(1)}, f32[136,256]{1,0:T(8,128)S(1)}, f32[8,256]{1,0:T(8,128)S(1)}, f32[640,384]{1,0:T(8,128)S(1)}) custom-call(s32[1,2,4]{2,1,0:T(2,128)S(1)} %bitcast.8, s32[1,2,4]{2,1,0:T(2,128)S(1)} %bitcast.11, f32[1,4,512,512]{3,2,1,0:T(8,128)} %boxes.9, ...), custom_call_target="tpu_custom_call" | custom-call | flops 5628000256 | bytes 1048576 | tf_op jit(solution)/shard_map/shifted/pallas_call | solution.py:288
  31.4 0.1 collective-permute-start.5
  31.5 0.4 collective-permute-start.4
  31.9 1.8 %collective-permute-done.refs_3_.refs_7_.refs_10_.refs_14_.refs_2_.refs_6_ = f32[256,512]{1,0:T(8,128)S(1)} collective-permute-done((f32[256,512]{1,0:T(8,128)S(1)}, f32[256,512]{1,0:T(8,128)S(1)}, u32[]{:S(2)}, u32[]{:S(2)}) %collective-permute-start) | collective-permute-done | bytes 524320 | tf_op jit(solution)/shard_map/ppermute | solution.py:426
  33.7 6.9 %shifted.4 = (f32[264,512]{1,0:T(8,128)S(1)}, f32[272,512]{1,0:T(8,128)S(1)}, f32[136,512]{1,0:T(8,128)S(1)}, f32[8,768]{1,0:T(8,128)S(1)}, f32[640,640]{1,0:T(8,128)S(1)}) custom-call(s32[1,2,4]{2,1,0:T(2,128)S(1)} %bitcast.9, s32[1,2,4]{2,1,0:T(2,128)S(1)} %bitcast.12, f32[1,4,512,512]{3,2,1,0:T(8,128)} %boxes.9, ...), custom_call_target="tpu_custom_call" | custom-call | flops 11256000512 | bytes 2097152 | tf_op jit(solution)/shard_map/shifted/pallas_call | solution.py:288
  40.6 0.1 collective-permute-start.8
  40.7 0.1 collective-permute-start.7
  40.8 1.7 %collective-permute-start.6 = (f32[272,512]{1,0:T(8,128)S(1)}, f32[272,512]{1,0:T(8,128)S(1)}, u32[]{:S(2)}, u32[]{:S(2)}) collective-permute-start(f32[272,512]{1,0:T(8,128)S(1)} %get-tuple-element.53), channel_id=1, source_target_pairs={{0,8},{8,16},{16,24},{24,32},{32,40},{40,48},{48,56},{56,64},{64,7... | collective-permute-start | bytes 1671176 | tf_op jit(solution)/shard_map/ppermute | solution.py:426
  42.5 0.0 collective-permute-done.5.refs_2_
  42.5 0.0 collective-permute-done.4.refs_1_
  42.5 0.0 copy-start
  42.5 0.0 copy-start.1
  42.5 5.3 %shifted.5 = (f32[264,640]{1,0:T(8,128)S(1)}, f32[272,640]{1,0:T(8,128)S(1)}, f32[136,640]{1,0:T(8,128)S(1)}, f32[8,640]{1,0:T(8,128)S(1)}) custom-call(s32[1,2,4]{2,1,0:T(2,128)S(1)} %bitcast.10, s32[1,2,4]{2,1,0:T(2,128)S(1)} %bitcast.13, f32[1,4,512,512]{3,2,1,0:T(8,128)} %boxes.9, f32[904,128]{1,0:T(8,128)S(1)} %get-tuple-element.41.refs_0_.base_ref, ...), custom_call_target="tpu_custom_call" | custom-call | flops 5628000256 | bytes 1048576 | tf_op jit(solution)/shard_map/shifted/pallas_call | solution.py:288
  47.8 0.0 collective-permute-done.8.refs_6_
  47.8 0.6 collective-permute-done.7.refs_5_
  48.4 1.3 %collective-permute-start.9 = (f32[136,640]{1,0:T(8,128)S(1)}, f32[136,640]{1,0:T(8,128)S(1)}, u32[]{:S(2)}, u32[]{:S(2)}) collective-permute-start(f32[136,640]{1,0:T(8,128)S(1)} %get-tuple-element.58), channel_id=1, source_target_pairs={{0,8},{16,24},{32,40},{48,56},{64,72},{80,88},{96,104},{112,120},{... | collective-permute-start | bytes 1044488 | tf_op jit(solution)/shard_map/ppermute | solution.py:490
  49.7 3.6 %collective-permute-done.6.refs_4_ = f32[272,512]{1,0:T(8,128)S(1)} collective-permute-done((f32[272,512]{1,0:T(8,128)S(1)}, f32[272,512]{1,0:T(8,128)S(1)}, u32[]{:S(2)}, u32[]{:S(2)}) %collective-permute-start.6) | collective-permute-done | bytes 557088 | tf_op jit(solution)/shard_map/ppermute | solution.py:426
  53.3 5.5 %collective-permute-done.9.refs_8_ = f32[136,640]{1,0:T(8,128)S(1)} collective-permute-done((f32[136,640]{1,0:T(8,128)S(1)}, f32[136,640]{1,0:T(8,128)S(1)}, u32[]{:S(2)}, u32[]{:S(2)}) %collective-permute-start.9) | collective-permute-done | bytes 348192 | tf_op jit(solution)/shard_map/ppermute | solution.py:490
  58.8 1.5 %edges.1 = (f32[256,384]{1,0:T(8,128)S(1)}, f32[256,128]{1,0:T(8,128)S(1)}, f32[264,384]{1,0:T(8,128)S(1)}, f32[8,256]{1,0:T(8,128)S(1)}, f32[272,640]{1,0:T(8,128)S(1)}) custom-call(f32[264,256]{1,0:T(8,128)S(1)} %get-tuple-element.51.refs_0_, f32[272,256]{1,0:T(8,128)S(1)} %collective-permute-done.4.refs_1_, ...), custom_call_target="tpu_custom_call" | custom-call | tf_op jit(solution)/shard_map/edges/pallas_call | solution.py:358
  60.4 0.1 collective-permute-start.10
  60.4 0.9 %collective-permute-start.13 = (f32[264,384]{1,0:T(8,128)S(1)}, f32[264,384]{1,0:T(8,128)S(1)}, u32[]{:S(2)}, u32[]{:S(2)}) collective-permute-start(f32[264,384]{1,0:T(8,128)S(1)} %get-tuple-element.63), channel_id=1, source_target_pairs={{0,1},{1,2},{2,3},{3,4},{4,5},{5,6},{6,7},{7,0},{8,9},{9,10},{10,1... | collective-permute-start | bytes 1216520 | tf_op jit(solution)/shard_map/ppermute | solution.py:428
  61.3 1.9 %collective-permute-start.11 = (f32[136,640]{1,0:T(8,128)S(1)}, f32[136,640]{1,0:T(8,128)S(1)}, u32[]{:S(2)}, u32[]{:S(2)}) collective-permute-start(f32[136,640]{1,0:T(8,128)S(1)} %get-tuple-element.58), channel_id=1, source_target_pairs={{8,24},{24,40},{40,56},{56,72},{72,88},{88,104},{104,120},{120,136... | collective-permute-start | bytes 1044488 | tf_op jit(solution)/shard_map/ppermute | solution.py:492
  63.2 0.1 collective-permute-start.12
  63.3 4.4 %collective-permute-start.14 = (f32[8,256]{1,0:T(8,128)S(1)}, f32[8,256]{1,0:T(8,128)S(1)}, u32[]{:S(2)}, u32[]{:S(2)}) collective-permute-start(f32[8,256]{1,0:T(8,128)S(1)} %get-tuple-element.64), channel_id=1, source_target_pairs={{0,7},{1,0},{2,1},{3,2},{4,3},{5,4},{6,5},{7,6},{8,15},{9,8},{10,9... | collective-permute-start | bytes 24584 | tf_op jit(solution)/shard_map/ppermute | solution.py:428
  67.7 14.8 %collective-permute-done.12.back1 = f32[8,640]{1,0:T(8,128)S(1)} collective-permute-done((f32[8,640]{1,0:T(8,128)S(1)}, f32[8,640]{1,0:T(8,128)S(1)}, u32[]{:S(2)}, u32[]{:S(2)}) %collective-permute-start.12) | collective-permute-done | bytes 20512 | tf_op jit(solution)/shard_map/ppermute | solution.py:426
  82.5 0.0 collective-permute-done.11.far1
  82.5 0.0 collective-permute-done.14.west_ref
  82.5 0.0 collective-permute-done.13.east_ref
  82.5 0.0 collective-permute-done.10.next1
  82.5 0.0 copy-done
  82.5 0.0 copy-done.1
  82.6 2.8 %final.1 = f32[256,1024]{1,0:T(8,128)} custom-call(f32[264,640]{1,0:T(8,128)S(1)} %get-tuple-element.50.own1, f32[272,640]{1,0:T(8,128)S(1)} %collective-permute-done.10.next1, f32[136,640]{1,0:T(8,128)S(1)} %collective-permute-done.11.far1, f32[8,640]{1,0:T(8,128)S(1)} %collective-permute-done.12.back1, f32[256,384]{1,0:T(8,128)S(1)} %get-tuple-element.61.main_ref, ...), custom_call_target="tpu_custom_call" | custom-call | tf_op jit(solution)/shard_map/final/pallas_call | solution.py:409
Async XLA Ops:
  0.0 0.7 copy-start.3
  0.7 0.7 copy-start.4
  7.1 19.4 %collective-permute-start.2 = (f32[256,128]{1,0:T(8,128)S(1)}, f32[256,128]{1,0:T(8,128)S(1)}, u32[]{:S(2)}, u32[]{:S(2)}) collective-permute-start(f32[256,128]{1,0:T(8,128)S(1)} %get-tuple-element.42), channel_id=1, source_target_pairs={{0,7},{1,0},{2,1},{3,2},{4,3},{5,4},{6,5},{7,6},{8,15},{9,8},{10,9... | collective-permute-start | bytes 393224 | tf_op jit(solution)/shard_map/ppermute | solution.py:428
  13.1 13.4 %collective-permute-start.3 = (f32[256,128]{1,0:T(8,128)S(1)}, f32[256,128]{1,0:T(8,128)S(1)}, u32[]{:S(2)}, u32[]{:S(2)}) collective-permute-start(f32[256,128]{1,0:T(8,128)S(1)} %get-tuple-element.43), channel_id=1, source_target_pairs={{0,255},{1,248},{2,249},{3,250},{4,251},{5,252},{6,253},{7,254},{8... | collective-permute-start | bytes 393224 | tf_op jit(solution)/shard_map/ppermute | solution.py:434
  14.5 12.0 %collective-permute-start.1 = (f32[256,512]{1,0:T(8,128)S(1)}, f32[256,512]{1,0:T(8,128)S(1)}, u32[]{:S(2)}, u32[]{:S(2)}) collective-permute-start(f32[256,512]{1,0:T(8,128)S(1)} %get-tuple-element.40), channel_id=1, source_target_pairs={{0,248},{8,0},{16,8},{24,16},{32,24},{40,32},{48,40},{56,48},{64,5... | collective-permute-start | bytes 1572872 | tf_op jit(solution)/shard_map/ppermute | solution.py:426
  19.2 7.3 %copy-start.2 = (f32[256,1024]{1,0:T(8,128)S(1)}, f32[256,1024]{1,0:T(8,128)}, u32[]{:S(2)}) copy-start(f32[256,1024]{1,0:T(8,128)} %refs_5_.3) | copy-start | bytes 3145732
  19.2 7.3 %copy-start.5 = (s32[1,4,2]{1,2,0:T(2,128)S(1)}, s32[1,4,2]{1,2,0:T(2,128)}, u32[]{:S(2)}) copy-start(s32[1,4,2]{1,2,0:T(2,128)} %param.14) | copy-start | bytes 100
  19.2 7.3 %copy-start.6 = (s32[1,4,2]{1,2,0:T(2,128)S(1)}, s32[1,4,2]{1,2,0:T(2,128)}, u32[]{:S(2)}) copy-start(s32[1,4,2]{1,2,0:T(2,128)} %param.15) | copy-start | bytes 100
  24.8 8.9 %collective-permute-start = (f32[256,512]{1,0:T(8,128)S(1)}, f32[256,512]{1,0:T(8,128)S(1)}, u32[]{:S(2)}, u32[]{:S(2)}) collective-permute-start(f32[256,512]{1,0:T(8,128)S(1)} %get-tuple-element.39), channel_id=1, source_target_pairs={{0,248},{8,0},{16,8},{24,16},{32,24},{40,32},{48,40},{56,48},{64,5... | collective-permute-start | bytes 1572872 | tf_op jit(solution)/shard_map/ppermute | solution.py:426
  31.4 11.1 %collective-permute-start.5 = (f32[136,256]{1,0:T(8,128)S(1)}, f32[136,256]{1,0:T(8,128)S(1)}, u32[]{:S(2)}, u32[]{:S(2)}) collective-permute-start(f32[136,256]{1,0:T(8,128)S(1)} %get-tuple-element.48), channel_id=1, source_target_pairs={{0,16},{8,24},{16,32},{24,40},{32,48},{40,56},{48,64},{56,72},{64,... | collective-permute-start | bytes 417800 | tf_op jit(solution)/shard_map/ppermute | solution.py:426
  31.5 11.0 %collective-permute-start.4 = (f32[272,256]{1,0:T(8,128)S(1)}, f32[272,256]{1,0:T(8,128)S(1)}, u32[]{:S(2)}, u32[]{:S(2)}) collective-permute-start(f32[272,256]{1,0:T(8,128)S(1)} %get-tuple-element.47), channel_id=1, source_target_pairs={{0,8},{8,16},{16,24},{24,32},{32,40},{40,48},{48,56},{56,64},{64,7... | collective-permute-start | bytes 835592 | tf_op jit(solution)/shard_map/ppermute | solution.py:426
  40.6 7.2 %collective-permute-start.8 = (f32[8,768]{1,0:T(8,128)S(1)}, f32[8,768]{1,0:T(8,128)S(1)}, u32[]{:S(2)}, u32[]{:S(2)}) collective-permute-start(f32[8,768]{1,0:T(8,128)S(1)} %get-tuple-element.55), channel_id=1, source_target_pairs={{0,248},{8,0},{16,8},{24,16},{32,24},{40,32},{48,40},{56,48},{64,5... | collective-permute-start | bytes 73736 | tf_op jit(solution)/shard_map/ppermute | solution.py:426
  40.7 7.7 %collective-permute-start.7 = (f32[136,512]{1,0:T(8,128)S(1)}, f32[136,512]{1,0:T(8,128)S(1)}, u32[]{:S(2)}, u32[]{:S(2)}) collective-permute-start(f32[136,512]{1,0:T(8,128)S(1)} %get-tuple-element.54), channel_id=1, source_target_pairs={{0,16},{8,24},{16,32},{24,40},{32,48},{40,56},{48,64},{56,72},{64,... | collective-permute-start | bytes 835592 | tf_op jit(solution)/shard_map/ppermute | solution.py:426
  40.8 12.5 %collective-permute-start.6 = (f32[272,512]{1,0:T(8,128)S(1)}, f32[272,512]{1,0:T(8,128)S(1)}, u32[]{:S(2)}, u32[]{:S(2)}) collective-permute-start(f32[272,512]{1,0:T(8,128)S(1)} %get-tuple-element.53), channel_id=1, source_target_pairs={{0,8},{8,16},{16,24},{24,32},{32,40},{40,48},{48,56},{56,64},{64,7... | collective-permute-start | bytes 1671176 | tf_op jit(solution)/shard_map/ppermute | solution.py:426
  42.5 40.1 %copy-start = (bf16[512,256]{1,0:T(8,128)(2,1)S(1)}, bf16[512,256]{1,0:T(8,128)(2,1)}, u32[]{:S(2)}) copy-start(bf16[512,256]{1,0:T(8,128)(2,1)} %constant.5.clone.low_ref) | copy-start | bytes 786436
  42.5 40.1 %copy-start.1 = (bf16[512,256]{1,0:T(8,128)(2,1)S(1)}, bf16[512,256]{1,0:T(8,128)(2,1)}, u32[]{:S(2)}) copy-start(bf16[512,256]{1,0:T(8,128)(2,1)} %constant.4.clone.high_ref) | copy-start | bytes 786436
  48.4 10.4 %collective-permute-start.9 = (f32[136,640]{1,0:T(8,128)S(1)}, f32[136,640]{1,0:T(8,128)S(1)}, u32[]{:S(2)}, u32[]{:S(2)}) collective-permute-start(f32[136,640]{1,0:T(8,128)S(1)} %get-tuple-element.58), channel_id=1, source_target_pairs={{0,8},{16,24},{32,40},{48,56},{64,72},{80,88},{96,104},{112,120},{... | collective-permute-start | bytes 1044488 | tf_op jit(solution)/shard_map/ppermute | solution.py:490
  60.4 22.2 %collective-permute-start.10 = (f32[272,640]{1,0:T(8,128)S(1)}, f32[272,640]{1,0:T(8,128)S(1)}, u32[]{:S(2)}, u32[]{:S(2)}) collective-permute-start(f32[272,640]{1,0:T(8,128)S(1)} %get-tuple-element.59), channel_id=1, source_target_pairs={{0,8},{8,16},{16,24},{24,32},{32,40},{40,48},{48,56},{56,64},{64,7... | collective-permute-start | bytes 2088968 | tf_op jit(solution)/shard_map/ppermute | solution.py:426
  60.4 22.1 %collective-permute-start.13 = (f32[264,384]{1,0:T(8,128)S(1)}, f32[264,384]{1,0:T(8,128)S(1)}, u32[]{:S(2)}, u32[]{:S(2)}) collective-permute-start(f32[264,384]{1,0:T(8,128)S(1)} %get-tuple-element.63), channel_id=1, source_target_pairs={{0,1},{1,2},{2,3},{3,4},{4,5},{5,6},{6,7},{7,0},{8,9},{9,10},{10,1... | collective-permute-start | bytes 1216520 | tf_op jit(solution)/shard_map/ppermute | solution.py:428
  61.3 21.2 %collective-permute-start.11 = (f32[136,640]{1,0:T(8,128)S(1)}, f32[136,640]{1,0:T(8,128)S(1)}, u32[]{:S(2)}, u32[]{:S(2)}) collective-permute-start(f32[136,640]{1,0:T(8,128)S(1)} %get-tuple-element.58), channel_id=1, source_target_pairs={{8,24},{24,40},{40,56},{56,72},{72,88},{88,104},{104,120},{120,136... | collective-permute-start | bytes 1044488 | tf_op jit(solution)/shard_map/ppermute | solution.py:492
  63.2 19.3 %collective-permute-start.12 = (f32[8,640]{1,0:T(8,128)S(1)}, f32[8,640]{1,0:T(8,128)S(1)}, u32[]{:S(2)}, u32[]{:S(2)}) collective-permute-start(f32[8,640]{1,0:T(8,128)S(1)} %get-tuple-element.60), channel_id=1, source_target_pairs={{0,248},{8,0},{16,8},{24,16},{32,24},{40,32},{48,40},{56,48},{64,5... | collective-permute-start | bytes 61448 | tf_op jit(solution)/shard_map/ppermute | solution.py:426
  63.3 19.2 %collective-permute-start.14 = (f32[8,256]{1,0:T(8,128)S(1)}, f32[8,256]{1,0:T(8,128)S(1)}, u32[]{:S(2)}, u32[]{:S(2)}) collective-permute-start(f32[8,256]{1,0:T(8,128)S(1)} %get-tuple-element.64), channel_id=1, source_target_pairs={{0,7},{1,0},{2,1},{3,2},{4,3},{5,4},{6,5},{7,6},{8,15},{9,8},{10,9... | collective-permute-start | bytes 24584 | tf_op jit(solution)/shard_map/ppermute | solution.py:428

commit v2 on v1

--- a/solution.py
+++ b/solution.py
@@ -87,22 +87,33 @@
     return mass / dot(inner, tables[3][...])
 
 
-def aligned_kernel(cells, shifts, widths, source, boxes, *refs):
+def fetch(boxes, cells, ref, sems):
+    copies = [
+        pltpu.make_async_copy(boxes.at[0, j], ref.at[i], sems.at[i]) for i, j in enumerate(cells)
+    ]
+    for copy in copies:
+        copy.start()
+    return copies
+
+
+def aligned_kernel(cells, later, shifts, widths, source, boxes, later_boxes, *refs):
     n = len(cells)
     if 0 in cells:
-        outs, base_ref, refs = refs[:4], refs[4], refs[5:]
+        outs, base_ref, later_ref, box_ref, refs = refs[:4], refs[4], refs[5], refs[6], refs[7:]
     else:
-        base_ref, outs, refs = refs[0], refs[1:3], refs[3:]
-    box_ref, mass_ref, vb_ref, tables, sems = refs
+        base_ref, outs, later_ref, refs = refs[0], refs[1:3], refs[3], refs[4:]
+        box_ref = boxes
+    mass_ref, vb_ref, tables, sems, later_sems = refs
     copies = []
     for i, j in enumerate(cells):
-        copies.append((
-            pltpu.make_async_copy(boxes.at[0, j], box_ref.at[i], sems.at[i, 0]),
+        copies.append([
             pltpu.make_async_copy(
                 source.at[:, pl.ds(j * S, S)], mass_ref.at[:, pl.ds(i * S, S)], sems.at[i, 1]),
-        ))
+        ])
+        if 0 in cells:
+            copies[i].append(pltpu.make_async_copy(boxes.at[0, j], box_ref.at[i], sems.at[i, 0]))
     for pair in copies:
-        for copy in pair:
+        for copy in reversed(pair):
             copy.start()
     if 0 in cells:
         fill_base(base_ref)
@@ -120,6 +131,8 @@
             if step == 0:
                 for copy in copies[i]:
                     copy.wait()
+                if i == n - 1:
+                    later_copies = fetch(later_boxes, later, later_ref, later_sems)
                 down, across = scales[i]
                 for c in range(0, BOX, HALF):
                     v = box_ref[i, c : c + HALF] * down[c : c + HALF] * across
@@ -137,6 +150,8 @@
             for k in range(2):
                 outs[2 + k][:HALF] = u[i][k * HALF : (k + 1) * HALF, :HALF]
                 outs[2 + k][HALF:] = mass_ref[k * HALF : (k + 1) * HALF, i * S : i * S + HALF]
+    for copy in later_copies:
+        copy.wait()
 
 
 def cost(cells, applies):
@@ -144,28 +159,31 @@
         flops=cells * applies * 804_000_000, bytes_accessed=cells << 20, transcendentals=0)
 
 
-def aligned(cells, source, boxes, shifts, widths, *base):
+def aligned(cells, later, source, boxes, later_boxes, shifts, widths, *base):
     n = len(cells)
     corner = jax.ShapeDtypeStruct((S, HALF), F32)
     shapes = [jax.ShapeDtypeStruct((S, n * S), F32), jax.ShapeDtypeStruct((HALF, n * S), F32)]
+    scratch = []
     if 0 in cells:
         shapes += [corner, corner, jax.ShapeDtypeStruct((BASE, HALF), F32)]
+        scratch.append(pltpu.VMEM((n, BOX, BOX), F32))
+    shapes.append(jax.ShapeDtypeStruct((len(later), BOX, BOX), F32))
     return pl.pallas_call(
-        functools.partial(aligned_kernel, cells),
-        in_specs=[SMEM, SMEM, HBM, HBM] + [VMEM] * len(base),
+        functools.partial(aligned_kernel, cells, later),
+        in_specs=[SMEM, SMEM, HBM, HBM if 0 in cells else VMEM, HBM] + [VMEM] * len(base),
         out_specs=[VMEM] * len(shapes),
         out_shape=shapes,
-        scratch_shapes=[
-            pltpu.VMEM((n, BOX, BOX), F32),
+        scratch_shapes=scratch + [
             pltpu.VMEM((S, n * S), F32),
             pltpu.VMEM((n, BOX, BOX), BF16),
             [table_scratch() for _ in cells],
             pltpu.SemaphoreType.DMA((n, 2)),
+            pltpu.SemaphoreType.DMA((len(later),)),
         ],
         compiler_params=PARAMS,
         cost_estimate=cost(n, 5),
         name="aligned",
-    )(shifts, widths, source, boxes, *base)
+    )(shifts, widths, source, boxes, later_boxes, *base)
 
 
 def place(plan_ref, top, left, canvas_ref, first):
@@ -191,24 +209,24 @@
             before = now
 
 
-def shifted_kernel(cells, origin, carried, finals, kept, shifts, widths, boxes, base_ref, *refs):
+def shifted_kernel(cells, later, origin, carried, finals, kept, quads, count, shifts, widths,
+                   box_ref, base_ref, *refs):
     n = len(cells)
-    quads, refs = refs[: 8 * n], refs[8 * n :]
+    arrays, refs = refs[:count], refs[count:]
     upper_ref = None
     if carried:
         carry_ref, refs = refs[0], refs[1:]
         if kept:
             upper_ref, refs = refs[0], refs[1:]
+    if later:
+        later_boxes, refs = refs[0], refs[1:]
     outs, refs = refs[:4], refs[4:]
     if kept:
         keep_ref, refs = refs[0], refs[1:]
-    box_ref, mass_ref, ub_ref, vb_ref, v_ref, canvas_ref, tables, sems, out_sems = refs
-    copies = [
-        pltpu.make_async_copy(boxes.at[0, j], box_ref.at[i], sems.at[i])
-        for i, j in enumerate(cells)
-    ]
-    for copy in copies:
-        copy.start()
+    if later:
+        later_ref, refs = refs[0], refs[1:]
+    mass_ref, ub_ref, vb_ref, v_ref, canvas_ref, tables, sems, out_sems = refs
+    later_copies = fetch(later_boxes, later, later_ref, sems) if later else []
     canvas_ref[...] = jnp.zeros_like(canvas_ref)
     if carried:
         first, last = carried[0] - origin, carried[1] - origin
@@ -219,15 +237,17 @@
         for k in range(4):
             rows = slice(k // 2 * HALF, (k // 2 + 1) * HALF)
             cols = slice(k % 2 * HALF, (k % 2 + 1) * HALF)
-            ub_ref[i, rows, cols] = quads[8 * i + k][...].astype(BF16)
-            mass_ref[i, rows, cols] = quads[8 * i + 4 + k][...]
+            for ref, (array, down, across) in (
+                (ub_ref, quads[i][k]), (mass_ref, quads[i][4 + k])
+            ):
+                part = arrays[array][
+                    down * HALF : (down + 1) * HALF, across * HALF : (across + 1) * HALF]
+                ref[i, rows, cols] = part.astype(ref.dtype)
     u = [ub_ref[i] for i in range(n)]
     for step in range(ITERS):
         for i in range(n):
             inner = dot(tables[i][0][...], u[i]).astype(BF16)
             den = dot(inner, tables[i][1][...])
-            if step == 0:
-                copies[i].wait()
             v = box_ref[i] / den
             if step == ITERS - 1:
                 v_ref[i] = v
@@ -263,49 +283,56 @@
             out_sems.at[len(writes)]))
     for copy in writes:
         copy.start()
-    for copy in writes:
+    for copy in writes + later_copies:
         copy.wait()
 
 
-def shifted(cells, boxes, shifts, widths, base, quads, carried=None, carry=None, finals=(), kept=None):
+def shifted(cells, later, boxes, later_boxes, shifts, widths, base, quads, carried=None,
+            carry=(), finals=(), kept=None):
     n = len(cells)
     origin = min(j * S for j in cells)
     width = max(j * S + REACH for j in cells) - origin
     total = sum(last - first for first, last in finals)
     shapes = [jax.ShapeDtypeStruct((rows, total), F32) for rows in (OWN, NEXT, FAR, RADIUS)]
     if kept:
+        if carried:
+            shapes[3] = jax.ShapeDtypeStruct((RADIUS, total + carry[1].shape[1]), F32)
         shapes.append(jax.ShapeDtypeStruct((REACH, kept[1] - kept[0]), F32))
-    blocks, arrays = [], []
+    outs = [ANY] * len(shapes)
+    if later:
+        shapes.append(jax.ShapeDtypeStruct((len(later), BOX, BOX), F32))
+        outs.append(VMEM)
+    arrays, where = [], []
     for j in cells:
-        for array, at in quads[j]:
-            arrays.append(array)
-            blocks.append(pl.BlockSpec((HALF, HALF), lambda g, at=at: at))
-    if carried:
-        arrays += carry
-        blocks += [VMEM] * len(carry)
-        if kept:
-            shapes[3] = jax.ShapeDtypeStruct((RADIUS, total + carry[1].shape[1]), F32)
+        where.append([])
+        for array, (down, across) in quads[j]:
+            known = [k for k, other in enumerate(arrays) if other is array]
+            if not known:
+                known = [len(arrays)]
+                arrays.append(array)
+            where[-1].append((known[0], down, across))
+    count = len(arrays)
+    arrays += carry
     return pl.pallas_call(
-        functools.partial(shifted_kernel, cells, origin, carried, finals, kept),
-        grid=(1,),
-        in_specs=[SMEM, SMEM, HBM, VMEM] + blocks,
-        out_specs=[ANY] * len(shapes),
+        functools.partial(
+            shifted_kernel, cells, later, origin, carried, finals, kept, where, count),
+        in_specs=[SMEM, SMEM, VMEM, VMEM] + [VMEM] * len(arrays) + [HBM] * bool(later),
+        out_specs=outs,
         out_shape=shapes,
         scratch_shapes=[
-            pltpu.VMEM((n, BOX, BOX), F32),
             pltpu.VMEM((n, S, S), F32),
             pltpu.VMEM((n, S, S), BF16),
             pltpu.VMEM((n, BOX, BOX), BF16),
             pltpu.VMEM((n, BOX, BOX), F32),
             pltpu.VMEM((REACH + 8, width), F32),
             [table_scratch() for _ in cells],
-            pltpu.SemaphoreType.DMA((n,)),
+            pltpu.SemaphoreType.DMA((max(1, len(later)),)),
             pltpu.SemaphoreType.DMA((4 * len(finals) + 2,)),
         ],
         compiler_params=PARAMS,
         cost_estimate=cost(n, 7),
         name="shifted",
-    )(shifts, widths, boxes, base, *arrays)
+    )(shifts, widths, boxes, base, *arrays, *([later_boxes] if later else []))
 
 
 def blur_weights():
@@ -330,10 +357,8 @@
 
 
 def edges_kernel(*refs):
-    (own3, next3, far3, own2, next2, far2, back2, next1, joined, main_ref, right_ref, east_ref,
-     west_ref, sum_ref, win_ref) = refs
-    sum_ref[:FAR] = next1[:FAR] + joined[...]
-    sum_ref[FAR:] = next1[FAR:]
+    (own3, next3, far3, own2, next2, far2, back2, main_ref, right_ref, east_ref, west_ref,
+     win_ref) = refs
 
     def outer(c, out):
         east_ref[:S, HALF + c : 2 * HALF + c] = out
@@ -357,14 +382,13 @@
 def edges(*arrays):
     return pl.pallas_call(
         edges_kernel,
-        in_specs=[VMEM] * 9,
-        out_specs=[VMEM] * 5,
+        in_specs=[VMEM] * 7,
+        out_specs=[VMEM] * 4,
         out_shape=[
             jax.ShapeDtypeStruct((S, 3 * HALF), F32),
             jax.ShapeDtypeStruct((S, HALF), F32),
             jax.ShapeDtypeStruct((S + RADIUS, 3 * HALF), F32),
             jax.ShapeDtypeStruct((RADIUS, S), F32),
-            jax.ShapeDtypeStruct((NEXT, REACH), F32),
         ],
         scratch_shapes=[pltpu.VMEM((NEXT, 2 * S), F32)],
         compiler_params=PARAMS,
@@ -449,13 +473,15 @@
     boxes_a = pltpu.with_memory_space_constraint(boxes_a, pltpu.HBM)
     boxes_b = pltpu.with_memory_space_constraint(boxes_b, pltpu.HBM)
     masses = pltpu.with_memory_space_constraint(source, pltpu.HBM)
-    top03, bot03, left_top, left_bot, base = aligned(
-        (0, 3), masses, boxes_a, shifts_a, widths_a)
+    shifts_a = pltpu.with_memory_space_constraint(shifts_a, pltpu.HBM)
+    widths_a = pltpu.with_memory_space_constraint(widths_a, pltpu.HBM)
+    top03, bot03, left_top, left_bot, base, boxes12 = aligned(
+        (0, 3), (1, 2), masses, boxes_a, boxes_a, shifts_a, widths_a)
     rtop03 = moved(top03, -1, 0)
     east = moved(left_bot, 0, -1)
     diag = moved(left_top, -1, -1)
-    top12, bot12 = aligned(
-        (1, 2), masses, boxes_a, shifts_a, widths_a, behind(base, bot03))
+    top12, bot12, boxes3 = aligned(
+        (1, 2), (3,), masses, boxes12, boxes_b, shifts_a, widths_a, base)
     rtop12 = moved(top12, -1, 0)
     own = [(bot03, 0), (bot03, 1), (bot12, 0), (bot12, 1), (bot12, 2), (bot12, 3), (bot03, 2),
            (bot03, 3), (east, 0)]
@@ -470,20 +496,20 @@
             (source, (1, b)) if j < 3 else (east, (1, 0)),
         ]
         quads[j] += [(array, (1, at)) for array, at in (below[a], below[b])]
-    own3, next3, far3, back3, carry = shifted(
-        (3,), boxes_b, shifts_b, widths_b, behind(base, bot12), quads,
+    own3, next3, far3, back3, carry, boxes02 = shifted(
+        (3,), (0, 2), boxes3, boxes_b, shifts_b, widths_b, base, quads,
         finals=((1152, 1408),), kept=(768, 1152))
     next3 = moved(next3, 1, 0)
     far3 = moved(far3, 2, 0)
-    own2, next2, far2, back2, carry = shifted(
-        (0, 2), boxes_b, shifts_b, widths_b, base, quads,
+    own2, next2, far2, back2, carry, boxes1 = shifted(
+        (0, 2), (1,), boxes02, boxes_b, shifts_b, widths_b, base, quads,
         carried=(768, 1152), carry=(carry, back3), finals=((0, 256), (896, 1152)),
         kept=(256, 896))
     next2 = moved(next2, 1, 0)
     far2 = moved(far2, 2, 0)
     rback2 = moved(back2, -1, 0)
     own1, next1, far1, back1 = shifted(
-        (1,), boxes_b, shifts_b, widths_b, base, quads,
+        (1,), (), boxes1, None, shifts_b, widths_b, base, quads,
         carried=(256, 896), carry=(behind(carry, next3, far3),),
         finals=((256, 896),))
     n_row = lax.axis_size("row")
@@ -491,9 +517,8 @@
         behind(far1, far2, rback2), "row", [(i, i + 1) for i in range(0, n_row, 2)])
     far1 = lax.ppermute(far1, "row", [(i, (i + 2) % n_row) for i in range(1, n_row, 2)])
     back1 = moved(back1, -1, 0)
-    main, right, east, west, next1 = edges(
-        own3, next3, far3, own2, next2, far2, rback2, next1, joined)
-    next1 = moved(next1, 1, 0)
+    next1 = moved(next1.at[:FAR].add(behind(joined, next2)), 1, 0)
+    main, right, east, west = edges(own3, next3, far3, own2, next2, far2, rback2)
     return final(
         source.shape[1], own1, next1, far1, back1, main, right, moved(east, 0, 1),
         moved(west, 0, -1))

time: 85.6 us -> 83.7 us (0.978)
  Pallas kernels: 32.8 us -> 30.9 us
  local copies, waits for them, and re-layouts: 1.38 us -> 0.02 us
  waiting for transfers between devices: 26.3 us -> 27.5 us
    pallas_call x6, Pallas kernels: 30 us -> 28.1 us  [the longest x3 15.3 us: shifted(): pl.pallas_call(functools.partial(shifted_kernel, cells, later, origin, ca...]
    unnamed x14 -> x10, local copies, waits for them, and re-layouts: 1.38 us -> 0.02 us
    ppermute x9, waiting for transfers between devices: 20.8 us -> 21.9 us  [moved(): lax.ppermute(array, 'row', [(i, (i + by_row) % n_row) for i in range(n_ro...]
where the time goes in v2:
time: 83.7 us; the launch traced here: 83.4 us
  Pallas kernels  30.9 us (37%)
  waiting for transfers between devices  27.5 us (33%)
  starting transfers between devices  24.7 us (30%)
    ppermute x9, waiting for transfers between devices, moved(): lax.ppermute(array, 'row', [(i, (i + by_row) % n_row) for i in range(n_ro...  21.9 us
    pallas_call x3, Pallas kernels, shifted(): pl.pallas_call(functools.partial(shifted_kernel, cells, later, origin, ca...  15.3 us
    pallas_call x2, Pallas kernels, aligned(): pl.pallas_call(functools.partial(aligned_kernel, cells, later), in_specs=...  11.3 us
    ppermute x3, starting transfers between devices, moved(): lax.ppermute(array, 'col', [(i, (i + by_col) % n_col) for i in range(n_co...  11.3 us
    ppermute x9, starting transfers between devices, moved(): lax.ppermute(array, 'row', [(i, (i + by_row) % n_row) for i in range(n_ro...  8.86 us
    ppermute x1, waiting for transfers between devices, on_device(): lax.ppermute(behind(far1, far2, rback2), 'row', [(i, i + 1) for i in rang...  5.6 us
    pallas_call x1, Pallas kernels, final(): pl.pallas_call(final_kernel, in_specs=[VMEM] * 10, out_specs=VMEM, out_sh...  2.78 us
    ppermute x1, starting transfers between devices, on_device(): lax.ppermute(far1, 'row', [(i, (i + 2) % n_row) for i in range(1, n_row,...  1.91 us
  transfers between devices with their start and end apart: 15, of which 5 were waited for; matrix products, arithmetic and copies ran while one was open for 0% of the time, Pallas kernels for 27%

profile of v2, /device:TPU:1, one launch (start us, length us, event | category | flops | bytes accessed | tf_op | source)
XLA Modules:
  0.0 83.4 jit_solution(17299451055590438401)
XLA Ops:
  0.0 5.9 %aligned.2 = (f32[256,512]{1,0:T(8,128)S(1)}, f32[128,512]{1,0:T(8,128)S(1)}, f32[256,128]{1,0:T(8,128)S(1)}, f32[256,128]{1,0:T(8,128)S(1)}, f32[904,128]{1,0:T(8,128)S(1)}, /*index=5*/f32[2,512,512]{2,1,0:T(8,128)S(1)}) custom-call(s32[1,2,4]{2,1,0:T(2,128)} %bitcast.10, s32[1,2,4]{2,1,0:T(2,128)} %bitcast.12, f32[256,1024]{1,0:T(8,128)} %refs_2_.1, ...), custom_call_target="tpu_custom_call" | custom-call | flops 8040000000 | bytes 2097152 | tf_op jit(solution)/shard_map/aligned/pallas_call | solution.py:171
  5.9 6.0 %collective-permute-start = (f32[256,128]{1,0:T(8,128)S(1)}, f32[256,128]{1,0:T(8,128)S(1)}, u32[]{:S(2)}, u32[]{:S(2)}) collective-permute-start(f32[256,128]{1,0:T(8,128)S(1)} %get-tuple-element.53), channel_id=1, source_target_pairs={{0,7},{1,0},{2,1},{3,2},{4,3},{5,4},{6,5},{7,6},{8,15},{9,8},{10,9... | collective-permute-start | bytes 393224 | tf_op jit(solution)/shard_map/ppermute | solution.py:452
  11.9 1.4 %collective-permute-start.2 = (f32[256,128]{1,0:T(8,128)S(1)}, f32[256,128]{1,0:T(8,128)S(1)}, u32[]{:S(2)}, u32[]{:S(2)}) collective-permute-start(f32[256,128]{1,0:T(8,128)S(1)} %get-tuple-element.55), channel_id=1, source_target_pairs={{0,255},{1,248},{2,249},{3,250},{4,251},{5,252},{6,253},{7,254},{8... | collective-permute-start | bytes 393224 | tf_op jit(solution)/shard_map/ppermute | solution.py:458
  13.3 4.7 %collective-permute-start.1 = (f32[256,512]{1,0:T(8,128)S(1)}, f32[256,512]{1,0:T(8,128)S(1)}, u32[]{:S(2)}, u32[]{:S(2)}) collective-permute-start(f32[256,512]{1,0:T(8,128)S(1)} %get-tuple-element.54), channel_id=1, source_target_pairs={{0,248},{8,0},{16,8},{24,16},{32,24},{40,32},{48,40},{56,48},{64,5... | collective-permute-start | bytes 1572872 | tf_op jit(solution)/shard_map/ppermute | solution.py:450
  18.0 0.0 copy-start.2
  18.0 0.0 copy-start.3
  18.0 0.0 copy-start.4
  18.0 5.4 %aligned.3 = (f32[256,512]{1,0:T(8,128)S(1)}, f32[128,512]{1,0:T(8,128)S(1)}, f32[1,512,512]{2,1,0:T(8,128)S(1)}) custom-call(s32[1,2,4]{2,1,0:T(2,128)} %bitcast.11, s32[1,2,4]{2,1,0:T(2,128)} %bitcast.13, f32[256,1024]{1,0:T(8,128)} %refs_2_.1, f32[2,512,512]{2,1,0:T(8,128)S(1)} %get-tuple-element.49.boxes, f32[1,4,512,512]{3,2,1,0:T(8,128)} %refs_7_.1, ...), custom_call_target="tpu_custom_call" | custom-call | flops 8040000000 | bytes 2097152 | tf_op jit(solution)/shard_map/aligned/pallas_call | solution.py:171
  23.4 1.7 %collective-permute-start.3 = (f32[256,512]{1,0:T(8,128)S(1)}, f32[256,512]{1,0:T(8,128)S(1)}, u32[]{:S(2)}, u32[]{:S(2)}) collective-permute-start(f32[256,512]{1,0:T(8,128)S(1)} %get-tuple-element.58), channel_id=1, source_target_pairs={{0,248},{8,0},{16,8},{24,16},{32,24},{40,32},{48,40},{56,48},{64,5... | collective-permute-start | bytes 1572872 | tf_op jit(solution)/shard_map/ppermute | solution.py:450
  25.1 0.0 collective-permute-done.refs_1_
  25.1 0.0 collective-permute-done.2.refs_3_
  25.1 0.0 collective-permute-done.1.refs_2_
  25.1 0.0 copy-done.2
  25.1 0.0 copy-done.3
  25.1 0.0 copy-done.4
  25.1 4.8 %shifted.3 = (f32[264,256]{1,0:T(8,128)S(1)}, f32[272,256]{1,0:T(8,128)S(1)}, f32[136,256]{1,0:T(8,128)S(1)}, f32[8,256]{1,0:T(8,128)S(1)}, f32[640,384]{1,0:T(8,128)S(1)}, /*index=5*/f32[2,512,512]{2,1,0:T(8,128)S(1)}) custom-call(s32[1,2,4]{2,1,0:T(2,128)S(1)} %bitcast.4, s32[1,2,4]{2,1,0:T(2,128)S(1)} %bitcast.7, ...), custom_call_target="tpu_custom_call" | custom-call | flops 5628000256 | bytes 1048576 | tf_op jit(solution)/shard_map/shifted/pallas_call | solution.py:316
  29.9 0.1 collective-permute-start.5
  30.0 0.4 collective-permute-start.4
  30.4 1.8 %collective-permute-done.3.refs_3_.refs_1_ = f32[256,512]{1,0:T(8,128)S(1)} collective-permute-done((f32[256,512]{1,0:T(8,128)S(1)}, f32[256,512]{1,0:T(8,128)S(1)}, u32[]{:S(2)}, u32[]{:S(2)}) %collective-permute-start.3) | collective-permute-done | bytes 524320 | tf_op jit(solution)/shard_map/ppermute | solution.py:450
  32.3 6.1 %shifted.4 = (f32[264,512]{1,0:T(8,128)S(1)}, f32[272,512]{1,0:T(8,128)S(1)}, f32[136,512]{1,0:T(8,128)S(1)}, f32[8,768]{1,0:T(8,128)S(1)}, f32[640,640]{1,0:T(8,128)S(1)}, /*index=5*/f32[1,512,512]{2,1,0:T(8,128)S(1)}) custom-call(s32[1,2,4]{2,1,0:T(2,128)S(1)} %bitcast.5, s32[1,2,4]{2,1,0:T(2,128)S(1)} %bitcast.8, ...), custom_call_target="tpu_custom_call" | custom-call | flops 11256000512 | bytes 2097152 | tf_op jit(solution)/shard_map/shifted/pallas_call | solution.py:316
  38.4 0.3 collective-permute-start.7
  38.8 0.0 collective-permute-start.6
  38.8 1.5 %collective-permute-start.9 = (f32[272,512]{1,0:T(8,128)S(1)}, f32[272,512]{1,0:T(8,128)S(1)}, u32[]{:S(2)}, u32[]{:S(2)}) collective-permute-start(f32[272,512]{1,0:T(8,128)S(1)} %get-tuple-element.72), channel_id=1, source_target_pairs={{0,8},{8,16},{16,24},{24,32},{32,40},{40,48},{48,56},{56,64},{64,7... | collective-permute-start | bytes 1671176 | tf_op jit(solution)/shard_map/ppermute | solution.py:450
  40.3 0.0 collective-permute-done.5.refs_2_
  40.3 0.0 collective-permute-done.4.refs_1_
  40.3 4.4 %shifted.5 = (f32[264,640]{1,0:T(8,128)S(1)}, f32[272,640]{1,0:T(8,128)S(1)}, f32[136,640]{1,0:T(8,128)S(1)}, f32[8,640]{1,0:T(8,128)S(1)}) custom-call(s32[1,2,4]{2,1,0:T(2,128)S(1)} %bitcast.6, s32[1,2,4]{2,1,0:T(2,128)S(1)} %bitcast.9, f32[1,512,512]{2,1,0:T(8,128)S(1)} %get-tuple-element.61.box_ref, f32[904,128]{1,0:T(8,128)S(1)} %get-tuple-element.50.refs_0_.base_ref, ...), custom_call_target="tpu_custom_call" | custom-call | flops 5628000256 | bytes 1048576 | tf_op jit(solution)/shard_map/shifted/pallas_call | solution.py:316
  44.7 0.0 copy-start
  44.7 0.0 copy-start.1
  44.7 0.0 collective-permute-done.7.refs_6_
  44.7 1.7 %collective-permute-done.6.refs_5_ = f32[136,512]{1,0:T(8,128)S(1)} collective-permute-done((f32[136,512]{1,0:T(8,128)S(1)}, f32[136,512]{1,0:T(8,128)S(1)}, u32[]{:S(2)}, u32[]{:S(2)}) %collective-permute-start.6) | collective-permute-done | bytes 278560 | tf_op jit(solution)/shard_map/ppermute | solution.py:450
  46.5 1.3 %collective-permute-start.8 = (f32[136,640]{1,0:T(8,128)S(1)}, f32[136,640]{1,0:T(8,128)S(1)}, u32[]{:S(2)}, u32[]{:S(2)}) collective-permute-start(f32[136,640]{1,0:T(8,128)S(1)} %get-tuple-element.71), channel_id=1, source_target_pairs={{0,8},{16,24},{32,40},{48,56},{64,72},{80,88},{96,104},{112,120},{... | collective-permute-start | bytes 1044488 | tf_op jit(solution)/shard_map/ppermute | solution.py:516
  47.8 3.5 %collective-permute-done.9.refs_4_ = f32[272,512]{1,0:T(8,128)S(1)} collective-permute-done((f32[272,512]{1,0:T(8,128)S(1)}, f32[272,512]{1,0:T(8,128)S(1)}, u32[]{:S(2)}, u32[]{:S(2)}) %collective-permute-start.9) | collective-permute-done | bytes 557088 | tf_op jit(solution)/shard_map/ppermute | solution.py:450
  51.2 5.6 %collective-permute-done.8 = f32[136,640]{1,0:T(8,128)S(1)} collective-permute-done((f32[136,640]{1,0:T(8,128)S(1)}, f32[136,640]{1,0:T(8,128)S(1)}, u32[]{:S(2)}, u32[]{:S(2)}) %collective-permute-start.8) | collective-permute-done | bytes 348192 | tf_op jit(solution)/shard_map/ppermute | solution.py:516
  56.8 0.1 add_dynamic-update-slice_fusion
  56.9 0.1 collective-permute-start.10
  57.0 1.5 %edges.1 = (f32[256,384]{1,0:T(8,128)S(1)}, f32[256,128]{1,0:T(8,128)S(1)}, f32[264,384]{1,0:T(8,128)S(1)}, f32[8,256]{1,0:T(8,128)S(1)}) custom-call(f32[264,256]{1,0:T(8,128)S(1)} %get-tuple-element.75.refs_0_, f32[272,256]{1,0:T(8,128)S(1)} %collective-permute-done.4.refs_1_, f32[136,256]{1,0:T(8,128)S(1)} %collective-permute-done.5.refs_2_, ...), custom_call_target="tpu_custom_call" | custom-call | tf_op jit(solution)/shard_map/edges/pallas_call | solution.py:383
  58.5 0.6 collective-permute-start.13
  59.1 1.9 %collective-permute-start.11 = (f32[136,640]{1,0:T(8,128)S(1)}, f32[136,640]{1,0:T(8,128)S(1)}, u32[]{:S(2)}, u32[]{:S(2)}) collective-permute-start(f32[136,640]{1,0:T(8,128)S(1)} %get-tuple-element.71), channel_id=1, source_target_pairs={{8,24},{24,40},{40,56},{56,72},{72,88},{88,104},{104,120},{120,136... | collective-permute-start | bytes 1044488 | tf_op jit(solution)/shard_map/ppermute | solution.py:518
  61.1 0.1 collective-permute-start.12
  61.1 4.6 %collective-permute-start.14 = (f32[8,256]{1,0:T(8,128)S(1)}, f32[8,256]{1,0:T(8,128)S(1)}, u32[]{:S(2)}, u32[]{:S(2)}) collective-permute-start(f32[8,256]{1,0:T(8,128)S(1)} %get-tuple-element.80), channel_id=1, source_target_pairs={{0,7},{1,0},{2,1},{3,2},{4,3},{5,4},{6,5},{7,6},{8,15},{9,8},{10,9... | collective-permute-start | bytes 24584 | tf_op jit(solution)/shard_map/ppermute | solution.py:452
  65.7 14.8 %collective-permute-done.12.back1 = f32[8,640]{1,0:T(8,128)S(1)} collective-permute-done((f32[8,640]{1,0:T(8,128)S(1)}, f32[8,640]{1,0:T(8,128)S(1)}, u32[]{:S(2)}, u32[]{:S(2)}) %collective-permute-start.12) | collective-permute-done | bytes 20512 | tf_op jit(solution)/shard_map/ppermute | solution.py:450
  80.6 0.0 collective-permute-done.14.west_ref
  80.6 0.0 collective-permute-done.11.far1
  80.6 0.0 collective-permute-done.13.east_ref
  80.6 0.0 collective-permute-done.10.next1
  80.6 0.0 copy-done
  80.6 0.0 copy-done.1
  80.6 2.8 %final.1 = f32[256,1024]{1,0:T(8,128)} custom-call(f32[264,640]{1,0:T(8,128)S(1)} %get-tuple-element.66.own1, f32[272,640]{1,0:T(8,128)S(1)} %collective-permute-done.10.next1, f32[136,640]{1,0:T(8,128)S(1)} %collective-permute-done.11.far1, f32[8,640]{1,0:T(8,128)S(1)} %collective-permute-done.12.back1, f32[256,384]{1,0:T(8,128)S(1)} %get-tuple-element.77.main_ref, ...), custom_call_target="tpu_custom_call" | custom-call | tf_op jit(solution)/shard_map/final/pallas_call | solution.py:433
Async XLA Ops:
  5.9 19.2 %collective-permute-start = (f32[256,128]{1,0:T(8,128)S(1)}, f32[256,128]{1,0:T(8,128)S(1)}, u32[]{:S(2)}, u32[]{:S(2)}) collective-permute-start(f32[256,128]{1,0:T(8,128)S(1)} %get-tuple-element.53), channel_id=1, source_target_pairs={{0,7},{1,0},{2,1},{3,2},{4,3},{5,4},{6,5},{7,6},{8,15},{9,8},{10,9... | collective-permute-start | bytes 393224 | tf_op jit(solution)/shard_map/ppermute | solution.py:452
  11.9 13.2 %collective-permute-start.2 = (f32[256,128]{1,0:T(8,128)S(1)}, f32[256,128]{1,0:T(8,128)S(1)}, u32[]{:S(2)}, u32[]{:S(2)}) collective-permute-start(f32[256,128]{1,0:T(8,128)S(1)} %get-tuple-element.55), channel_id=1, source_target_pairs={{0,255},{1,248},{2,249},{3,250},{4,251},{5,252},{6,253},{7,254},{8... | collective-permute-start | bytes 393224 | tf_op jit(solution)/shard_map/ppermute | solution.py:458
  13.3 11.8 %collective-permute-start.1 = (f32[256,512]{1,0:T(8,128)S(1)}, f32[256,512]{1,0:T(8,128)S(1)}, u32[]{:S(2)}, u32[]{:S(2)}) collective-permute-start(f32[256,512]{1,0:T(8,128)S(1)} %get-tuple-element.54), channel_id=1, source_target_pairs={{0,248},{8,0},{16,8},{24,16},{32,24},{40,32},{48,40},{56,48},{64,5... | collective-permute-start | bytes 1572872 | tf_op jit(solution)/shard_map/ppermute | solution.py:450
  18.0 7.1 %copy-start.2 = (f32[256,1024]{1,0:T(8,128)S(1)}, f32[256,1024]{1,0:T(8,128)}, u32[]{:S(2)}) copy-start(f32[256,1024]{1,0:T(8,128)} %refs_2_.1) | copy-start | bytes 3145732
  18.0 7.1 %copy-start.3 = (s32[1,4,2]{1,2,0:T(2,128)S(1)}, s32[1,4,2]{1,2,0:T(2,128)}, u32[]{:S(2)}) copy-start(s32[1,4,2]{1,2,0:T(2,128)} %param.16) | copy-start | bytes 100
  18.0 7.2 %copy-start.4 = (s32[1,4,2]{1,2,0:T(2,128)S(1)}, s32[1,4,2]{1,2,0:T(2,128)}, u32[]{:S(2)}) copy-start(s32[1,4,2]{1,2,0:T(2,128)} %param.17) | copy-start | bytes 100
  23.4 8.9 %collective-permute-start.3 = (f32[256,512]{1,0:T(8,128)S(1)}, f32[256,512]{1,0:T(8,128)S(1)}, u32[]{:S(2)}, u32[]{:S(2)}) collective-permute-start(f32[256,512]{1,0:T(8,128)S(1)} %get-tuple-element.58), channel_id=1, source_target_pairs={{0,248},{8,0},{16,8},{24,16},{32,24},{40,32},{48,40},{56,48},{64,5... | collective-permute-start | bytes 1572872 | tf_op jit(solution)/shard_map/ppermute | solution.py:450
  29.9 10.4 %collective-permute-start.5 = (f32[136,256]{1,0:T(8,128)S(1)}, f32[136,256]{1,0:T(8,128)S(1)}, u32[]{:S(2)}, u32[]{:S(2)}) collective-permute-start(f32[136,256]{1,0:T(8,128)S(1)} %get-tuple-element.64), channel_id=1, source_target_pairs={{0,16},{8,24},{16,32},{24,40},{32,48},{40,56},{48,64},{56,72},{64,... | collective-permute-start | bytes 417800 | tf_op jit(solution)/shard_map/ppermute | solution.py:450
  30.0 10.3 %collective-permute-start.4 = (f32[272,256]{1,0:T(8,128)S(1)}, f32[272,256]{1,0:T(8,128)S(1)}, u32[]{:S(2)}, u32[]{:S(2)}) collective-permute-start(f32[272,256]{1,0:T(8,128)S(1)} %get-tuple-element.63), channel_id=1, source_target_pairs={{0,8},{8,16},{16,24},{24,32},{32,40},{40,48},{48,56},{56,64},{64,7... | collective-permute-start | bytes 835592 | tf_op jit(solution)/shard_map/ppermute | solution.py:450
  38.4 6.3 %collective-permute-start.7 = (f32[8,768]{1,0:T(8,128)S(1)}, f32[8,768]{1,0:T(8,128)S(1)}, u32[]{:S(2)}, u32[]{:S(2)}) collective-permute-start(f32[8,768]{1,0:T(8,128)S(1)} %get-tuple-element.70), channel_id=1, source_target_pairs={{0,248},{8,0},{16,8},{24,16},{32,24},{40,32},{48,40},{56,48},{64,5... | collective-permute-start | bytes 73736 | tf_op jit(solution)/shard_map/ppermute | solution.py:450
  38.8 7.7 %collective-permute-start.6 = (f32[136,512]{1,0:T(8,128)S(1)}, f32[136,512]{1,0:T(8,128)S(1)}, u32[]{:S(2)}, u32[]{:S(2)}) collective-permute-start(f32[136,512]{1,0:T(8,128)S(1)} %get-tuple-element.69), channel_id=1, source_target_pairs={{0,16},{8,24},{16,32},{24,40},{32,48},{40,56},{48,64},{56,72},{64,... | collective-permute-start | bytes 835592 | tf_op jit(solution)/shard_map/ppermute | solution.py:450
  38.8 12.4 %collective-permute-start.9 = (f32[272,512]{1,0:T(8,128)S(1)}, f32[272,512]{1,0:T(8,128)S(1)}, u32[]{:S(2)}, u32[]{:S(2)}) collective-permute-start(f32[272,512]{1,0:T(8,128)S(1)} %get-tuple-element.72), channel_id=1, source_target_pairs={{0,8},{8,16},{16,24},{24,32},{32,40},{40,48},{48,56},{56,64},{64,7... | collective-permute-start | bytes 1671176 | tf_op jit(solution)/shard_map/ppermute | solution.py:450
  44.7 35.9 %copy-start = (bf16[512,256]{1,0:T(8,128)(2,1)S(1)}, bf16[512,256]{1,0:T(8,128)(2,1)}, u32[]{:S(2)}) copy-start(bf16[512,256]{1,0:T(8,128)(2,1)} %constant.33.clone.low_ref) | copy-start | bytes 786436
  44.7 35.9 %copy-start.1 = (bf16[512,256]{1,0:T(8,128)(2,1)S(1)}, bf16[512,256]{1,0:T(8,128)(2,1)}, u32[]{:S(2)}) copy-start(bf16[512,256]{1,0:T(8,128)(2,1)} %constant.32.clone.high_ref) | copy-start | bytes 786436
  46.5 10.4 %collective-permute-start.8 = (f32[136,640]{1,0:T(8,128)S(1)}, f32[136,640]{1,0:T(8,128)S(1)}, u32[]{:S(2)}, u32[]{:S(2)}) collective-permute-start(f32[136,640]{1,0:T(8,128)S(1)} %get-tuple-element.71), channel_id=1, source_target_pairs={{0,8},{16,24},{32,40},{48,56},{64,72},{80,88},{96,104},{112,120},{... | collective-permute-start | bytes 1044488 | tf_op jit(solution)/shard_map/ppermute | solution.py:516
  56.9 23.7 %collective-permute-start.10 = (f32[272,640]{1,0:T(8,128)S(1)}, f32[272,640]{1,0:T(8,128)S(1)}, u32[]{:S(2)}, u32[]{:S(2)}) collective-permute-start(f32[272,640]{1,0:T(8,128)S(1)} %add_dynamic-update-slice_fusion), channel_id=1, source_target_pairs={{0,8},{8,16},{16,24},{24,32},{32,40},{40,48},{48,56},{56,64},{64,7... | collective-permute-start | bytes 2088968 | tf_op jit(solution)/shard_map/ppermute | solution.py:450
  58.5 22.1 %collective-permute-start.13 = (f32[264,384]{1,0:T(8,128)S(1)}, f32[264,384]{1,0:T(8,128)S(1)}, u32[]{:S(2)}, u32[]{:S(2)}) collective-permute-start(f32[264,384]{1,0:T(8,128)S(1)} %get-tuple-element.79), channel_id=1, source_target_pairs={{0,1},{1,2},{2,3},{3,4},{4,5},{5,6},{6,7},{7,0},{8,9},{9,10},{10,1... | collective-permute-start | bytes 1216520 | tf_op jit(solution)/shard_map/ppermute | solution.py:452
  59.1 21.4 %collective-permute-start.11 = (f32[136,640]{1,0:T(8,128)S(1)}, f32[136,640]{1,0:T(8,128)S(1)}, u32[]{:S(2)}, u32[]{:S(2)}) collective-permute-start(f32[136,640]{1,0:T(8,128)S(1)} %get-tuple-element.71), channel_id=1, source_target_pairs={{8,24},{24,40},{40,56},{56,72},{72,88},{88,104},{104,120},{120,136... | collective-permute-start | bytes 1044488 | tf_op jit(solution)/shard_map/ppermute | solution.py:518
  61.1 19.5 %collective-permute-start.12 = (f32[8,640]{1,0:T(8,128)S(1)}, f32[8,640]{1,0:T(8,128)S(1)}, u32[]{:S(2)}, u32[]{:S(2)}) collective-permute-start(f32[8,640]{1,0:T(8,128)S(1)} %get-tuple-element.74), channel_id=1, source_target_pairs={{0,248},{8,0},{16,8},{24,16},{32,24},{40,32},{48,40},{56,48},{64,5... | collective-permute-start | bytes 61448 | tf_op jit(solution)/shard_map/ppermute | solution.py:450
  61.1 19.4 %collective-permute-start.14 = (f32[8,256]{1,0:T(8,128)S(1)}, f32[8,256]{1,0:T(8,128)S(1)}, u32[]{:S(2)}, u32[]{:S(2)}) collective-permute-start(f32[8,256]{1,0:T(8,128)S(1)} %get-tuple-element.80), channel_id=1, source_target_pairs={{0,7},{1,0},{2,1},{3,2},{4,3},{5,4},{6,5},{7,6},{8,15},{9,8},{10,9... | collective-permute-start | bytes 24584 | tf_op jit(solution)/shard_map/ppermute | solution.py:452

commit v3 on v2

--- a/solution.py
+++ b/solution.py
@@ -103,15 +103,18 @@
     else:
         base_ref, outs, later_ref, refs = refs[0], refs[1:3], refs[3], refs[4:]
         box_ref = boxes
-    mass_ref, vb_ref, tables, sems, later_sems = refs
-    copies = []
-    for i, j in enumerate(cells):
-        copies.append([
-            pltpu.make_async_copy(
-                source.at[:, pl.ds(j * S, S)], mass_ref.at[:, pl.ds(i * S, S)], sems.at[i, 1]),
-        ])
-        if 0 in cells:
-            copies[i].append(pltpu.make_async_copy(boxes.at[0, j], box_ref.at[i], sems.at[i, 0]))
+    copies = [[] for _ in cells]
+    if 0 in cells:
+        mass_ref, vb_ref, tables, sems, later_sems = refs
+        masses = [mass_ref.at[:, pl.ds(i * S, S)] for i in range(n)]
+        for i, j in enumerate(cells):
+            copies[i] += [
+                pltpu.make_async_copy(source.at[:, pl.ds(j * S, S)], masses[i], sems.at[i, 1]),
+                pltpu.make_async_copy(boxes.at[0, j], box_ref.at[i], sems.at[i, 0]),
+            ]
+    else:
+        vb_ref, tables, later_sems = refs
+        masses = [source.at[:, pl.ds(j * S, S)] for j in cells]
     for pair in copies:
         for copy in reversed(pair):
             copy.start()
@@ -141,15 +144,15 @@
                 inner = dot(tables[i][0][...], u[i].astype(BF16)).astype(BF16)
                 vb_ref[i] = (box_ref[i] / dot(inner, tables[i][1][...])).astype(BF16)
         for i in range(n):
-            u[i] = forward(mass_ref[:, i * S : (i + 1) * S], tables[i], vb_ref.at[i])
+            u[i] = forward(masses[i][...], tables[i], vb_ref.at[i])
     for i, j in enumerate(cells):
         outs[0][:HALF, i * S : (i + 1) * S] = u[i][:HALF]
-        outs[0][HALF:, i * S : (i + 1) * S] = mass_ref[:HALF, i * S : (i + 1) * S]
+        outs[0][HALF:, i * S : (i + 1) * S] = masses[i][:HALF]
         outs[1][:, i * S : (i + 1) * S] = u[i][HALF:]
         if j == 0:
             for k in range(2):
                 outs[2 + k][:HALF] = u[i][k * HALF : (k + 1) * HALF, :HALF]
-                outs[2 + k][HALF:] = mass_ref[k * HALF : (k + 1) * HALF, i * S : i * S + HALF]
+                outs[2 + k][HALF:] = masses[i][k * HALF : (k + 1) * HALF, :HALF]
     for copy in later_copies:
         copy.wait()
 
@@ -166,18 +169,17 @@
     scratch = []
     if 0 in cells:
         shapes += [corner, corner, jax.ShapeDtypeStruct((BASE, HALF), F32)]
-        scratch.append(pltpu.VMEM((n, BOX, BOX), F32))
+        scratch += [pltpu.VMEM((n, BOX, BOX), F32), pltpu.VMEM((S, n * S), F32)]
     shapes.append(jax.ShapeDtypeStruct((len(later), BOX, BOX), F32))
     return pl.pallas_call(
         functools.partial(aligned_kernel, cells, later),
-        in_specs=[SMEM, SMEM, HBM, HBM if 0 in cells else VMEM, HBM] + [VMEM] * len(base),
+        in_specs=[SMEM, SMEM] + ([HBM, HBM] if 0 in cells else [VMEM, VMEM]) + [HBM] + [VMEM] * len(base),
         out_specs=[VMEM] * len(shapes),
         out_shape=shapes,
         scratch_shapes=scratch + [
-            pltpu.VMEM((S, n * S), F32),
             pltpu.VMEM((n, BOX, BOX), BF16),
             [table_scratch() for _ in cells],
-            pltpu.SemaphoreType.DMA((n, 2)),
+        ] + [pltpu.SemaphoreType.DMA((n, 2))] * (0 in cells) + [
             pltpu.SemaphoreType.DMA((len(later),)),
         ],
         compiler_params=PARAMS,
@@ -209,28 +211,24 @@
             before = now
 
 
-def shifted_kernel(cells, later, origin, carried, finals, kept, quads, count, shifts, widths,
-                   box_ref, base_ref, *refs):
+def shifted_kernel(cells, later, origin, carried, finals, quads, count, shifts, widths, box_ref,
+                   base_ref, *refs):
     n = len(cells)
     arrays, refs = refs[:count], refs[count:]
-    upper_ref = None
     if carried:
-        carry_ref, refs = refs[0], refs[1:]
-        if kept:
-            upper_ref, refs = refs[0], refs[1:]
+        carry_ref, upper_ref, refs = refs[0], refs[1], refs[2:]
     if later:
         later_boxes, refs = refs[0], refs[1:]
-    outs, refs = refs[:4], refs[4:]
-    if kept:
-        keep_ref, refs = refs[0], refs[1:]
+    canvas_ref, outs, refs = refs[0], refs[1:4], refs[4:]
     if later:
         later_ref, refs = refs[0], refs[1:]
-    mass_ref, ub_ref, vb_ref, v_ref, canvas_ref, tables, sems, out_sems = refs
+    mass_ref, ub_ref, vb_ref, v_ref, tables, sems = refs
     later_copies = fetch(later_boxes, later, later_ref, sems) if later else []
     canvas_ref[...] = jnp.zeros_like(canvas_ref)
     if carried:
-        first, last = carried[0] - origin, carried[1] - origin
-        canvas_ref[:REACH, first:last] = carry_ref[...]
+        first, last, start = carried
+        canvas_ref[:, first - origin : last - origin] = carry_ref[
+            :, first - start : last - start]
     for i, j in enumerate(cells):
         fill_tables(
             shifts[0, 0, j], shifts[0, 1, j], widths[0, 0, j], widths[0, 1, j], base_ref, tables[i])
@@ -263,45 +261,33 @@
     for i, j in enumerate(cells):
         place(v_ref.at[i], shifts[0, 0, j] + HALF, shifts[0, 1, j] + HALF, canvas_ref,
               j * S - origin)
-    writes = []
     at = 0
     for first, last in finals:
-        size = last - first
-        for ref, row in zip(outs, (0, S - RADIUS, 2 * S - RADIUS, 0)):
-            writes.append(pltpu.make_async_copy(
-                canvas_ref.at[pl.ds(row, ref.shape[0]), pl.ds(first - origin, size)],
-                ref.at[:, pl.ds(at, size)],
-                out_sems.at[len(writes)]))
-        at += size
-    if upper_ref is not None:
-        writes.append(pltpu.make_async_copy(
-            upper_ref, outs[3].at[:, pl.ds(at, upper_ref.shape[1])], out_sems.at[len(writes)]))
-    if kept:
-        size = kept[1] - kept[0]
-        writes.append(pltpu.make_async_copy(
-            canvas_ref.at[pl.ds(0, REACH), pl.ds(kept[0] - origin, size)], keep_ref,
-            out_sems.at[len(writes)]))
-    for copy in writes:
-        copy.start()
-    for copy in writes + later_copies:
+        for ref, row in zip(outs, (S - RADIUS, 2 * S - RADIUS, 0)):
+            ref[:, at : at + last - first] = canvas_ref[
+                row : row + ref.shape[0], first - origin : last - origin]
+        at += last - first
+    if carried and later:
+        outs[2][:, at:] = upper_ref[...]
+    for copy in later_copies:
         copy.wait()
 
 
 def shifted(cells, later, boxes, later_boxes, shifts, widths, base, quads, carried=None,
-            carry=(), finals=(), kept=None):
+            carry=(), finals=()):
     n = len(cells)
     origin = min(j * S for j in cells)
     width = max(j * S + REACH for j in cells) - origin
     total = sum(last - first for first, last in finals)
-    shapes = [jax.ShapeDtypeStruct((rows, total), F32) for rows in (OWN, NEXT, FAR, RADIUS)]
-    if kept:
-        if carried:
-            shapes[3] = jax.ShapeDtypeStruct((RADIUS, total + carry[1].shape[1]), F32)
-        shapes.append(jax.ShapeDtypeStruct((REACH, kept[1] - kept[0]), F32))
-    outs = [ANY] * len(shapes)
+    upper = carry[1].shape[1] if carried and later else 0
+    shapes = [
+        jax.ShapeDtypeStruct((REACH + 8, width), F32),
+        jax.ShapeDtypeStruct((NEXT, total), F32),
+        jax.ShapeDtypeStruct((FAR, total), F32),
+        jax.ShapeDtypeStruct((RADIUS, total + upper), F32),
+    ]
     if later:
         shapes.append(jax.ShapeDtypeStruct((len(later), BOX, BOX), F32))
-        outs.append(VMEM)
     arrays, where = [], []
     for j in cells:
         where.append([])
@@ -315,19 +301,17 @@
     arrays += carry
     return pl.pallas_call(
         functools.partial(
-            shifted_kernel, cells, later, origin, carried, finals, kept, where, count),
+            shifted_kernel, cells, later, origin, carried, finals, where, count),
         in_specs=[SMEM, SMEM, VMEM, VMEM] + [VMEM] * len(arrays) + [HBM] * bool(later),
-        out_specs=outs,
+        out_specs=[VMEM] * len(shapes),
         out_shape=shapes,
         scratch_shapes=[
             pltpu.VMEM((n, S, S), F32),
             pltpu.VMEM((n, S, S), BF16),
             pltpu.VMEM((n, BOX, BOX), BF16),
             pltpu.VMEM((n, BOX, BOX), F32),
-            pltpu.VMEM((REACH + 8, width), F32),
             [table_scratch() for _ in cells],
             pltpu.SemaphoreType.DMA((max(1, len(later)),)),
-            pltpu.SemaphoreType.DMA((4 * len(finals) + 2,)),
         ],
         compiler_params=PARAMS,
         cost_estimate=cost(n, 7),
@@ -341,9 +325,13 @@
     return [w / total for w in raw]
 
 
-def blurred_rows(own_ref, next_ref, far_ref, back_ref, win_ref, width, put):
+def blurred_rows(own, next_ref, far_ref, back_ref, win_ref, width, put):
     win_ref[:, :width] = next_ref[...]
-    win_ref[RADIUS:, :width] = win_ref[RADIUS:, :width] + own_ref[...]
+    at = 0
+    for part in own:
+        cols = slice(at, at + part.shape[1])
+        win_ref[RADIUS:, cols] = win_ref[RADIUS:, cols] + part[...]
+        at += part.shape[1]
     win_ref[:FAR, :width] = win_ref[:FAR, :width] + far_ref[...]
     win_ref[NEXT - RADIUS :, :width] = win_ref[NEXT - RADIUS :, :width] + back_ref[...]
     weights = blur_weights()
@@ -357,7 +345,7 @@
 
 
 def edges_kernel(*refs):
-    (own3, next3, far3, own2, next2, far2, back2, main_ref, right_ref, east_ref, west_ref,
+    (canvas3, next3, far3, canvas2, next2, far2, back2, main_ref, right_ref, east_ref, west_ref,
      win_ref) = refs
 
     def outer(c, out):
@@ -375,6 +363,8 @@
             east_ref[S:, :S] = out.T[HALF - RADIUS :]
             east_ref[S:, S:] = jnp.zeros((RADIUS, HALF), F32)
 
+    own3 = [canvas3.at[:OWN, 3 * HALF :]]
+    own2 = [canvas2.at[:OWN, :S], canvas2.at[:OWN, 7 * HALF :]]
     blurred_rows(own3, next3, far3, back2.at[:, 2 * S :], win_ref, S, outer)
     blurred_rows(own2, next2, far2, back2.at[:, : 2 * S], win_ref, 2 * S, inner)
 
@@ -405,8 +395,8 @@
     return high, (full - high.astype(np.float64)).astype(jnp.bfloat16)
 
 
-def final_kernel(own1, next1, far1, back1, main_ref, right_ref, east_ref, west_ref, high_ref,
-                 low_ref, out_ref, rows_ref, win_ref):
+def final_kernel(canvas1, next1, far1, back1, main_ref, right_ref, east_ref, west_ref, high_ref,
+                 low_ref, out_ref, rows_ref, win_ref, done_ref, sems):
     span = out_ref.shape[1]
     none = jnp.zeros((HALF - RADIUS, S), F32)
     win_ref[:, :HALF] = jnp.concatenate([none, east_ref[S:, :S]], 0).T
@@ -419,13 +409,19 @@
             out = out + east_ref[:S, S:]
         win_ref[:, HALF + S + c : 2 * HALF + S + c] = out
 
-    blurred_rows(own1, next1, far1, back1, rows_ref, REACH, middle)
+    blurred_rows([canvas1.at[:OWN]], next1, far1, back1, rows_ref, REACH, middle)
+    copies = []
     for c in range(0, span, S):
         strip = win_ref[:, c : c + 2 * S]
         high = strip.astype(BF16)
         low = (strip - high.astype(F32)).astype(BF16)
-        out_ref[:, c : c + S] = (
+        done_ref[:, c : c + S] = (
             dot(high, high_ref[...]) + dot(high, low_ref[...]) + dot(low, high_ref[...]))
+        copies.append(pltpu.make_async_copy(
+            done_ref.at[:, pl.ds(c, S)], out_ref.at[:, pl.ds(c, S)], sems.at[c // S]))
+        copies[-1].start()
+    for copy in copies:
+        copy.wait()
 
 
 def final(span, *arrays):
@@ -433,11 +429,13 @@
     return pl.pallas_call(
         final_kernel,
         in_specs=[VMEM] * 10,
-        out_specs=VMEM,
+        out_specs=ANY,
         out_shape=jax.ShapeDtypeStruct((S, span), F32),
         scratch_shapes=[
             pltpu.VMEM((NEXT, REACH), F32),
             pltpu.VMEM((S, span + 2 * HALF), F32),
+            pltpu.VMEM((S, span), F32),
+            pltpu.SemaphoreType.DMA((span // S,)),
         ],
         compiler_params=PARAMS,
         name="final",
@@ -481,7 +479,7 @@
     east = moved(left_bot, 0, -1)
     diag = moved(left_top, -1, -1)
     top12, bot12, boxes3 = aligned(
-        (1, 2), (3,), masses, boxes12, boxes_b, shifts_a, widths_a, base)
+        (1, 2), (3,), source, boxes12, boxes_b, shifts_a, widths_a, base)
     rtop12 = moved(top12, -1, 0)
     own = [(bot03, 0), (bot03, 1), (bot12, 0), (bot12, 1), (bot12, 2), (bot12, 3), (bot03, 2),
            (bot03, 3), (east, 0)]
@@ -496,21 +494,20 @@
             (source, (1, b)) if j < 3 else (east, (1, 0)),
         ]
         quads[j] += [(array, (1, at)) for array, at in (below[a], below[b])]
-    own3, next3, far3, back3, carry, boxes02 = shifted(
+    canvas3, next3, far3, back3, boxes02 = shifted(
         (3,), (0, 2), boxes3, boxes_b, shifts_b, widths_b, base, quads,
-        finals=((1152, 1408),), kept=(768, 1152))
+        finals=((1152, 1408),))
     next3 = moved(next3, 1, 0)
     far3 = moved(far3, 2, 0)
-    own2, next2, far2, back2, carry, boxes1 = shifted(
+    canvas2, next2, far2, back2, boxes1 = shifted(
         (0, 2), (1,), boxes02, boxes_b, shifts_b, widths_b, base, quads,
-        carried=(768, 1152), carry=(carry, back3), finals=((0, 256), (896, 1152)),
-        kept=(256, 896))
+        carried=(768, 1152, 768), carry=(canvas3, back3), finals=((0, 256), (896, 1152)))
     next2 = moved(next2, 1, 0)
     far2 = moved(far2, 2, 0)
     rback2 = moved(back2, -1, 0)
-    own1, next1, far1, back1 = shifted(
+    canvas1, next1, far1, back1 = shifted(
         (1,), (), boxes1, None, shifts_b, widths_b, base, quads,
-        carried=(256, 896), carry=(behind(carry, next3, far3),),
+        carried=(256, 896, 0), carry=(canvas2, behind(back3, next3, far3)),
         finals=((256, 896),))
     n_row = lax.axis_size("row")
     joined = lax.ppermute(
@@ -518,9 +515,9 @@
     far1 = lax.ppermute(far1, "row", [(i, (i + 2) % n_row) for i in range(1, n_row, 2)])
     back1 = moved(back1, -1, 0)
     next1 = moved(next1.at[:FAR].add(behind(joined, next2)), 1, 0)
-    main, right, east, west = edges(own3, next3, far3, own2, next2, far2, rback2)
+    main, right, east, west = edges(canvas3, next3, far3, canvas2, next2, far2, rback2)
     return final(
-        source.shape[1], own1, next1, far1, back1, main, right, moved(east, 0, 1),
+        source.shape[1], canvas1, next1, far1, back1, main, right, moved(east, 0, 1),
         moved(west, 0, -1))
 
 

time: 83.7 us -> 83.6 us (level)
  Pallas kernels: 30.9 us -> 29 us
  starting transfers between devices: 24.7 us -> 25.6 us
  waiting for transfers between devices: 27.5 us -> 28.4 us
    pallas_call x2, Pallas kernels: 11.3 us -> 10.3 us  [aligned(): pl.pallas_call(functools.partial(aligned_kernel, cells, later), in_specs=...]
    ppermute x9, waiting for transfers between devices: 21.9 us -> 22.8 us  [moved(): lax.ppermute(array, 'row', [(i, (i + by_row) % n_row) for i in range(n_ro...]
    ppermute x9, starting transfers between devices: 8.86 us -> 9.74 us  [moved(): lax.ppermute(array, 'row', [(i, (i + by_row) % n_row) for i in range(n_ro...]
  transfers between devices with their start and end apart: 15 -> 15, of which waited for: 5 -> 5; matrix products, arithmetic and copies ran while one was open for 0% -> 0% of each run, Pallas kernels for 27% -> 24%
where the time goes in v3:
time: 83.6 us; the launch traced here: 83.3 us
  Pallas kernels  29 us (35%)
  waiting for transfers between devices  28.4 us (34%)
  starting transfers between devices  25.6 us (31%)
    ppermute x9, waiting for transfers between devices, moved(): lax.ppermute(array, 'row', [(i, (i + by_row) % n_row) for i in range(n_ro...  22.8 us
    pallas_call x3, Pallas kernels, shifted(): pl.pallas_call(functools.partial(shifted_kernel, cells, later, origin, ca...  14.5 us
    ppermute x3, starting transfers between devices, moved(): lax.ppermute(array, 'col', [(i, (i + by_col) % n_col) for i in range(n_co...  11.3 us
    pallas_call x2, Pallas kernels, aligned(): pl.pallas_call(functools.partial(aligned_kernel, cells, later), in_specs=...  10.3 us
    ppermute x9, starting transfers between devices, moved(): lax.ppermute(array, 'row', [(i, (i + by_row) % n_row) for i in range(n_ro...  9.74 us
    ppermute x1, waiting for transfers between devices, on_device(): lax.ppermute(behind(far1, far2, rback2), 'row', [(i, i + 1) for i in rang...  5.58 us
    pallas_call x1, Pallas kernels, final(): pl.pallas_call(final_kernel, in_specs=[VMEM] * 10, out_specs=ANY, out_sha...  2.63 us
    ppermute x1, starting transfers between devices, on_device(): lax.ppermute(far1, 'row', [(i, (i + 2) % n_row) for i in range(1, n_row,...  1.91 us
  transfers between devices with their start and end apart: 15, of which 5 were waited for; matrix products, arithmetic and copies ran while one was open for 0% of the time, Pallas kernels for 24%

profile of v3, /device:TPU:1, one launch (start us, length us, event | category | flops | bytes accessed | tf_op | source)
XLA Modules:
  0.0 83.3 jit_solution(6371726200218517040)
XLA Ops:
  0.0 0.0 copy-start.2
  0.0 6.0 %aligned.2 = (f32[256,512]{1,0:T(8,128)S(1)}, f32[128,512]{1,0:T(8,128)S(1)}, f32[256,128]{1,0:T(8,128)S(1)}, f32[256,128]{1,0:T(8,128)S(1)}, f32[904,128]{1,0:T(8,128)S(1)}, /*index=5*/f32[2,512,512]{2,1,0:T(8,128)S(1)}) custom-call(s32[1,2,4]{2,1,0:T(2,128)} %bitcast.10, s32[1,2,4]{2,1,0:T(2,128)} %bitcast.12, f32[256,1024]{1,0:T(8,128)} %refs_2_.1, ...), custom_call_target="tpu_custom_call" | custom-call | flops 8040000000 | bytes 2097152 | tf_op jit(solution)/shard_map/aligned/pallas_call | solution.py:174
  6.0 6.0 %collective-permute-start = (f32[256,128]{1,0:T(8,128)S(1)}, f32[256,128]{1,0:T(8,128)S(1)}, u32[]{:S(2)}, u32[]{:S(2)}) collective-permute-start(f32[256,128]{1,0:T(8,128)S(1)} %get-tuple-element.51), channel_id=1, source_target_pairs={{0,7},{1,0},{2,1},{3,2},{4,3},{5,4},{6,5},{7,6},{8,15},{9,8},{10,9... | collective-permute-start | bytes 393224 | tf_op jit(solution)/shard_map/ppermute | solution.py:450
  12.1 1.4 %collective-permute-start.2 = (f32[256,128]{1,0:T(8,128)S(1)}, f32[256,128]{1,0:T(8,128)S(1)}, u32[]{:S(2)}, u32[]{:S(2)}) collective-permute-start(f32[256,128]{1,0:T(8,128)S(1)} %get-tuple-element.53), channel_id=1, source_target_pairs={{0,255},{1,248},{2,249},{3,250},{4,251},{5,252},{6,253},{7,254},{8... | collective-permute-start | bytes 393224 | tf_op jit(solution)/shard_map/ppermute | solution.py:456
  13.4 4.7 %collective-permute-start.1 = (f32[256,512]{1,0:T(8,128)S(1)}, f32[256,512]{1,0:T(8,128)S(1)}, u32[]{:S(2)}, u32[]{:S(2)}) collective-permute-start(f32[256,512]{1,0:T(8,128)S(1)} %get-tuple-element.52), channel_id=1, source_target_pairs={{0,248},{8,0},{16,8},{24,16},{32,24},{40,32},{48,40},{56,48},{64,5... | collective-permute-start | bytes 1572872 | tf_op jit(solution)/shard_map/ppermute | solution.py:448
  18.1 0.0 copy-done.2
  18.1 0.0 copy-start.3
  18.1 0.0 copy-start.4
  18.1 4.3 %aligned.3 = (f32[256,512]{1,0:T(8,128)S(1)}, f32[128,512]{1,0:T(8,128)S(1)}, f32[1,512,512]{2,1,0:T(8,128)S(1)}) custom-call(s32[1,2,4]{2,1,0:T(2,128)} %bitcast.11, s32[1,2,4]{2,1,0:T(2,128)} %bitcast.13, f32[256,1024]{1,0:T(8,128)S(1)} %copy-done.2, f32[2,512,512]{2,1,0:T(8,128)S(1)} %get-tuple-element.47.boxes, f32[1,4,512,512]{3,2,1,0:T(8,128)} %refs_7_.1, ...), custom_call_target="tpu_custom_call" | custom-call | flops 8040000000 | bytes 2097152 | tf_op jit(solution)/shard_map/aligned/pallas_call | solution.py:174
  22.4 1.7 %collective-permute-start.3 = (f32[256,512]{1,0:T(8,128)S(1)}, f32[256,512]{1,0:T(8,128)S(1)}, u32[]{:S(2)}, u32[]{:S(2)}) collective-permute-start(f32[256,512]{1,0:T(8,128)S(1)} %get-tuple-element.56), channel_id=1, source_target_pairs={{0,248},{8,0},{16,8},{24,16},{32,24},{40,32},{48,40},{56,48},{64,5... | collective-permute-start | bytes 1572872 | tf_op jit(solution)/shard_map/ppermute | solution.py:448
  24.1 0.0 collective-permute-done.refs_1_
  24.1 0.0 collective-permute-done.2.refs_3_
  24.1 0.0 collective-permute-done.1.refs_2_
  24.1 0.0 copy-done.3
  24.1 0.0 copy-done.4
  24.1 4.8 %shifted.3 = (f32[648,640]{1,0:T(8,128)S(1)}, f32[272,256]{1,0:T(8,128)S(1)}, f32[136,256]{1,0:T(8,128)S(1)}, f32[8,256]{1,0:T(8,128)S(1)}, f32[2,512,512]{2,1,0:T(8,128)S(1)}) custom-call(s32[1,2,4]{2,1,0:T(2,128)S(1)} %bitcast.4, s32[1,2,4]{2,1,0:T(2,128)S(1)} %bitcast.7, f32[1,512,512]{2,1,0:T(8,128)S(1)} %get-tuple-element.49.box_ref, ...), custom_call_target="tpu_custom_call" | custom-call | flops 5628000256 | bytes 1048576 | tf_op jit(solution)/shard_map/shifted/pallas_call | solution.py:302
  29.0 0.3 collective-permute-start.5
  29.3 0.2 collective-permute-start.4
  29.5 1.8 %collective-permute-done.3.refs_3_.refs_1_ = f32[256,512]{1,0:T(8,128)S(1)} collective-permute-done((f32[256,512]{1,0:T(8,128)S(1)}, f32[256,512]{1,0:T(8,128)S(1)}, u32[]{:S(2)}, u32[]{:S(2)}) %collective-permute-start.3) | collective-permute-done | bytes 524320 | tf_op jit(solution)/shard_map/ppermute | solution.py:448
  31.3 6.0 %shifted.4 = (f32[648,1152]{1,0:T(8,128)S(1)}, f32[272,512]{1,0:T(8,128)S(1)}, f32[136,512]{1,0:T(8,128)S(1)}, f32[8,768]{1,0:T(8,128)S(1)}, f32[1,512,512]{2,1,0:T(8,128)S(1)}) custom-call(s32[1,2,4]{2,1,0:T(2,128)S(1)} %bitcast.5, s32[1,2,4]{2,1,0:T(2,128)S(1)} %bitcast.8, f32[2,512,512]{2,1,0:T(8,128)S(1)} %get-tuple-element.54.box_ref, ...), custom_call_target="tpu_custom_call" | custom-call | flops 11256000512 | bytes 2097152 | tf_op jit(solution)/shard_map/shifted/pallas_call | solution.py:302
  37.3 1.5 %collective-permute-start.7 = (f32[8,768]{1,0:T(8,128)S(1)}, f32[8,768]{1,0:T(8,128)S(1)}, u32[]{:S(2)}, u32[]{:S(2)}) collective-permute-start(f32[8,768]{1,0:T(8,128)S(1)} %get-tuple-element.68), channel_id=1, source_target_pairs={{0,248},{8,0},{16,8},{24,16},{32,24},{40,32},{48,40},{56,48},{64,5... | collective-permute-start | bytes 73736 | tf_op jit(solution)/shard_map/ppermute | solution.py:448
  38.7 0.0 collective-permute-start.6
  38.7 1.2 %collective-permute-start.9 = (f32[272,512]{1,0:T(8,128)S(1)}, f32[272,512]{1,0:T(8,128)S(1)}, u32[]{:S(2)}, u32[]{:S(2)}) collective-permute-start(f32[272,512]{1,0:T(8,128)S(1)} %get-tuple-element.70), channel_id=1, source_target_pairs={{0,8},{8,16},{16,24},{24,32},{32,40},{40,48},{48,56},{56,64},{64,7... | collective-permute-start | bytes 1671176 | tf_op jit(solution)/shard_map/ppermute | solution.py:448
  40.0 0.0 collective-permute-done.5.refs_2_
  40.0 0.0 collective-permute-done.4.refs_1_
  40.0 3.7 %shifted.5 = (f32[648,640]{1,0:T(8,128)S(1)}, f32[272,640]{1,0:T(8,128)S(1)}, f32[136,640]{1,0:T(8,128)S(1)}, f32[8,640]{1,0:T(8,128)S(1)}) custom-call(s32[1,2,4]{2,1,0:T(2,128)S(1)} %bitcast.6, s32[1,2,4]{2,1,0:T(2,128)S(1)} %bitcast.9, f32[1,512,512]{2,1,0:T(8,128)S(1)} %get-tuple-element.59.box_ref, f32[904,128]{1,0:T(8,128)S(1)} %get-tuple-element.48.refs_0_.base_ref, ...), custom_call_target="tpu_custom_call" | custom-call | flops 5628000256 | bytes 1048576 | tf_op jit(solution)/shard_map/shifted/pallas_call | solution.py:302
  43.7 0.0 collective-permute-done.7.refs_6_
  43.7 2.7 %collective-permute-done.6.refs_5_ = f32[136,512]{1,0:T(8,128)S(1)} collective-permute-done((f32[136,512]{1,0:T(8,128)S(1)}, f32[136,512]{1,0:T(8,128)S(1)}, u32[]{:S(2)}, u32[]{:S(2)}) %collective-permute-start.6) | collective-permute-done | bytes 278560 | tf_op jit(solution)/shard_map/ppermute | solution.py:448
  46.4 1.3 %collective-permute-start.8 = (f32[136,640]{1,0:T(8,128)S(1)}, f32[136,640]{1,0:T(8,128)S(1)}, u32[]{:S(2)}, u32[]{:S(2)}) collective-permute-start(f32[136,640]{1,0:T(8,128)S(1)} %get-tuple-element.69), channel_id=1, source_target_pairs={{0,8},{16,24},{32,40},{48,56},{64,72},{80,88},{96,104},{112,120},{... | collective-permute-start | bytes 1044488 | tf_op jit(solution)/shard_map/ppermute | solution.py:513
  47.7 3.5 %collective-permute-done.9.refs_4_ = f32[272,512]{1,0:T(8,128)S(1)} collective-permute-done((f32[272,512]{1,0:T(8,128)S(1)}, f32[272,512]{1,0:T(8,128)S(1)}, u32[]{:S(2)}, u32[]{:S(2)}) %collective-permute-start.9) | collective-permute-done | bytes 557088 | tf_op jit(solution)/shard_map/ppermute | solution.py:448
  51.2 5.6 %collective-permute-done.8 = f32[136,640]{1,0:T(8,128)S(1)} collective-permute-done((f32[136,640]{1,0:T(8,128)S(1)}, f32[136,640]{1,0:T(8,128)S(1)}, u32[]{:S(2)}, u32[]{:S(2)}) %collective-permute-start.8) | collective-permute-done | bytes 348192 | tf_op jit(solution)/shard_map/ppermute | solution.py:513
  56.8 0.1 add_dynamic-update-slice_fusion
  56.9 0.0 copy-start
  56.9 0.0 copy-start.1
  56.9 0.1 collective-permute-start.10
  57.0 1.5 %edges.1 = (f32[256,384]{1,0:T(8,128)S(1)}, f32[256,128]{1,0:T(8,128)S(1)}, f32[264,384]{1,0:T(8,128)S(1)}, f32[8,256]{1,0:T(8,128)S(1)}) custom-call(f32[648,640]{1,0:T(8,128)S(1)} %get-tuple-element.57.refs_5_.refs_0_, f32[272,256]{1,0:T(8,128)S(1)} %collective-permute-done.4.refs_1_, f32[136,256]{1,0:T(8,128)S(1)} %collective-permute-done.5.refs_2_, ...), custom_call_target="tpu_custom_call" | custom-call | tf_op jit(solution)/shard_map/edges/pallas_call | solution.py:373
  58.5 0.4 collective-permute-start.13
  58.9 1.9 %collective-permute-start.11 = (f32[136,640]{1,0:T(8,128)S(1)}, f32[136,640]{1,0:T(8,128)S(1)}, u32[]{:S(2)}, u32[]{:S(2)}) collective-permute-start(f32[136,640]{1,0:T(8,128)S(1)} %get-tuple-element.69), channel_id=1, source_target_pairs={{8,24},{24,40},{40,56},{56,72},{72,88},{88,104},{104,120},{120,136... | collective-permute-start | bytes 1044488 | tf_op jit(solution)/shard_map/ppermute | solution.py:515
  60.8 0.1 collective-permute-start.12
  60.9 4.8 %collective-permute-start.14 = (f32[8,256]{1,0:T(8,128)S(1)}, f32[8,256]{1,0:T(8,128)S(1)}, u32[]{:S(2)}, u32[]{:S(2)}) collective-permute-start(f32[8,256]{1,0:T(8,128)S(1)} %get-tuple-element.76), channel_id=1, source_target_pairs={{0,7},{1,0},{2,1},{3,2},{4,3},{5,4},{6,5},{7,6},{8,15},{9,8},{10,9... | collective-permute-start | bytes 24584 | tf_op jit(solution)/shard_map/ppermute | solution.py:450
  65.7 14.7 %collective-permute-done.12.back1 = f32[8,640]{1,0:T(8,128)S(1)} collective-permute-done((f32[8,640]{1,0:T(8,128)S(1)}, f32[8,640]{1,0:T(8,128)S(1)}, u32[]{:S(2)}, u32[]{:S(2)}) %collective-permute-start.12) | collective-permute-done | bytes 20512 | tf_op jit(solution)/shard_map/ppermute | solution.py:448
  80.5 0.0 collective-permute-done.14.west_ref
  80.5 0.0 collective-permute-done.11.far1
  80.5 0.0 collective-permute-done.13.east_ref
  80.5 0.0 collective-permute-done.10.next1
  80.5 0.0 copy-done
  80.5 0.0 copy-done.1
  80.5 2.6 %final.1 = f32[256,1024]{1,0:T(8,128)} custom-call(f32[648,640]{1,0:T(8,128)S(1)} %get-tuple-element.64.canvas1, f32[272,640]{1,0:T(8,128)S(1)} %collective-permute-done.10.next1, f32[136,640]{1,0:T(8,128)S(1)} %collective-permute-done.11.far1, f32[8,640]{1,0:T(8,128)S(1)} %collective-permute-done.12.back1, f32[256,384]{1,0:T(8,128)S(1)} %get-tuple-element.73.main_ref, ...), custom_call_target="tpu_custom_call" | custom-call | tf_op jit(solution)/shard_map/final/pallas_call | solution.py:429
Async XLA Ops:
  0.0 18.1 %copy-start.2 = (f32[256,1024]{1,0:T(8,128)S(1)}, f32[256,1024]{1,0:T(8,128)}, u32[]{:S(2)}) copy-start(f32[256,1024]{1,0:T(8,128)} %refs_2_.1) | copy-start | bytes 3145732
  6.0 18.1 %collective-permute-start = (f32[256,128]{1,0:T(8,128)S(1)}, f32[256,128]{1,0:T(8,128)S(1)}, u32[]{:S(2)}, u32[]{:S(2)}) collective-permute-start(f32[256,128]{1,0:T(8,128)S(1)} %get-tuple-element.51), channel_id=1, source_target_pairs={{0,7},{1,0},{2,1},{3,2},{4,3},{5,4},{6,5},{7,6},{8,15},{9,8},{10,9... | collective-permute-start | bytes 393224 | tf_op jit(solution)/shard_map/ppermute | solution.py:450
  12.1 12.1 %collective-permute-start.2 = (f32[256,128]{1,0:T(8,128)S(1)}, f32[256,128]{1,0:T(8,128)S(1)}, u32[]{:S(2)}, u32[]{:S(2)}) collective-permute-start(f32[256,128]{1,0:T(8,128)S(1)} %get-tuple-element.53), channel_id=1, source_target_pairs={{0,255},{1,248},{2,249},{3,250},{4,251},{5,252},{6,253},{7,254},{8... | collective-permute-start | bytes 393224 | tf_op jit(solution)/shard_map/ppermute | solution.py:456
  13.4 10.7 %collective-permute-start.1 = (f32[256,512]{1,0:T(8,128)S(1)}, f32[256,512]{1,0:T(8,128)S(1)}, u32[]{:S(2)}, u32[]{:S(2)}) collective-permute-start(f32[256,512]{1,0:T(8,128)S(1)} %get-tuple-element.52), channel_id=1, source_target_pairs={{0,248},{8,0},{16,8},{24,16},{32,24},{40,32},{48,40},{56,48},{64,5... | collective-permute-start | bytes 1572872 | tf_op jit(solution)/shard_map/ppermute | solution.py:448
  18.1 6.0 %copy-start.3 = (s32[1,4,2]{1,2,0:T(2,128)S(1)}, s32[1,4,2]{1,2,0:T(2,128)}, u32[]{:S(2)}) copy-start(s32[1,4,2]{1,2,0:T(2,128)} %param.16) | copy-start | bytes 100
  18.1 6.0 %copy-start.4 = (s32[1,4,2]{1,2,0:T(2,128)S(1)}, s32[1,4,2]{1,2,0:T(2,128)}, u32[]{:S(2)}) copy-start(s32[1,4,2]{1,2,0:T(2,128)} %param.17) | copy-start | bytes 100
  22.4 8.9 %collective-permute-start.3 = (f32[256,512]{1,0:T(8,128)S(1)}, f32[256,512]{1,0:T(8,128)S(1)}, u32[]{:S(2)}, u32[]{:S(2)}) collective-permute-start(f32[256,512]{1,0:T(8,128)S(1)} %get-tuple-element.56), channel_id=1, source_target_pairs={{0,248},{8,0},{16,8},{24,16},{32,24},{40,32},{48,40},{56,48},{64,5... | collective-permute-start | bytes 1572872 | tf_op jit(solution)/shard_map/ppermute | solution.py:448
  29.0 11.0 %collective-permute-start.5 = (f32[136,256]{1,0:T(8,128)S(1)}, f32[136,256]{1,0:T(8,128)S(1)}, u32[]{:S(2)}, u32[]{:S(2)}) collective-permute-start(f32[136,256]{1,0:T(8,128)S(1)} %get-tuple-element.62), channel_id=1, source_target_pairs={{0,16},{8,24},{16,32},{24,40},{32,48},{40,56},{48,64},{56,72},{64,... | collective-permute-start | bytes 417800 | tf_op jit(solution)/shard_map/ppermute | solution.py:448
  29.3 10.7 %collective-permute-start.4 = (f32[272,256]{1,0:T(8,128)S(1)}, f32[272,256]{1,0:T(8,128)S(1)}, u32[]{:S(2)}, u32[]{:S(2)}) collective-permute-start(f32[272,256]{1,0:T(8,128)S(1)} %get-tuple-element.61), channel_id=1, source_target_pairs={{0,8},{8,16},{16,24},{24,32},{32,40},{40,48},{48,56},{56,64},{64,7... | collective-permute-start | bytes 835592 | tf_op jit(solution)/shard_map/ppermute | solution.py:448
  37.3 6.5 %collective-permute-start.7 = (f32[8,768]{1,0:T(8,128)S(1)}, f32[8,768]{1,0:T(8,128)S(1)}, u32[]{:S(2)}, u32[]{:S(2)}) collective-permute-start(f32[8,768]{1,0:T(8,128)S(1)} %get-tuple-element.68), channel_id=1, source_target_pairs={{0,248},{8,0},{16,8},{24,16},{32,24},{40,32},{48,40},{56,48},{64,5... | collective-permute-start | bytes 73736 | tf_op jit(solution)/shard_map/ppermute | solution.py:448
  38.7 7.7 %collective-permute-start.6 = (f32[136,512]{1,0:T(8,128)S(1)}, f32[136,512]{1,0:T(8,128)S(1)}, u32[]{:S(2)}, u32[]{:S(2)}) collective-permute-start(f32[136,512]{1,0:T(8,128)S(1)} %get-tuple-element.67), channel_id=1, source_target_pairs={{0,16},{8,24},{16,32},{24,40},{32,48},{40,56},{48,64},{56,72},{64,... | collective-permute-start | bytes 835592 | tf_op jit(solution)/shard_map/ppermute | solution.py:448
  38.7 12.5 %collective-permute-start.9 = (f32[272,512]{1,0:T(8,128)S(1)}, f32[272,512]{1,0:T(8,128)S(1)}, u32[]{:S(2)}, u32[]{:S(2)}) collective-permute-start(f32[272,512]{1,0:T(8,128)S(1)} %get-tuple-element.70), channel_id=1, source_target_pairs={{0,8},{8,16},{16,24},{24,32},{32,40},{40,48},{48,56},{56,64},{64,7... | collective-permute-start | bytes 1671176 | tf_op jit(solution)/shard_map/ppermute | solution.py:448
  46.4 10.4 %collective-permute-start.8 = (f32[136,640]{1,0:T(8,128)S(1)}, f32[136,640]{1,0:T(8,128)S(1)}, u32[]{:S(2)}, u32[]{:S(2)}) collective-permute-start(f32[136,640]{1,0:T(8,128)S(1)} %get-tuple-element.69), channel_id=1, source_target_pairs={{0,8},{16,24},{32,40},{48,56},{64,72},{80,88},{96,104},{112,120},{... | collective-permute-start | bytes 1044488 | tf_op jit(solution)/shard_map/ppermute | solution.py:513
  56.9 23.6 %copy-start = (bf16[512,256]{1,0:T(8,128)(2,1)S(1)}, bf16[512,256]{1,0:T(8,128)(2,1)}, u32[]{:S(2)}) copy-start(bf16[512,256]{1,0:T(8,128)(2,1)} %constant.33.clone.low_ref) | copy-start | bytes 786436
  56.9 23.6 %copy-start.1 = (bf16[512,256]{1,0:T(8,128)(2,1)S(1)}, bf16[512,256]{1,0:T(8,128)(2,1)}, u32[]{:S(2)}) copy-start(bf16[512,256]{1,0:T(8,128)(2,1)} %constant.32.clone.high_ref) | copy-start | bytes 786436
  56.9 23.6 %collective-permute-start.10 = (f32[272,640]{1,0:T(8,128)S(1)}, f32[272,640]{1,0:T(8,128)S(1)}, u32[]{:S(2)}, u32[]{:S(2)}) collective-permute-start(f32[272,640]{1,0:T(8,128)S(1)} %add_dynamic-update-slice_fusion), channel_id=1, source_target_pairs={{0,8},{8,16},{16,24},{24,32},{32,40},{40,48},{48,56},{56,64},{64,7... | collective-permute-start | bytes 2088968 | tf_op jit(solution)/shard_map/ppermute | solution.py:448
  58.5 22.0 %collective-permute-start.13 = (f32[264,384]{1,0:T(8,128)S(1)}, f32[264,384]{1,0:T(8,128)S(1)}, u32[]{:S(2)}, u32[]{:S(2)}) collective-permute-start(f32[264,384]{1,0:T(8,128)S(1)} %get-tuple-element.75), channel_id=1, source_target_pairs={{0,1},{1,2},{2,3},{3,4},{4,5},{5,6},{6,7},{7,0},{8,9},{9,10},{10,1... | collective-permute-start | bytes 1216520 | tf_op jit(solution)/shard_map/ppermute | solution.py:450
  58.9 21.6 %collective-permute-start.11 = (f32[136,640]{1,0:T(8,128)S(1)}, f32[136,640]{1,0:T(8,128)S(1)}, u32[]{:S(2)}, u32[]{:S(2)}) collective-permute-start(f32[136,640]{1,0:T(8,128)S(1)} %get-tuple-element.69), channel_id=1, source_target_pairs={{8,24},{24,40},{40,56},{56,72},{72,88},{88,104},{104,120},{120,136... | collective-permute-start | bytes 1044488 | tf_op jit(solution)/shard_map/ppermute | solution.py:515
  60.8 19.7 %collective-permute-start.12 = (f32[8,640]{1,0:T(8,128)S(1)}, f32[8,640]{1,0:T(8,128)S(1)}, u32[]{:S(2)}, u32[]{:S(2)}) collective-permute-start(f32[8,640]{1,0:T(8,128)S(1)} %get-tuple-element.72), channel_id=1, source_target_pairs={{0,248},{8,0},{16,8},{24,16},{32,24},{40,32},{48,40},{56,48},{64,5... | collective-permute-start | bytes 61448 | tf_op jit(solution)/shard_map/ppermute | solution.py:448
  60.9 19.6 %collective-permute-start.14 = (f32[8,256]{1,0:T(8,128)S(1)}, f32[8,256]{1,0:T(8,128)S(1)}, u32[]{:S(2)}, u32[]{:S(2)}) collective-permute-start(f32[8,256]{1,0:T(8,128)S(1)} %get-tuple-element.76), channel_id=1, source_target_pairs={{0,7},{1,0},{2,1},{3,2},{4,3},{5,4},{6,5},{7,6},{8,15},{9,8},{10,9... | collective-permute-start | bytes 24584 | tf_op jit(solution)/shard_map/ppermute | solution.py:450

commit v4 on v3

--- a/solution.py
+++ b/solution.py
@@ -99,9 +99,11 @@
 def aligned_kernel(cells, later, shifts, widths, source, boxes, later_boxes, *refs):
     n = len(cells)
     if 0 in cells:
-        outs, base_ref, later_ref, box_ref, refs = refs[:4], refs[4], refs[5], refs[6], refs[7:]
+        tops, outs, refs = refs[:n], refs[n - 1 : n + 3], refs[n + 3 :]
+        base_ref, later_ref, box_ref, refs = refs[0], refs[1], refs[2], refs[3:]
     else:
         base_ref, outs, later_ref, refs = refs[0], refs[1:3], refs[3], refs[4:]
+        tops = [outs[0].at[:, pl.ds(i * S, S)] for i in range(n)]
         box_ref = boxes
     copies = [[] for _ in cells]
     if 0 in cells:
@@ -146,8 +148,8 @@
         for i in range(n):
             u[i] = forward(masses[i][...], tables[i], vb_ref.at[i])
     for i, j in enumerate(cells):
-        outs[0][:HALF, i * S : (i + 1) * S] = u[i][:HALF]
-        outs[0][HALF:, i * S : (i + 1) * S] = masses[i][:HALF]
+        tops[i][:HALF] = u[i][:HALF]
+        tops[i][HALF:] = masses[i][:HALF]
         outs[1][:, i * S : (i + 1) * S] = u[i][HALF:]
         if j == 0:
             for k in range(2):
@@ -165,7 +167,9 @@
 def aligned(cells, later, source, boxes, later_boxes, shifts, widths, *base):
     n = len(cells)
     corner = jax.ShapeDtypeStruct((S, HALF), F32)
-    shapes = [jax.ShapeDtypeStruct((S, n * S), F32), jax.ShapeDtypeStruct((HALF, n * S), F32)]
+    apart = n if 0 in cells else 1
+    shapes = [jax.ShapeDtypeStruct((S, n * S // apart), F32)] * apart
+    shapes.append(jax.ShapeDtypeStruct((HALF, n * S), F32))
     scratch = []
     if 0 in cells:
         shapes += [corner, corner, jax.ShapeDtypeStruct((BASE, HALF), F32)]
@@ -473,9 +477,10 @@
     masses = pltpu.with_memory_space_constraint(source, pltpu.HBM)
     shifts_a = pltpu.with_memory_space_constraint(shifts_a, pltpu.HBM)
     widths_a = pltpu.with_memory_space_constraint(widths_a, pltpu.HBM)
-    top03, bot03, left_top, left_bot, base, boxes12 = aligned(
+    top0, top3, bot03, left_top, left_bot, base, boxes12 = aligned(
         (0, 3), (1, 2), masses, boxes_a, boxes_a, shifts_a, widths_a)
-    rtop03 = moved(top03, -1, 0)
+    rtop3 = moved(top3, -1, 0)
+    rtop0 = moved(top0, -1, 0)
     east = moved(left_bot, 0, -1)
     diag = moved(left_top, -1, -1)
     top12, bot12, boxes3 = aligned(
@@ -483,8 +488,8 @@
     rtop12 = moved(top12, -1, 0)
     own = [(bot03, 0), (bot03, 1), (bot12, 0), (bot12, 1), (bot12, 2), (bot12, 3), (bot03, 2),
            (bot03, 3), (east, 0)]
-    below = [(rtop03, 0), (rtop03, 1), (rtop12, 0), (rtop12, 1), (rtop12, 2), (rtop12, 3),
-             (rtop03, 2), (rtop03, 3), (diag, 0)]
+    below = [(rtop0, 0), (rtop0, 1), (rtop12, 0), (rtop12, 1), (rtop12, 2), (rtop12, 3),
+             (rtop3, 0), (rtop3, 1), (diag, 0)]
     quads = {}
     for j in range(4):
         a, b = 2 * j + 1, 2 * j + 2
@@ -511,10 +516,10 @@
         finals=((256, 896),))
     n_row = lax.axis_size("row")
     joined = lax.ppermute(
-        behind(far1, far2, rback2), "row", [(i, i + 1) for i in range(0, n_row, 2)])
+        behind(far1, far2), "row", [(i, i + 1) for i in range(0, n_row, 2)])
     far1 = lax.ppermute(far1, "row", [(i, (i + 2) % n_row) for i in range(1, n_row, 2)])
     back1 = moved(back1, -1, 0)
-    next1 = moved(next1.at[:FAR].add(behind(joined, next2)), 1, 0)
+    next1 = moved(next1.at[:FAR].add(behind(joined, next2, rback2)), 1, 0)
     main, right, east, west = edges(canvas3, next3, far3, canvas2, next2, far2, rback2)
     return final(
         source.shape[1], canvas1, next1, far1, back1, main, right, moved(east, 0, 1),

time: 83.6 us -> 81.9 us (0.980)
  waiting for transfers between devices: 28.4 us -> 26.2 us
    ppermute x1, waiting for transfers between devices: 5.58 us -> 0.01 us  [on_device(): lax.ppermute(behind(far1, far2), 'row', [(i, i + 1) for i in range(0, n_r...]
    ppermute x9 -> x10, waiting for transfers between devices: 22.8 us -> 26.1 us  [moved(): lax.ppermute(array, 'row', [(i, (i + by_row) % n_row) for i in range(n_ro...]
    ppermute x9 -> x10, starting transfers between devices: 9.74 us -> 10.1 us  [moved(): lax.ppermute(array, 'row', [(i, (i + by_row) % n_row) for i in range(n_ro...]
  transfers between devices with their start and end apart: 15 -> 16, of which waited for: 5 -> 4; matrix products, arithmetic and copies ran while one was open for 0% -> 0% of each run, Pallas kernels for 24% -> 25%
where the time goes in v4:
time: 81.9 us; the launch traced here: 81.6 us
  Pallas kernels  29.1 us (36%)
  waiting for transfers between devices  26.2 us (32%)
  starting transfers between devices  25.9 us (32%)
    ppermute x10, waiting for transfers between devices, moved(): lax.ppermute(array, 'row', [(i, (i + by_row) % n_row) for i in range(n_ro...  26.1 us
    pallas_call x3, Pallas kernels, shifted(): pl.pallas_call(functools.partial(shifted_kernel, cells, later, origin, ca...  14.7 us
    ppermute x3, starting transfers between devices, moved(): lax.ppermute(array, 'col', [(i, (i + by_col) % n_col) for i in range(n_co...  11.2 us
    pallas_call x2, Pallas kernels, aligned(): pl.pallas_call(functools.partial(aligned_kernel, cells, later), in_specs=...  10.3 us
    ppermute x10, starting transfers between devices, moved(): lax.ppermute(array, 'row', [(i, (i + by_row) % n_row) for i in range(n_ro...  10.1 us
    pallas_call x1, Pallas kernels, final(): pl.pallas_call(final_kernel, in_specs=[VMEM] * 10, out_specs=ANY, out_sha...  2.62 us
    ppermute x1, starting transfers between devices, on_device(): lax.ppermute(far1, 'row', [(i, (i + 2) % n_row) for i in range(1, n_row,...  1.91 us
  transfers between devices with their start and end apart: 16, of which 4 were waited for; matrix products, arithmetic and copies ran while one was open for 0% of the time, Pallas kernels for 25%

profile of v4, /device:TPU:1, one launch (start us, length us, event | category | flops | bytes accessed | tf_op | source)
XLA Modules:
  0.0 81.6 jit_solution(8147363068463530058)
XLA Ops:
  0.0 0.0 copy-start.2
  0.0 6.0 %aligned.2 = (f32[256,256]{1,0:T(8,128)S(1)}, f32[256,256]{1,0:T(8,128)S(1)}, f32[128,512]{1,0:T(8,128)S(1)}, f32[256,128]{1,0:T(8,128)S(1)}, f32[256,128]{1,0:T...) custom-call(s32[1,2,4]{2,1,0:T(2,128)} %bitcast.10, s32[1,2,4]{2,1,0:T(2,128)} %bitcast.12, ...), custom_call_target="tpu_custom_call" | custom-call | flops 8040000000 | bytes 2097152 | tf_op jit(solution)/shard_map/aligned/pallas_call | solution.py:178
  6.0 6.0 %collective-permute-start = (f32[256,128]{1,0:T(8,128)S(1)}, f32[256,128]{1,0:T(8,128)S(1)}, u32[]{:S(2)}, u32[]{:S(2)}) collective-permute-start(f32[256,128]{1,0:T(8,128)S(1)} %get-tuple-element.52), channel_id=1, source_target_pairs={{0,7},{1,0},{2,1},{3,2},{4,3},{5,4},{6,5},{7,6},{8,15},{9,8},{10,9... | collective-permute-start | bytes 393224 | tf_op jit(solution)/shard_map/ppermute | solution.py:454
  12.0 1.4 %collective-permute-start.2 = (f32[256,128]{1,0:T(8,128)S(1)}, f32[256,128]{1,0:T(8,128)S(1)}, u32[]{:S(2)}, u32[]{:S(2)}) collective-permute-start(f32[256,128]{1,0:T(8,128)S(1)} %get-tuple-element.54), channel_id=1, source_target_pairs={{0,255},{1,248},{2,249},{3,250},{4,251},{5,252},{6,253},{7,254},{8... | collective-permute-start | bytes 393224 | tf_op jit(solution)/shard_map/ppermute | solution.py:460
  13.4 4.7 %collective-permute-start.1 = (f32[256,256]{1,0:T(8,128)S(1)}, f32[256,256]{1,0:T(8,128)S(1)}, u32[]{:S(2)}, u32[]{:S(2)}) collective-permute-start(f32[256,256]{1,0:T(8,128)S(1)} %get-tuple-element.53), channel_id=1, source_target_pairs={{0,248},{8,0},{16,8},{24,16},{32,24},{40,32},{48,40},{56,48},{64,5... | collective-permute-start | bytes 786440 | tf_op jit(solution)/shard_map/ppermute | solution.py:452
  18.1 1.4 %collective-permute-start.3 = (f32[256,256]{1,0:T(8,128)S(1)}, f32[256,256]{1,0:T(8,128)S(1)}, u32[]{:S(2)}, u32[]{:S(2)}) collective-permute-start(f32[256,256]{1,0:T(8,128)S(1)} %get-tuple-element.57), channel_id=1, source_target_pairs={{0,248},{8,0},{16,8},{24,16},{32,24},{40,32},{48,40},{56,48},{64,5... | collective-permute-start | bytes 786440 | tf_op jit(solution)/shard_map/ppermute | solution.py:452
  19.5 0.0 copy-done.2
  19.5 0.0 copy-start.3
  19.5 0.0 copy-start.4
  19.5 4.3 %aligned.3 = (f32[256,512]{1,0:T(8,128)S(1)}, f32[128,512]{1,0:T(8,128)S(1)}, f32[1,512,512]{2,1,0:T(8,128)S(1)}) custom-call(s32[1,2,4]{2,1,0:T(2,128)} %bitcast.11, s32[1,2,4]{2,1,0:T(2,128)} %bitcast.13, f32[256,1024]{1,0:T(8,128)S(1)} %copy-done.2, f32[2,512,512]{2,1,0:T(8,128)S(1)} %get-tuple-element.48.boxes, f32[1,4,512,512]{3,2,1,0:T(8,128)} %refs_8_.1, ...), custom_call_target="tpu_custom_call" | custom-call | flops 8040000000 | bytes 2097152 | tf_op jit(solution)/shard_map/aligned/pallas_call | solution.py:178
  23.8 0.3 collective-permute-start.4
  24.1 0.0 collective-permute-done.refs_1_
  24.1 0.0 collective-permute-done.2.refs_3_
  24.1 0.0 collective-permute-done.1.refs_2_.refs_5_
  24.2 0.0 copy-done.3
  24.2 0.0 copy-done.4
  24.2 4.8 %shifted.3 = (f32[648,640]{1,0:T(8,128)S(1)}, f32[272,256]{1,0:T(8,128)S(1)}, f32[136,256]{1,0:T(8,128)S(1)}, f32[8,256]{1,0:T(8,128)S(1)}, f32[2,512,512]{2,1,0:T(8,128)S(1)}) custom-call(s32[1,2,4]{2,1,0:T(2,128)S(1)} %bitcast.4, s32[1,2,4]{2,1,0:T(2,128)S(1)} %bitcast.7, f32[1,512,512]{2,1,0:T(8,128)S(1)} %get-tuple-element.50.box_ref, ...), custom_call_target="tpu_custom_call" | custom-call | flops 5628000256 | bytes 1048576 | tf_op jit(solution)/shard_map/shifted/pallas_call | solution.py:306
  29.0 0.5 collective-permute-start.6
  29.5 1.4 %collective-permute-start.5 = (f32[272,256]{1,0:T(8,128)S(1)}, f32[272,256]{1,0:T(8,128)S(1)}, u32[]{:S(2)}, u32[]{:S(2)}) collective-permute-start(f32[272,256]{1,0:T(8,128)S(1)} %get-tuple-element.63), channel_id=1, source_target_pairs={{0,8},{8,16},{16,24},{24,32},{32,40},{40,48},{48,56},{56,64},{64,7... | collective-permute-start | bytes 835592 | tf_op jit(solution)/shard_map/ppermute | solution.py:452
  30.9 0.0 collective-permute-done.3.refs_2_
  30.9 1.8 %collective-permute-done.4.refs_3_.refs_1_ = f32[256,512]{1,0:T(8,128)S(1)} collective-permute-done((f32[256,512]{1,0:T(8,128)S(1)}, f32[256,512]{1,0:T(8,128)S(1)}, u32[]{:S(2)}, u32[]{:S(2)}) %collective-permute-start.4) | collective-permute-done | bytes 524320 | tf_op jit(solution)/shard_map/ppermute | solution.py:452
  32.7 6.1 %shifted.4 = (f32[648,1152]{1,0:T(8,128)S(1)}, f32[272,512]{1,0:T(8,128)S(1)}, f32[136,512]{1,0:T(8,128)S(1)}, f32[8,768]{1,0:T(8,128)S(1)}, f32[1,512,512]{2,1,0:T(8,128)S(1)}) custom-call(s32[1,2,4]{2,1,0:T(2,128)S(1)} %bitcast.5, s32[1,2,4]{2,1,0:T(2,128)S(1)} %bitcast.8, f32[2,512,512]{2,1,0:T(8,128)S(1)} %get-tuple-element.55.box_ref, ...), custom_call_target="tpu_custom_call" | custom-call | flops 11256000512 | bytes 2097152 | tf_op jit(solution)/shard_map/shifted/pallas_call | solution.py:306
  38.8 0.1 collective-permute-start.7
  38.9 0.3 collective-permute-start.9
  39.2 0.0 collective-permute-done.6.refs_2_
  39.3 0.0 collective-permute-done.5.refs_1_
  39.3 3.8 %shifted.5 = (f32[648,640]{1,0:T(8,128)S(1)}, f32[272,640]{1,0:T(8,128)S(1)}, f32[136,640]{1,0:T(8,128)S(1)}, f32[8,640]{1,0:T(8,128)S(1)}) custom-call(s32[1,2,4]{2,1,0:T(2,128)S(1)} %bitcast.6, s32[1,2,4]{2,1,0:T(2,128)S(1)} %bitcast.9, f32[1,512,512]{2,1,0:T(8,128)S(1)} %get-tuple-element.61.box_ref, f32[904,128]{1,0:T(8,128)S(1)} %get-tuple-element.49.refs_0_.base_ref, ...), custom_call_target="tpu_custom_call" | custom-call | flops 5628000256 | bytes 1048576 | tf_op jit(solution)/shard_map/shifted/pallas_call | solution.py:306
  43.0 6.6 %collective-permute-done.7.refs_5_ = f32[136,512]{1,0:T(8,128)S(1)} collective-permute-done((f32[136,512]{1,0:T(8,128)S(1)}, f32[136,512]{1,0:T(8,128)S(1)}, u32[]{:S(2)}, u32[]{:S(2)}) %collective-permute-start.7) | collective-permute-done | bytes 278560 | tf_op jit(solution)/shard_map/ppermute | solution.py:452
  49.6 1.3 %collective-permute-start.8 = (f32[136,640]{1,0:T(8,128)S(1)}, f32[136,640]{1,0:T(8,128)S(1)}, u32[]{:S(2)}, u32[]{:S(2)}) collective-permute-start(f32[136,640]{1,0:T(8,128)S(1)} %get-tuple-element.70), channel_id=1, source_target_pairs={{0,8},{16,24},{32,40},{48,56},{64,72},{80,88},{96,104},{112,120},{... | collective-permute-start | bytes 1044488 | tf_op jit(solution)/shard_map/ppermute | solution.py:518
  50.9 1.2 %collective-permute-start.10 = (f32[8,768]{1,0:T(8,128)S(1)}, f32[8,768]{1,0:T(8,128)S(1)}, u32[]{:S(2)}, u32[]{:S(2)}) collective-permute-start(f32[8,768]{1,0:T(8,128)S(1)} %get-tuple-element.72), channel_id=1, source_target_pairs={{0,248},{8,0},{16,8},{24,16},{32,24},{40,32},{48,40},{56,48},{64,5... | collective-permute-start | bytes 73736 | tf_op jit(solution)/shard_map/ppermute | solution.py:452
  52.1 3.8 %collective-permute-done.10.refs_6_ = f32[8,768]{1,0:T(8,128)S(1)} collective-permute-done((f32[8,768]{1,0:T(8,128)S(1)}, f32[8,768]{1,0:T(8,128)S(1)}, u32[]{:S(2)}, u32[]{:S(2)}) %collective-permute-start.10) | collective-permute-done | bytes 24608 | tf_op jit(solution)/shard_map/ppermute | solution.py:452
  55.8 0.0 collective-permute-done.9.refs_4_
  55.8 0.0 collective-permute-done.8
  55.8 0.1 add_dynamic-update-slice_fusion
  55.9 0.0 copy-start
  55.9 0.0 copy-start.1
  56.0 0.1 collective-permute-start.11
  56.0 1.5 %edges.1 = (f32[256,384]{1,0:T(8,128)S(1)}, f32[256,128]{1,0:T(8,128)S(1)}, f32[264,384]{1,0:T(8,128)S(1)}, f32[8,256]{1,0:T(8,128)S(1)}) custom-call(f32[648,640]{1,0:T(8,128)S(1)} %get-tuple-element.59.refs_6_.refs_0_, f32[272,256]{1,0:T(8,128)S(1)} %collective-permute-done.5.refs_1_, f32[136,256]{1,0:T(8,128)S(1)} %collective-permute-done.6.refs_2_, ...), custom_call_target="tpu_custom_call" | custom-call | tf_op jit(solution)/shard_map/edges/pallas_call | solution.py:377
  57.6 0.8 collective-permute-start.14
  58.3 1.9 %collective-permute-start.12 = (f32[136,640]{1,0:T(8,128)S(1)}, f32[136,640]{1,0:T(8,128)S(1)}, u32[]{:S(2)}, u32[]{:S(2)}) collective-permute-start(f32[136,640]{1,0:T(8,128)S(1)} %get-tuple-element.70), channel_id=1, source_target_pairs={{8,24},{24,40},{40,56},{56,72},{72,88},{88,104},{104,120},{120,136... | collective-permute-start | bytes 1044488 | tf_op jit(solution)/shard_map/ppermute | solution.py:520
  60.2 0.1 collective-permute-start.13
  60.3 4.5 %collective-permute-start.15 = (f32[8,256]{1,0:T(8,128)S(1)}, f32[8,256]{1,0:T(8,128)S(1)}, u32[]{:S(2)}, u32[]{:S(2)}) collective-permute-start(f32[8,256]{1,0:T(8,128)S(1)} %get-tuple-element.78), channel_id=1, source_target_pairs={{0,7},{1,0},{2,1},{3,2},{4,3},{5,4},{6,5},{7,6},{8,15},{9,8},{10,9... | collective-permute-start | bytes 24584 | tf_op jit(solution)/shard_map/ppermute | solution.py:454
  64.8 14.0 %collective-permute-done.13.back1 = f32[8,640]{1,0:T(8,128)S(1)} collective-permute-done((f32[8,640]{1,0:T(8,128)S(1)}, f32[8,640]{1,0:T(8,128)S(1)}, u32[]{:S(2)}, u32[]{:S(2)}) %collective-permute-start.13) | collective-permute-done | bytes 20512 | tf_op jit(solution)/shard_map/ppermute | solution.py:452
  78.8 0.0 collective-permute-done.12.far1
  78.8 0.0 collective-permute-done.15.west_ref
  78.8 0.0 collective-permute-done.14.east_ref
  78.8 0.0 collective-permute-done.11.next1
  78.8 0.0 copy-done
  78.8 0.0 copy-done.1
  78.8 2.6 %final.1 = f32[256,1024]{1,0:T(8,128)} custom-call(f32[648,640]{1,0:T(8,128)S(1)} %get-tuple-element.66.canvas1, f32[272,640]{1,0:T(8,128)S(1)} %collective-permute-done.11.next1, f32[136,640]{1,0:T(8,128)S(1)} %collective-permute-done.12.far1, f32[8,640]{1,0:T(8,128)S(1)} %collective-permute-done.13.back1, f32[256,384]{1,0:T(8,128)S(1)} %get-tuple-element.75.main_ref, ...), custom_call_target="tpu_custom_call" | custom-call | tf_op jit(solution)/shard_map/final/pallas_call | solution.py:433
Async XLA Ops:
  0.0 19.5 %copy-start.2 = (f32[256,1024]{1,0:T(8,128)S(1)}, f32[256,1024]{1,0:T(8,128)}, u32[]{:S(2)}) copy-start(f32[256,1024]{1,0:T(8,128)} %refs_2_.1) | copy-start | bytes 3145732
  6.0 18.1 %collective-permute-start = (f32[256,128]{1,0:T(8,128)S(1)}, f32[256,128]{1,0:T(8,128)S(1)}, u32[]{:S(2)}, u32[]{:S(2)}) collective-permute-start(f32[256,128]{1,0:T(8,128)S(1)} %get-tuple-element.52), channel_id=1, source_target_pairs={{0,7},{1,0},{2,1},{3,2},{4,3},{5,4},{6,5},{7,6},{8,15},{9,8},{10,9... | collective-permute-start | bytes 393224 | tf_op jit(solution)/shard_map/ppermute | solution.py:454
  12.0 12.1 %collective-permute-start.2 = (f32[256,128]{1,0:T(8,128)S(1)}, f32[256,128]{1,0:T(8,128)S(1)}, u32[]{:S(2)}, u32[]{:S(2)}) collective-permute-start(f32[256,128]{1,0:T(8,128)S(1)} %get-tuple-element.54), channel_id=1, source_target_pairs={{0,255},{1,248},{2,249},{3,250},{4,251},{5,252},{6,253},{7,254},{8... | collective-permute-start | bytes 393224 | tf_op jit(solution)/shard_map/ppermute | solution.py:460
  13.4 10.7 %collective-permute-start.1 = (f32[256,256]{1,0:T(8,128)S(1)}, f32[256,256]{1,0:T(8,128)S(1)}, u32[]{:S(2)}, u32[]{:S(2)}) collective-permute-start(f32[256,256]{1,0:T(8,128)S(1)} %get-tuple-element.53), channel_id=1, source_target_pairs={{0,248},{8,0},{16,8},{24,16},{32,24},{40,32},{48,40},{56,48},{64,5... | collective-permute-start | bytes 786440 | tf_op jit(solution)/shard_map/ppermute | solution.py:452
  18.1 12.8 %collective-permute-start.3 = (f32[256,256]{1,0:T(8,128)S(1)}, f32[256,256]{1,0:T(8,128)S(1)}, u32[]{:S(2)}, u32[]{:S(2)}) collective-permute-start(f32[256,256]{1,0:T(8,128)S(1)} %get-tuple-element.57), channel_id=1, source_target_pairs={{0,248},{8,0},{16,8},{24,16},{32,24},{40,32},{48,40},{56,48},{64,5... | collective-permute-start | bytes 786440 | tf_op jit(solution)/shard_map/ppermute | solution.py:452
  19.5 4.6 %copy-start.3 = (s32[1,4,2]{1,2,0:T(2,128)S(1)}, s32[1,4,2]{1,2,0:T(2,128)}, u32[]{:S(2)}) copy-start(s32[1,4,2]{1,2,0:T(2,128)} %param.16) | copy-start | bytes 100
  19.5 4.6 %copy-start.4 = (s32[1,4,2]{1,2,0:T(2,128)S(1)}, s32[1,4,2]{1,2,0:T(2,128)}, u32[]{:S(2)}) copy-start(s32[1,4,2]{1,2,0:T(2,128)} %param.17) | copy-start | bytes 100
  23.8 8.9 %collective-permute-start.4 = (f32[256,512]{1,0:T(8,128)S(1)}, f32[256,512]{1,0:T(8,128)S(1)}, u32[]{:S(2)}, u32[]{:S(2)}) collective-permute-start(f32[256,512]{1,0:T(8,128)S(1)} %get-tuple-element.58), channel_id=1, source_target_pairs={{0,248},{8,0},{16,8},{24,16},{32,24},{40,32},{48,40},{56,48},{64,5... | collective-permute-start | bytes 1572872 | tf_op jit(solution)/shard_map/ppermute | solution.py:452
  29.0 10.3 %collective-permute-start.6 = (f32[136,256]{1,0:T(8,128)S(1)}, f32[136,256]{1,0:T(8,128)S(1)}, u32[]{:S(2)}, u32[]{:S(2)}) collective-permute-start(f32[136,256]{1,0:T(8,128)S(1)} %get-tuple-element.64), channel_id=1, source_target_pairs={{0,16},{8,24},{16,32},{24,40},{32,48},{40,56},{48,64},{56,72},{64,... | collective-permute-start | bytes 417800 | tf_op jit(solution)/shard_map/ppermute | solution.py:452
  29.5 9.8 %collective-permute-start.5 = (f32[272,256]{1,0:T(8,128)S(1)}, f32[272,256]{1,0:T(8,128)S(1)}, u32[]{:S(2)}, u32[]{:S(2)}) collective-permute-start(f32[272,256]{1,0:T(8,128)S(1)} %get-tuple-element.63), channel_id=1, source_target_pairs={{0,8},{8,16},{16,24},{24,32},{32,40},{40,48},{48,56},{56,64},{64,7... | collective-permute-start | bytes 835592 | tf_op jit(solution)/shard_map/ppermute | solution.py:452
  38.8 10.7 %collective-permute-start.7 = (f32[136,512]{1,0:T(8,128)S(1)}, f32[136,512]{1,0:T(8,128)S(1)}, u32[]{:S(2)}, u32[]{:S(2)}) collective-permute-start(f32[136,512]{1,0:T(8,128)S(1)} %get-tuple-element.69), channel_id=1, source_target_pairs={{0,16},{8,24},{16,32},{24,40},{32,48},{40,56},{48,64},{56,72},{64,... | collective-permute-start | bytes 835592 | tf_op jit(solution)/shard_map/ppermute | solution.py:452
  38.9 16.9 %collective-permute-start.9 = (f32[272,512]{1,0:T(8,128)S(1)}, f32[272,512]{1,0:T(8,128)S(1)}, u32[]{:S(2)}, u32[]{:S(2)}) collective-permute-start(f32[272,512]{1,0:T(8,128)S(1)} %get-tuple-element.71), channel_id=1, source_target_pairs={{0,8},{8,16},{16,24},{24,32},{32,40},{40,48},{48,56},{56,64},{64,7... | collective-permute-start | bytes 1671176 | tf_op jit(solution)/shard_map/ppermute | solution.py:452
  49.6 6.3 %collective-permute-start.8 = (f32[136,640]{1,0:T(8,128)S(1)}, f32[136,640]{1,0:T(8,128)S(1)}, u32[]{:S(2)}, u32[]{:S(2)}) collective-permute-start(f32[136,640]{1,0:T(8,128)S(1)} %get-tuple-element.70), channel_id=1, source_target_pairs={{0,8},{16,24},{32,40},{48,56},{64,72},{80,88},{96,104},{112,120},{... | collective-permute-start | bytes 1044488 | tf_op jit(solution)/shard_map/ppermute | solution.py:518
  50.9 5.0 %collective-permute-start.10 = (f32[8,768]{1,0:T(8,128)S(1)}, f32[8,768]{1,0:T(8,128)S(1)}, u32[]{:S(2)}, u32[]{:S(2)}) collective-permute-start(f32[8,768]{1,0:T(8,128)S(1)} %get-tuple-element.72), channel_id=1, source_target_pairs={{0,248},{8,0},{16,8},{24,16},{32,24},{40,32},{48,40},{56,48},{64,5... | collective-permute-start | bytes 73736 | tf_op jit(solution)/shard_map/ppermute | solution.py:452
  55.9 22.9 %copy-start = (bf16[512,256]{1,0:T(8,128)(2,1)S(1)}, bf16[512,256]{1,0:T(8,128)(2,1)}, u32[]{:S(2)}) copy-start(bf16[512,256]{1,0:T(8,128)(2,1)} %constant.33.clone.low_ref) | copy-start | bytes 786436
  55.9 22.9 %copy-start.1 = (bf16[512,256]{1,0:T(8,128)(2,1)S(1)}, bf16[512,256]{1,0:T(8,128)(2,1)}, u32[]{:S(2)}) copy-start(bf16[512,256]{1,0:T(8,128)(2,1)} %constant.32.clone.high_ref) | copy-start | bytes 786436
  56.0 22.9 %collective-permute-start.11 = (f32[272,640]{1,0:T(8,128)S(1)}, f32[272,640]{1,0:T(8,128)S(1)}, u32[]{:S(2)}, u32[]{:S(2)}) collective-permute-start(f32[272,640]{1,0:T(8,128)S(1)} %add_dynamic-update-slice_fusion), channel_id=1, source_target_pairs={{0,8},{8,16},{16,24},{24,32},{32,40},{40,48},{48,56},{56,64},{64,7... | collective-permute-start | bytes 2088968 | tf_op jit(solution)/shard_map/ppermute | solution.py:452
  57.6 21.3 %collective-permute-start.14 = (f32[264,384]{1,0:T(8,128)S(1)}, f32[264,384]{1,0:T(8,128)S(1)}, u32[]{:S(2)}, u32[]{:S(2)}) collective-permute-start(f32[264,384]{1,0:T(8,128)S(1)} %get-tuple-element.77), channel_id=1, source_target_pairs={{0,1},{1,2},{2,3},{3,4},{4,5},{5,6},{6,7},{7,0},{8,9},{9,10},{10,1... | collective-permute-start | bytes 1216520 | tf_op jit(solution)/shard_map/ppermute | solution.py:454
  58.3 20.5 %collective-permute-start.12 = (f32[136,640]{1,0:T(8,128)S(1)}, f32[136,640]{1,0:T(8,128)S(1)}, u32[]{:S(2)}, u32[]{:S(2)}) collective-permute-start(f32[136,640]{1,0:T(8,128)S(1)} %get-tuple-element.70), channel_id=1, source_target_pairs={{8,24},{24,40},{40,56},{56,72},{72,88},{88,104},{104,120},{120,136... | collective-permute-start | bytes 1044488 | tf_op jit(solution)/shard_map/ppermute | solution.py:520
  60.2 18.6 %collective-permute-start.13 = (f32[8,640]{1,0:T(8,128)S(1)}, f32[8,640]{1,0:T(8,128)S(1)}, u32[]{:S(2)}, u32[]{:S(2)}) collective-permute-start(f32[8,640]{1,0:T(8,128)S(1)} %get-tuple-element.74), channel_id=1, source_target_pairs={{0,248},{8,0},{16,8},{24,16},{32,24},{40,32},{48,40},{56,48},{64,5... | collective-permute-start | bytes 61448 | tf_op jit(solution)/shard_map/ppermute | solution.py:452
  60.3 18.5 %collective-permute-start.15 = (f32[8,256]{1,0:T(8,128)S(1)}, f32[8,256]{1,0:T(8,128)S(1)}, u32[]{:S(2)}, u32[]{:S(2)}) collective-permute-start(f32[8,256]{1,0:T(8,128)S(1)} %get-tuple-element.78), channel_id=1, source_target_pairs={{0,7},{1,0},{2,1},{3,2},{4,3},{5,4},{6,5},{7,6},{8,15},{9,8},{10,9... | collective-permute-start | bytes 24584 | tf_op jit(solution)/shard_map/ppermute | solution.py:454

commit v5 on v4

--- a/solution.py
+++ b/solution.py
@@ -21,6 +21,7 @@
 BF16 = jnp.bfloat16
 OWN = S + RADIUS
 NEXT = S + 2 * RADIUS
+NC_CELLS = 4
 FAR = REACH - 2 * S + RADIUS
 BASE = 904
 VMEM = pl.BlockSpec(memory_space=pltpu.VMEM)
@@ -102,8 +103,9 @@
         tops, outs, refs = refs[:n], refs[n - 1 : n + 3], refs[n + 3 :]
         base_ref, later_ref, box_ref, refs = refs[0], refs[1], refs[2], refs[3:]
     else:
-        base_ref, outs, later_ref, refs = refs[0], refs[1:3], refs[3], refs[4:]
-        tops = [outs[0].at[:, pl.ds(i * S, S)] for i in range(n)]
+        base_ref, first_ref, outs, later_ref, refs = refs[0], refs[1], refs[2:4], refs[4], refs[5:]
+        tops = [outs[0].at[:, pl.ds(S + i * S, S)] for i in range(n)]
+        outs[0][:, :S] = first_ref[...]
         box_ref = boxes
     copies = [[] for _ in cells]
     if 0 in cells:
@@ -148,8 +150,9 @@
         for i in range(n):
             u[i] = forward(masses[i][...], tables[i], vb_ref.at[i])
     for i, j in enumerate(cells):
-        tops[i][:HALF] = u[i][:HALF]
-        tops[i][HALF:] = masses[i][:HALF]
+        tops[i][:HALF, :S] = u[i][:HALF]
+        if j == NC_CELLS - 1:
+            tops[i][HALF:] = masses[i][:HALF]
         outs[1][:, i * S : (i + 1) * S] = u[i][HALF:]
         if j == 0:
             for k in range(2):
@@ -167,8 +170,10 @@
 def aligned(cells, later, source, boxes, later_boxes, shifts, widths, *base):
     n = len(cells)
     corner = jax.ShapeDtypeStruct((S, HALF), F32)
-    apart = n if 0 in cells else 1
-    shapes = [jax.ShapeDtypeStruct((S, n * S // apart), F32)] * apart
+    if 0 in cells:
+        shapes = [jax.ShapeDtypeStruct((HALF, S), F32), jax.ShapeDtypeStruct((S, S), F32)]
+    else:
+        shapes = [jax.ShapeDtypeStruct((HALF, (n + 1) * S), F32)]
     shapes.append(jax.ShapeDtypeStruct((HALF, n * S), F32))
     scratch = []
     if 0 in cells:
@@ -477,28 +482,30 @@
     masses = pltpu.with_memory_space_constraint(source, pltpu.HBM)
     shifts_a = pltpu.with_memory_space_constraint(shifts_a, pltpu.HBM)
     widths_a = pltpu.with_memory_space_constraint(widths_a, pltpu.HBM)
+    rmass = moved(source[:HALF, : (NC_CELLS - 1) * S], -1, 0)
     top0, top3, bot03, left_top, left_bot, base, boxes12 = aligned(
         (0, 3), (1, 2), masses, boxes_a, boxes_a, shifts_a, widths_a)
     rtop3 = moved(top3, -1, 0)
-    rtop0 = moved(top0, -1, 0)
     east = moved(left_bot, 0, -1)
     diag = moved(left_top, -1, -1)
-    top12, bot12, boxes3 = aligned(
-        (1, 2), (3,), source, boxes12, boxes_b, shifts_a, widths_a, base)
-    rtop12 = moved(top12, -1, 0)
+    top012, bot12, boxes3 = aligned(
+        (1, 2), (3,), source, boxes12, boxes_b, shifts_a, widths_a, behind(base, rmass), top0)
+    rtop012 = moved(top012, -1, 0)
     own = [(bot03, 0), (bot03, 1), (bot12, 0), (bot12, 1), (bot12, 2), (bot12, 3), (bot03, 2),
            (bot03, 3), (east, 0)]
-    below = [(rtop0, 0), (rtop0, 1), (rtop12, 0), (rtop12, 1), (rtop12, 2), (rtop12, 3),
-             (rtop3, 0), (rtop3, 1), (diag, 0)]
+    below = [(rtop012, k) for k in range(6)] + [(rtop3, 0), (rtop3, 1), (diag, 0)]
+    mass = [(rmass, (0, k)) for k in range(6)] + [
+        (rtop3, (1, 0)), (rtop3, (1, 1)), (diag, (1, 0))]
     quads = {}
-    for j in range(4):
+    for j in range(NC_CELLS):
         a, b = 2 * j + 1, 2 * j + 2
         quads[j] = [(array, (0, at)) for array, at in (own[a], own[b], below[a], below[b])]
         quads[j] += [
             (source, (1, a)),
-            (source, (1, b)) if j < 3 else (east, (1, 0)),
+            (source, (1, b)) if j < NC_CELLS - 1 else (east, (1, 0)),
+            mass[a],
+            mass[b],
         ]
-        quads[j] += [(array, (1, at)) for array, at in (below[a], below[b])]
     canvas3, next3, far3, back3, boxes02 = shifted(
         (3,), (0, 2), boxes3, boxes_b, shifts_b, widths_b, base, quads,
         finals=((1152, 1408),))
@@ -512,7 +519,7 @@
     rback2 = moved(back2, -1, 0)
     canvas1, next1, far1, back1 = shifted(
         (1,), (), boxes1, None, shifts_b, widths_b, base, quads,
-        carried=(256, 896, 0), carry=(canvas2, behind(back3, next3, far3)),
+        carried=(256, 896, 0), carry=(behind(canvas2, next3, far3), back3),
         finals=((256, 896),))
     n_row = lax.axis_size("row")
     joined = lax.ppermute(

time: 81.9 us -> 87.7 us (1.071)
  waiting for transfers between devices: 26.2 us -> 29.5 us
  local copies, waits for them, and re-layouts: 0.02 us -> 1.05 us
    ppermute x10, waiting for transfers between devices: 26.1 us -> 29.5 us  [moved(): lax.ppermute(array, 'row', [(i, (i + by_row) % n_row) for i in range(n_ro...]
    ppermute x10, starting transfers between devices: 10.1 us -> 11.8 us  [moved(): lax.ppermute(array, 'row', [(i, (i + by_row) % n_row) for i in range(n_ro...]
    ppermute x3, starting transfers between devices: 11.2 us -> 10 us  [moved(): lax.ppermute(array, 'col', [(i, (i + by_col) % n_col) for i in range(n_co...]
    slice x0 -> x1, local copies, waits for them, and re-layouts: none -> 1.02 us  [on_device(): rmass = moved(source[:HALF, :(NC_CELLS - 1) * S], -1, 0)]
  transfers between devices with their start and end apart: 16 -> 16, of which waited for: 4 -> 5; matrix products, arithmetic and copies ran while one was open for 0% -> 0% of each run, Pallas kernels for 25% -> 31%
where the time goes in v5:
time: 87.7 us; the launch traced here: 87.4 us
  Pallas kernels  29.9 us (34%)
  waiting for transfers between devices  29.5 us (34%)
  starting transfers between devices  26.4 us (30%)
  local copies, waits for them, and re-layouts  1.05 us (1%)
    ppermute x10, waiting for transfers between devices, moved(): lax.ppermute(array, 'row', [(i, (i + by_row) % n_row) for i in range(n_ro...  29.5 us
    pallas_call x3, Pallas kernels, shifted(): pl.pallas_call(functools.partial(shifted_kernel, cells, later, origin, ca...  14.7 us
    ppermute x10, starting transfers between devices, moved(): lax.ppermute(array, 'row', [(i, (i + by_row) % n_row) for i in range(n_ro...  11.8 us
    pallas_call x2, Pallas kernels, aligned(): pl.pallas_call(functools.partial(aligned_kernel, cells, later), in_specs=...  11.1 us
    ppermute x3, starting transfers between devices, moved(): lax.ppermute(array, 'col', [(i, (i + by_col) % n_col) for i in range(n_co...  10 us
    pallas_call x1, Pallas kernels, final(): pl.pallas_call(final_kernel, in_specs=[VMEM] * 10, out_specs=ANY, out_sha...  2.64 us
    ppermute x1, starting transfers between devices, on_device(): lax.ppermute(far1, 'row', [(i, (i + 2) % n_row) for i in range(1, n_row,...  1.91 us
  transfers between devices with their start and end apart: 16, of which 5 were waited for; matrix products, arithmetic and copies ran while one was open for 0% of the time, Pallas kernels for 31%

profile of v5, /device:TPU:1, one launch (start us, length us, event | category | flops | bytes accessed | tf_op | source)
XLA Modules:
  0.0 87.4 jit_solution(18190129800912480451)
XLA Ops:
  0.0 1.0 %slice.22 = f32[128,768]{1,0:T(8,128)S(1)} slice(f32[256,1024]{1,0:T(8,128)} %refs_2_.1), slice={[0:128], [0:768]} | slice | bytes 786432 | tf_op jit(solution)/shard_map/slice | solution.py:485
  1.0 3.3 %collective-permute-start = (f32[128,768]{1,0:T(8,128)S(1)}, f32[128,768]{1,0:T(8,128)S(1)}, u32[]{:S(2)}, u32[]{:S(2)}) collective-permute-start(f32[128,768]{1,0:T(8,128)S(1)} %slice.22), channel_id=1, source_target_pairs={{0,248},{8,0},{16,8},{24,16},{32,24},{40,32},{48,40},{56,48},{64,5... | collective-permute-start | bytes 1179656 | tf_op jit(solution)/shard_map/ppermute | solution.py:457
  4.3 0.0 copy-start.2
  4.3 6.0 %aligned.2 = (f32[128,256]{1,0:T(8,128)S(1)}, f32[256,256]{1,0:T(8,128)S(1)}, f32[128,512]{1,0:T(8,128)S(1)}, f32[256,128]{1,0:T(8,128)S(1)}, f32[256,128]{1,0:T...) custom-call(s32[1,2,4]{2,1,0:T(2,128)} %bitcast.10, s32[1,2,4]{2,1,0:T(2,128)} %bitcast.12, ...), custom_call_target="tpu_custom_call" | custom-call | flops 8040000000 | bytes 2097152 | tf_op jit(solution)/shard_map/aligned/pallas_call | solution.py:183
  10.4 4.7 %collective-permute-start.2 = (f32[256,256]{1,0:T(8,128)S(1)}, f32[256,256]{1,0:T(8,128)S(1)}, u32[]{:S(2)}, u32[]{:S(2)}) collective-permute-start(f32[256,256]{1,0:T(8,128)S(1)} %get-tuple-element.56), channel_id=1, source_target_pairs={{0,248},{8,0},{16,8},{24,16},{32,24},{40,32},{48,40},{56,48},{64,5... | collective-permute-start | bytes 786440 | tf_op jit(solution)/shard_map/ppermute | solution.py:457
  15.0 4.8 %collective-permute-start.1 = (f32[256,128]{1,0:T(8,128)S(1)}, f32[256,128]{1,0:T(8,128)S(1)}, u32[]{:S(2)}, u32[]{:S(2)}) collective-permute-start(f32[256,128]{1,0:T(8,128)S(1)} %get-tuple-element.55), channel_id=1, source_target_pairs={{0,7},{1,0},{2,1},{3,2},{4,3},{5,4},{6,5},{7,6},{8,15},{9,8},{10,9... | collective-permute-start | bytes 393224 | tf_op jit(solution)/shard_map/ppermute | solution.py:459
  19.8 1.4 %collective-permute-start.3 = (f32[256,128]{1,0:T(8,128)S(1)}, f32[256,128]{1,0:T(8,128)S(1)}, u32[]{:S(2)}, u32[]{:S(2)}) collective-permute-start(f32[256,128]{1,0:T(8,128)S(1)} %get-tuple-element.57), channel_id=1, source_target_pairs={{0,255},{1,248},{2,249},{3,250},{4,251},{5,252},{6,253},{7,254},{8... | collective-permute-start | bytes 393224 | tf_op jit(solution)/shard_map/ppermute | solution.py:465
  21.2 0.0 collective-permute-done.refs_4_.refs_3_
  21.2 0.0 copy-done.2
  21.2 0.0 copy-start.3
  21.2 0.0 copy-start.4
  21.2 5.1 %aligned.3 = (f32[128,768]{1,0:T(8,128)S(1)}, f32[128,512]{1,0:T(8,128)S(1)}, f32[1,512,512]{2,1,0:T(8,128)S(1)}) custom-call(s32[1,2,4]{2,1,0:T(2,128)} %bitcast.11, s32[1,2,4]{2,1,0:T(2,128)} %bitcast.13, f32[256,1024]{1,0:T(8,128)S(1)} %copy-done.2, f32[2,512,512]{2,1,0:T(8,128)S(1)} %get-tuple-element.49.boxes, f32[1,4,512,512]{3,2,1,0:T(8,128)} %refs_8_.1, ...), custom_call_target="tpu_custom_call" | custom-call | flops 8040000000 | bytes 2097152 | tf_op jit(solution)/shard_map/aligned/pallas_call | solution.py:183
  26.3 0.3 collective-permute-start.4
  26.6 0.0 collective-permute-done.1.refs_1_
  26.6 0.0 collective-permute-done.3.refs_3_
  26.6 0.0 collective-permute-done.2.refs_2_.refs_5_
  26.6 0.0 copy-done.3
  26.6 0.0 copy-done.4
  26.6 4.8 %shifted.3 = (f32[648,640]{1,0:T(8,128)S(1)}, f32[272,256]{1,0:T(8,128)S(1)}, f32[136,256]{1,0:T(8,128)S(1)}, f32[8,256]{1,0:T(8,128)S(1)}, f32[2,512,512]{2,1,0:T(8,128)S(1)}) custom-call(s32[1,2,4]{2,1,0:T(2,128)S(1)} %bitcast.4, s32[1,2,4]{2,1,0:T(2,128)S(1)} %bitcast.7, f32[1,512,512]{2,1,0:T(8,128)S(1)} %get-tuple-element.53.box_ref, ...), custom_call_target="tpu_custom_call" | custom-call | flops 5628000256 | bytes 1048576 | tf_op jit(solution)/shard_map/shifted/pallas_call | solution.py:311
  31.5 1.8 %collective-permute-start.5 = (f32[272,256]{1,0:T(8,128)S(1)}, f32[272,256]{1,0:T(8,128)S(1)}, u32[]{:S(2)}, u32[]{:S(2)}) collective-permute-start(f32[272,256]{1,0:T(8,128)S(1)} %get-tuple-element.65), channel_id=1, source_target_pairs={{0,8},{8,16},{16,24},{24,32},{32,40},{40,48},{48,56},{56,64},{64,7... | collective-permute-start | bytes 835592 | tf_op jit(solution)/shard_map/ppermute | solution.py:457
  33.3 0.0 collective-permute-start.6
  33.3 0.5 collective-permute-done.4.refs_2_.refs_1_
  33.8 6.1 %shifted.4 = (f32[648,1152]{1,0:T(8,128)S(1)}, f32[272,512]{1,0:T(8,128)S(1)}, f32[136,512]{1,0:T(8,128)S(1)}, f32[8,768]{1,0:T(8,128)S(1)}, f32[1,512,512]{2,1,0:T(8,128)S(1)}) custom-call(s32[1,2,4]{2,1,0:T(2,128)S(1)} %bitcast.5, s32[1,2,4]{2,1,0:T(2,128)S(1)} %bitcast.8, f32[2,512,512]{2,1,0:T(8,128)S(1)} %get-tuple-element.58.box_ref, ...), custom_call_target="tpu_custom_call" | custom-call | flops 11256000512 | bytes 2097152 | tf_op jit(solution)/shard_map/shifted/pallas_call | solution.py:311
  39.9 0.1 collective-permute-start.9
  40.0 0.3 collective-permute-start.7
  40.3 1.8 %collective-permute-done.6.refs_2_ = f32[136,256]{1,0:T(8,128)S(1)} collective-permute-done((f32[136,256]{1,0:T(8,128)S(1)}, f32[136,256]{1,0:T(8,128)S(1)}, u32[]{:S(2)}, u32[]{:S(2)}) %collective-permute-start.6) | collective-permute-done | bytes 139296 | tf_op jit(solution)/shard_map/ppermute | solution.py:457
  42.2 0.0 collective-permute-done.5.refs_1_
  42.2 3.7 %shifted.5 = (f32[648,640]{1,0:T(8,128)S(1)}, f32[272,640]{1,0:T(8,128)S(1)}, f32[136,640]{1,0:T(8,128)S(1)}, f32[8,640]{1,0:T(8,128)S(1)}) custom-call(s32[1,2,4]{2,1,0:T(2,128)S(1)} %bitcast.6, s32[1,2,4]{2,1,0:T(2,128)S(1)} %bitcast.9, f32[1,512,512]{2,1,0:T(8,128)S(1)} %get-tuple-element.63.box_ref, f32[904,128]{1,0:T(8,128)S(1)} %get-tuple-element.51.refs_0_.base_ref, ...), custom_call_target="tpu_custom_call" | custom-call | flops 5628000256 | bytes 1048576 | tf_op jit(solution)/shard_map/shifted/pallas_call | solution.py:311
  45.9 10.4 %collective-permute-done.7.refs_5_ = f32[136,512]{1,0:T(8,128)S(1)} collective-permute-done((f32[136,512]{1,0:T(8,128)S(1)}, f32[136,512]{1,0:T(8,128)S(1)}, u32[]{:S(2)}, u32[]{:S(2)}) %collective-permute-start.7) | collective-permute-done | bytes 278560 | tf_op jit(solution)/shard_map/ppermute | solution.py:457
  56.3 1.3 %collective-permute-start.8 = (f32[136,640]{1,0:T(8,128)S(1)}, f32[136,640]{1,0:T(8,128)S(1)}, u32[]{:S(2)}, u32[]{:S(2)}) collective-permute-start(f32[136,640]{1,0:T(8,128)S(1)} %get-tuple-element.72), channel_id=1, source_target_pairs={{0,8},{16,24},{32,40},{48,56},{64,72},{80,88},{96,104},{112,120},{... | collective-permute-start | bytes 1044488 | tf_op jit(solution)/shard_map/ppermute | solution.py:525
  57.6 1.2 %collective-permute-start.10 = (f32[8,768]{1,0:T(8,128)S(1)}, f32[8,768]{1,0:T(8,128)S(1)}, u32[]{:S(2)}, u32[]{:S(2)}) collective-permute-start(f32[8,768]{1,0:T(8,128)S(1)} %get-tuple-element.74), channel_id=1, source_target_pairs={{0,248},{8,0},{16,8},{24,16},{32,24},{40,32},{48,40},{56,48},{64,5... | collective-permute-start | bytes 73736 | tf_op jit(solution)/shard_map/ppermute | solution.py:457
  58.8 2.1 %collective-permute-done.10.refs_6_ = f32[8,768]{1,0:T(8,128)S(1)} collective-permute-done((f32[8,768]{1,0:T(8,128)S(1)}, f32[8,768]{1,0:T(8,128)S(1)}, u32[]{:S(2)}, u32[]{:S(2)}) %collective-permute-start.10) | collective-permute-done | bytes 24608 | tf_op jit(solution)/shard_map/ppermute | solution.py:457
  60.9 0.0 collective-permute-done.9.refs_4_
  60.9 0.0 collective-permute-done.8
  60.9 0.1 add_dynamic-update-slice_fusion
  61.0 0.0 copy-start
  61.0 0.0 copy-start.1
  61.0 0.1 collective-permute-start.11
  61.1 1.5 %edges.1 = (f32[256,384]{1,0:T(8,128)S(1)}, f32[256,128]{1,0:T(8,128)S(1)}, f32[264,384]{1,0:T(8,128)S(1)}, f32[8,256]{1,0:T(8,128)S(1)}) custom-call(f32[648,640]{1,0:T(8,128)S(1)} %get-tuple-element.61.refs_6_.refs_0_, f32[272,256]{1,0:T(8,128)S(1)} %collective-permute-done.5.refs_1_, f32[136,256]{1,0:T(8,128)S(1)} %collective-permute-done.6.refs_2_, ...), custom_call_target="tpu_custom_call" | custom-call | tf_op jit(solution)/shard_map/edges/pallas_call | solution.py:382
  62.6 1.0 %collective-permute-start.14 = (f32[264,384]{1,0:T(8,128)S(1)}, f32[264,384]{1,0:T(8,128)S(1)}, u32[]{:S(2)}, u32[]{:S(2)}) collective-permute-start(f32[264,384]{1,0:T(8,128)S(1)} %get-tuple-element.79), channel_id=1, source_target_pairs={{0,1},{1,2},{2,3},{3,4},{4,5},{5,6},{6,7},{7,0},{8,9},{9,10},{10,1... | collective-permute-start | bytes 1216520 | tf_op jit(solution)/shard_map/ppermute | solution.py:459
  63.6 1.9 %collective-permute-start.12 = (f32[136,640]{1,0:T(8,128)S(1)}, f32[136,640]{1,0:T(8,128)S(1)}, u32[]{:S(2)}, u32[]{:S(2)}) collective-permute-start(f32[136,640]{1,0:T(8,128)S(1)} %get-tuple-element.72), channel_id=1, source_target_pairs={{8,24},{24,40},{40,56},{56,72},{72,88},{88,104},{104,120},{120,136... | collective-permute-start | bytes 1044488 | tf_op jit(solution)/shard_map/ppermute | solution.py:527
  65.5 0.1 collective-permute-start.13
  65.6 4.2 %collective-permute-start.15 = (f32[8,256]{1,0:T(8,128)S(1)}, f32[8,256]{1,0:T(8,128)S(1)}, u32[]{:S(2)}, u32[]{:S(2)}) collective-permute-start(f32[8,256]{1,0:T(8,128)S(1)} %get-tuple-element.80), channel_id=1, source_target_pairs={{0,7},{1,0},{2,1},{3,2},{4,3},{5,4},{6,5},{7,6},{8,15},{9,8},{10,9... | collective-permute-start | bytes 24584 | tf_op jit(solution)/shard_map/ppermute | solution.py:459
  69.9 14.7 %collective-permute-done.13.back1 = f32[8,640]{1,0:T(8,128)S(1)} collective-permute-done((f32[8,640]{1,0:T(8,128)S(1)}, f32[8,640]{1,0:T(8,128)S(1)}, u32[]{:S(2)}, u32[]{:S(2)}) %collective-permute-start.13) | collective-permute-done | bytes 20512 | tf_op jit(solution)/shard_map/ppermute | solution.py:457
  84.5 0.0 collective-permute-done.12.far1
  84.6 0.0 collective-permute-done.15.west_ref
  84.6 0.0 collective-permute-done.14.east_ref
  84.6 0.0 collective-permute-done.11.next1
  84.6 0.0 copy-done
  84.6 0.0 copy-done.1
  84.6 2.6 %final.1 = f32[256,1024]{1,0:T(8,128)} custom-call(f32[648,640]{1,0:T(8,128)S(1)} %get-tuple-element.68.canvas1, f32[272,640]{1,0:T(8,128)S(1)} %collective-permute-done.11.next1, f32[136,640]{1,0:T(8,128)S(1)} %collective-permute-done.12.far1, f32[8,640]{1,0:T(8,128)S(1)} %collective-permute-done.13.back1, f32[256,384]{1,0:T(8,128)S(1)} %get-tuple-element.77.main_ref, ...), custom_call_target="tpu_custom_call" | custom-call | tf_op jit(solution)/shard_map/final/pallas_call | solution.py:438
Async XLA Ops:
  1.0 20.2 %collective-permute-start = (f32[128,768]{1,0:T(8,128)S(1)}, f32[128,768]{1,0:T(8,128)S(1)}, u32[]{:S(2)}, u32[]{:S(2)}) collective-permute-start(f32[128,768]{1,0:T(8,128)S(1)} %slice.22), channel_id=1, source_target_pairs={{0,248},{8,0},{16,8},{24,16},{32,24},{40,32},{48,40},{56,48},{64,5... | collective-permute-start | bytes 1179656 | tf_op jit(solution)/shard_map/ppermute | solution.py:457
  4.3 16.9 %copy-start.2 = (f32[256,1024]{1,0:T(8,128)S(1)}, f32[256,1024]{1,0:T(8,128)}, u32[]{:S(2)}) copy-start(f32[256,1024]{1,0:T(8,128)} %refs_2_.1) | copy-start | bytes 3145732
  10.4 16.2 %collective-permute-start.2 = (f32[256,256]{1,0:T(8,128)S(1)}, f32[256,256]{1,0:T(8,128)S(1)}, u32[]{:S(2)}, u32[]{:S(2)}) collective-permute-start(f32[256,256]{1,0:T(8,128)S(1)} %get-tuple-element.56), channel_id=1, source_target_pairs={{0,248},{8,0},{16,8},{24,16},{32,24},{40,32},{48,40},{56,48},{64,5... | collective-permute-start | bytes 786440 | tf_op jit(solution)/shard_map/ppermute | solution.py:457
  15.0 11.6 %collective-permute-start.1 = (f32[256,128]{1,0:T(8,128)S(1)}, f32[256,128]{1,0:T(8,128)S(1)}, u32[]{:S(2)}, u32[]{:S(2)}) collective-permute-start(f32[256,128]{1,0:T(8,128)S(1)} %get-tuple-element.55), channel_id=1, source_target_pairs={{0,7},{1,0},{2,1},{3,2},{4,3},{5,4},{6,5},{7,6},{8,15},{9,8},{10,9... | collective-permute-start | bytes 393224 | tf_op jit(solution)/shard_map/ppermute | solution.py:459
  19.8 6.8 %collective-permute-start.3 = (f32[256,128]{1,0:T(8,128)S(1)}, f32[256,128]{1,0:T(8,128)S(1)}, u32[]{:S(2)}, u32[]{:S(2)}) collective-permute-start(f32[256,128]{1,0:T(8,128)S(1)} %get-tuple-element.57), channel_id=1, source_target_pairs={{0,255},{1,248},{2,249},{3,250},{4,251},{5,252},{6,253},{7,254},{8... | collective-permute-start | bytes 393224 | tf_op jit(solution)/shard_map/ppermute | solution.py:465
  21.2 5.4 %copy-start.3 = (s32[1,4,2]{1,2,0:T(2,128)S(1)}, s32[1,4,2]{1,2,0:T(2,128)}, u32[]{:S(2)}) copy-start(s32[1,4,2]{1,2,0:T(2,128)} %param.16) | copy-start | bytes 100
  21.2 5.4 %copy-start.4 = (s32[1,4,2]{1,2,0:T(2,128)S(1)}, s32[1,4,2]{1,2,0:T(2,128)}, u32[]{:S(2)}) copy-start(s32[1,4,2]{1,2,0:T(2,128)} %param.17) | copy-start | bytes 100
  26.3 7.5 %collective-permute-start.4 = (f32[128,768]{1,0:T(8,128)S(1)}, f32[128,768]{1,0:T(8,128)S(1)}, u32[]{:S(2)}, u32[]{:S(2)}) collective-permute-start(f32[128,768]{1,0:T(8,128)S(1)} %get-tuple-element.60), channel_id=1, source_target_pairs={{0,248},{8,0},{16,8},{24,16},{32,24},{40,32},{48,40},{56,48},{64,5... | collective-permute-start | bytes 1179656 | tf_op jit(solution)/shard_map/ppermute | solution.py:457
  31.5 10.7 %collective-permute-start.5 = (f32[272,256]{1,0:T(8,128)S(1)}, f32[272,256]{1,0:T(8,128)S(1)}, u32[]{:S(2)}, u32[]{:S(2)}) collective-permute-start(f32[272,256]{1,0:T(8,128)S(1)} %get-tuple-element.65), channel_id=1, source_target_pairs={{0,8},{8,16},{16,24},{24,32},{32,40},{40,48},{48,56},{56,64},{64,7... | collective-permute-start | bytes 835592 | tf_op jit(solution)/shard_map/ppermute | solution.py:457
  33.3 8.9 %collective-permute-start.6 = (f32[136,256]{1,0:T(8,128)S(1)}, f32[136,256]{1,0:T(8,128)S(1)}, u32[]{:S(2)}, u32[]{:S(2)}) collective-permute-start(f32[136,256]{1,0:T(8,128)S(1)} %get-tuple-element.66), channel_id=1, source_target_pairs={{0,16},{8,24},{16,32},{24,40},{32,48},{40,56},{48,64},{56,72},{64,... | collective-permute-start | bytes 417800 | tf_op jit(solution)/shard_map/ppermute | solution.py:457
  39.9 21.0 %collective-permute-start.9 = (f32[272,512]{1,0:T(8,128)S(1)}, f32[272,512]{1,0:T(8,128)S(1)}, u32[]{:S(2)}, u32[]{:S(2)}) collective-permute-start(f32[272,512]{1,0:T(8,128)S(1)} %get-tuple-element.73), channel_id=1, source_target_pairs={{0,8},{8,16},{16,24},{24,32},{32,40},{40,48},{48,56},{56,64},{64,7... | collective-permute-start | bytes 1671176 | tf_op jit(solution)/shard_map/ppermute | solution.py:457
  40.0 16.3 %collective-permute-start.7 = (f32[136,512]{1,0:T(8,128)S(1)}, f32[136,512]{1,0:T(8,128)S(1)}, u32[]{:S(2)}, u32[]{:S(2)}) collective-permute-start(f32[136,512]{1,0:T(8,128)S(1)} %get-tuple-element.71), channel_id=1, source_target_pairs={{0,16},{8,24},{16,32},{24,40},{32,48},{40,56},{48,64},{56,72},{64,... | collective-permute-start | bytes 835592 | tf_op jit(solution)/shard_map/ppermute | solution.py:457
  56.3 4.6 %collective-permute-start.8 = (f32[136,640]{1,0:T(8,128)S(1)}, f32[136,640]{1,0:T(8,128)S(1)}, u32[]{:S(2)}, u32[]{:S(2)}) collective-permute-start(f32[136,640]{1,0:T(8,128)S(1)} %get-tuple-element.72), channel_id=1, source_target_pairs={{0,8},{16,24},{32,40},{48,56},{64,72},{80,88},{96,104},{112,120},{... | collective-permute-start | bytes 1044488 | tf_op jit(solution)/shard_map/ppermute | solution.py:525
  57.6 3.3 %collective-permute-start.10 = (f32[8,768]{1,0:T(8,128)S(1)}, f32[8,768]{1,0:T(8,128)S(1)}, u32[]{:S(2)}, u32[]{:S(2)}) collective-permute-start(f32[8,768]{1,0:T(8,128)S(1)} %get-tuple-element.74), channel_id=1, source_target_pairs={{0,248},{8,0},{16,8},{24,16},{32,24},{40,32},{48,40},{56,48},{64,5... | collective-permute-start | bytes 73736 | tf_op jit(solution)/shard_map/ppermute | solution.py:457
  61.0 23.6 %copy-start = (bf16[512,256]{1,0:T(8,128)(2,1)S(1)}, bf16[512,256]{1,0:T(8,128)(2,1)}, u32[]{:S(2)}) copy-start(bf16[512,256]{1,0:T(8,128)(2,1)} %constant.32.clone.high_ref) | copy-start | bytes 786436
  61.0 23.6 %copy-start.1 = (bf16[512,256]{1,0:T(8,128)(2,1)S(1)}, bf16[512,256]{1,0:T(8,128)(2,1)}, u32[]{:S(2)}) copy-start(bf16[512,256]{1,0:T(8,128)(2,1)} %constant.33.clone.low_ref) | copy-start | bytes 786436
  61.0 23.5 %collective-permute-start.11 = (f32[272,640]{1,0:T(8,128)S(1)}, f32[272,640]{1,0:T(8,128)S(1)}, u32[]{:S(2)}, u32[]{:S(2)}) collective-permute-start(f32[272,640]{1,0:T(8,128)S(1)} %add_dynamic-update-slice_fusion), channel_id=1, source_target_pairs={{0,8},{8,16},{16,24},{24,32},{32,40},{40,48},{48,56},{56,64},{64,7... | collective-permute-start | bytes 2088968 | tf_op jit(solution)/shard_map/ppermute | solution.py:457
  62.6 21.9 %collective-permute-start.14 = (f32[264,384]{1,0:T(8,128)S(1)}, f32[264,384]{1,0:T(8,128)S(1)}, u32[]{:S(2)}, u32[]{:S(2)}) collective-permute-start(f32[264,384]{1,0:T(8,128)S(1)} %get-tuple-element.79), channel_id=1, source_target_pairs={{0,1},{1,2},{2,3},{3,4},{4,5},{5,6},{6,7},{7,0},{8,9},{9,10},{10,1... | collective-permute-start | bytes 1216520 | tf_op jit(solution)/shard_map/ppermute | solution.py:459
  63.6 20.9 %collective-permute-start.12 = (f32[136,640]{1,0:T(8,128)S(1)}, f32[136,640]{1,0:T(8,128)S(1)}, u32[]{:S(2)}, u32[]{:S(2)}) collective-permute-start(f32[136,640]{1,0:T(8,128)S(1)} %get-tuple-element.72), channel_id=1, source_target_pairs={{8,24},{24,40},{40,56},{56,72},{72,88},{88,104},{104,120},{120,136... | collective-permute-start | bytes 1044488 | tf_op jit(solution)/shard_map/ppermute | solution.py:527
  65.5 19.0 %collective-permute-start.13 = (f32[8,640]{1,0:T(8,128)S(1)}, f32[8,640]{1,0:T(8,128)S(1)}, u32[]{:S(2)}, u32[]{:S(2)}) collective-permute-start(f32[8,640]{1,0:T(8,128)S(1)} %get-tuple-element.76), channel_id=1, source_target_pairs={{0,248},{8,0},{16,8},{24,16},{32,24},{40,32},{48,40},{56,48},{64,5... | collective-permute-start | bytes 61448 | tf_op jit(solution)/shard_map/ppermute | solution.py:457
  65.6 18.9 %collective-permute-start.15 = (f32[8,256]{1,0:T(8,128)S(1)}, f32[8,256]{1,0:T(8,128)S(1)}, u32[]{:S(2)}, u32[]{:S(2)}) collective-permute-start(f32[8,256]{1,0:T(8,128)S(1)} %get-tuple-element.80), channel_id=1, source_target_pairs={{0,7},{1,0},{2,1},{3,2},{4,3},{5,4},{6,5},{7,6},{8,15},{9,8},{10,9... | collective-permute-start | bytes 24584 | tf_op jit(solution)/shard_map/ppermute | solution.py:459

commit v6 on v5

--- a/solution.py
+++ b/solution.py
@@ -523,10 +523,10 @@
         finals=((256, 896),))
     n_row = lax.axis_size("row")
     joined = lax.ppermute(
-        behind(far1, far2), "row", [(i, i + 1) for i in range(0, n_row, 2)])
+        behind(far1, rback2), "row", [(i, i + 1) for i in range(0, n_row, 2)])
     far1 = lax.ppermute(far1, "row", [(i, (i + 2) % n_row) for i in range(1, n_row, 2)])
     back1 = moved(back1, -1, 0)
-    next1 = moved(next1.at[:FAR].add(behind(joined, next2, rback2)), 1, 0)
+    next1 = moved(next1.at[:FAR].add(behind(joined, next2, far2)), 1, 0)
     main, right, east, west = edges(canvas3, next3, far3, canvas2, next2, far2, rback2)
     return final(
         source.shape[1], canvas1, next1, far1, back1, main, right, moved(east, 0, 1),

time: 87.7 us -> 86.2 us (0.983)
  waiting for transfers between devices: 29.5 us -> 25.9 us
  starting transfers between devices: 26.4 us -> 28.6 us
    ppermute x10, waiting for transfers between devices: 29.5 us -> 25.9 us  [moved(): lax.ppermute(array, 'row', [(i, (i + by_row) % n_row) for i in range(n_ro...]
    ppermute x3, starting transfers between devices: 10 us -> 11.5 us  [moved(): lax.ppermute(array, 'col', [(i, (i + by_col) % n_col) for i in range(n_co...]
  transfers between devices with their start and end apart: 16 -> 16, of which waited for: 5 -> 4; matrix products, arithmetic and copies ran while one was open for 0% -> 0% of each run, Pallas kernels for 31% -> 32%
where the time goes in v6:
time: 86.2 us; the launch traced here: 85.9 us
  Pallas kernels  29.9 us (35%)
  starting transfers between devices  28.6 us (33%)
  waiting for transfers between devices  25.9 us (30%)
  local copies, waits for them, and re-layouts  1.05 us (1%)
    ppermute x10, waiting for transfers between devices, moved(): lax.ppermute(array, 'row', [(i, (i + by_row) % n_row) for i in range(n_ro...  25.9 us
    pallas_call x3, Pallas kernels, shifted(): pl.pallas_call(functools.partial(shifted_kernel, cells, later, origin, ca...  14.7 us
    ppermute x10, starting transfers between devices, moved(): lax.ppermute(array, 'row', [(i, (i + by_row) % n_row) for i in range(n_ro...  11.8 us
    ppermute x3, starting transfers between devices, moved(): lax.ppermute(array, 'col', [(i, (i + by_col) % n_col) for i in range(n_co...  11.5 us
    pallas_call x2, Pallas kernels, aligned(): pl.pallas_call(functools.partial(aligned_kernel, cells, later), in_specs=...  11.1 us
    ppermute x1, starting transfers between devices, on_device(): lax.ppermute(far1, 'row', [(i, (i + 2) % n_row) for i in range(1, n_row,...  2.66 us
    pallas_call x1, Pallas kernels, final(): pl.pallas_call(final_kernel, in_specs=[VMEM] * 10, out_specs=ANY, out_sha...  2.64 us
  transfers between devices with their start and end apart: 16, of which 4 were waited for; matrix products, arithmetic and copies ran while one was open for 0% of the time, Pallas kernels for 32%

profile of v6, /device:TPU:1, one launch (start us, length us, event | category | flops | bytes accessed | tf_op | source)
XLA Modules:
  0.0 85.9 jit_solution(11344934453912267475)
XLA Ops:
  0.0 1.0 %slice.22 = f32[128,768]{1,0:T(8,128)S(1)} slice(f32[256,1024]{1,0:T(8,128)} %refs_2_.1), slice={[0:128], [0:768]} | slice | bytes 786432 | tf_op jit(solution)/shard_map/slice | solution.py:485
  1.0 3.3 %collective-permute-start = (f32[128,768]{1,0:T(8,128)S(1)}, f32[128,768]{1,0:T(8,128)S(1)}, u32[]{:S(2)}, u32[]{:S(2)}) collective-permute-start(f32[128,768]{1,0:T(8,128)S(1)} %slice.22), channel_id=1, source_target_pairs={{0,248},{8,0},{16,8},{24,16},{32,24},{40,32},{48,40},{56,48},{64,5... | collective-permute-start | bytes 1179656 | tf_op jit(solution)/shard_map/ppermute | solution.py:457
  4.3 0.0 copy-start.2
  4.3 6.0 %aligned.2 = (f32[128,256]{1,0:T(8,128)S(1)}, f32[256,256]{1,0:T(8,128)S(1)}, f32[128,512]{1,0:T(8,128)S(1)}, f32[256,128]{1,0:T(8,128)S(1)}, f32[256,128]{1,0:T...) custom-call(s32[1,2,4]{2,1,0:T(2,128)} %bitcast.10, s32[1,2,4]{2,1,0:T(2,128)} %bitcast.12, ...), custom_call_target="tpu_custom_call" | custom-call | flops 8040000000 | bytes 2097152 | tf_op jit(solution)/shard_map/aligned/pallas_call | solution.py:183
  10.4 4.6 %collective-permute-start.2 = (f32[256,256]{1,0:T(8,128)S(1)}, f32[256,256]{1,0:T(8,128)S(1)}, u32[]{:S(2)}, u32[]{:S(2)}) collective-permute-start(f32[256,256]{1,0:T(8,128)S(1)} %get-tuple-element.56), channel_id=1, source_target_pairs={{0,248},{8,0},{16,8},{24,16},{32,24},{40,32},{48,40},{56,48},{64,5... | collective-permute-start | bytes 786440 | tf_op jit(solution)/shard_map/ppermute | solution.py:457
  15.0 4.8 %collective-permute-start.1 = (f32[256,128]{1,0:T(8,128)S(1)}, f32[256,128]{1,0:T(8,128)S(1)}, u32[]{:S(2)}, u32[]{:S(2)}) collective-permute-start(f32[256,128]{1,0:T(8,128)S(1)} %get-tuple-element.55), channel_id=1, source_target_pairs={{0,7},{1,0},{2,1},{3,2},{4,3},{5,4},{6,5},{7,6},{8,15},{9,8},{10,9... | collective-permute-start | bytes 393224 | tf_op jit(solution)/shard_map/ppermute | solution.py:459
  19.8 1.4 %collective-permute-start.3 = (f32[256,128]{1,0:T(8,128)S(1)}, f32[256,128]{1,0:T(8,128)S(1)}, u32[]{:S(2)}, u32[]{:S(2)}) collective-permute-start(f32[256,128]{1,0:T(8,128)S(1)} %get-tuple-element.57), channel_id=1, source_target_pairs={{0,255},{1,248},{2,249},{3,250},{4,251},{5,252},{6,253},{7,254},{8... | collective-permute-start | bytes 393224 | tf_op jit(solution)/shard_map/ppermute | solution.py:465
  21.2 0.0 collective-permute-done.refs_4_.refs_3_
  21.2 0.0 copy-done.2
  21.2 0.0 copy-start.3
  21.2 0.0 copy-start.4
  21.2 5.1 %aligned.3 = (f32[128,768]{1,0:T(8,128)S(1)}, f32[128,512]{1,0:T(8,128)S(1)}, f32[1,512,512]{2,1,0:T(8,128)S(1)}) custom-call(s32[1,2,4]{2,1,0:T(2,128)} %bitcast.11, s32[1,2,4]{2,1,0:T(2,128)} %bitcast.13, f32[256,1024]{1,0:T(8,128)S(1)} %copy-done.2, f32[2,512,512]{2,1,0:T(8,128)S(1)} %get-tuple-element.49.boxes, f32[1,4,512,512]{3,2,1,0:T(8,128)} %refs_8_.1, ...), custom_call_target="tpu_custom_call" | custom-call | flops 8040000000 | bytes 2097152 | tf_op jit(solution)/shard_map/aligned/pallas_call | solution.py:183
  26.3 0.3 collective-permute-start.4
  26.6 0.0 collective-permute-done.1.refs_1_
  26.6 0.0 collective-permute-done.3.refs_3_
  26.6 0.0 collective-permute-done.2.refs_2_.refs_5_
  26.6 0.0 copy-done.3
  26.6 0.0 copy-done.4
  26.6 4.8 %shifted.3 = (f32[648,640]{1,0:T(8,128)S(1)}, f32[272,256]{1,0:T(8,128)S(1)}, f32[136,256]{1,0:T(8,128)S(1)}, f32[8,256]{1,0:T(8,128)S(1)}, f32[2,512,512]{2,1,0:T(8,128)S(1)}) custom-call(s32[1,2,4]{2,1,0:T(2,128)S(1)} %bitcast.4, s32[1,2,4]{2,1,0:T(2,128)S(1)} %bitcast.7, f32[1,512,512]{2,1,0:T(8,128)S(1)} %get-tuple-element.53.box_ref, ...), custom_call_target="tpu_custom_call" | custom-call | flops 5628000256 | bytes 1048576 | tf_op jit(solution)/shard_map/shifted/pallas_call | solution.py:311
  31.5 1.8 %collective-permute-start.5 = (f32[272,256]{1,0:T(8,128)S(1)}, f32[272,256]{1,0:T(8,128)S(1)}, u32[]{:S(2)}, u32[]{:S(2)}) collective-permute-start(f32[272,256]{1,0:T(8,128)S(1)} %get-tuple-element.65), channel_id=1, source_target_pairs={{0,8},{8,16},{16,24},{24,32},{32,40},{40,48},{48,56},{56,64},{64,7... | collective-permute-start | bytes 835592 | tf_op jit(solution)/shard_map/ppermute | solution.py:457
  33.3 0.0 collective-permute-start.6
  33.3 0.5 collective-permute-done.4.refs_2_.refs_1_
  33.8 6.1 %shifted.4 = (f32[648,1152]{1,0:T(8,128)S(1)}, f32[272,512]{1,0:T(8,128)S(1)}, f32[136,512]{1,0:T(8,128)S(1)}, f32[8,768]{1,0:T(8,128)S(1)}, f32[1,512,512]{2,1,0:T(8,128)S(1)}) custom-call(s32[1,2,4]{2,1,0:T(2,128)S(1)} %bitcast.5, s32[1,2,4]{2,1,0:T(2,128)S(1)} %bitcast.8, f32[2,512,512]{2,1,0:T(8,128)S(1)} %get-tuple-element.58.box_ref, ...), custom_call_target="tpu_custom_call" | custom-call | flops 11256000512 | bytes 2097152 | tf_op jit(solution)/shard_map/shifted/pallas_call | solution.py:311
  39.9 0.1 collective-permute-start.9
  40.0 0.5 collective-permute-start.7
  40.5 1.6 %collective-permute-done.6.refs_2_ = f32[136,256]{1,0:T(8,128)S(1)} collective-permute-done((f32[136,256]{1,0:T(8,128)S(1)}, f32[136,256]{1,0:T(8,128)S(1)}, u32[]{:S(2)}, u32[]{:S(2)}) %collective-permute-start.6) | collective-permute-done | bytes 139296 | tf_op jit(solution)/shard_map/ppermute | solution.py:457
  42.1 0.0 collective-permute-done.5.refs_1_
  42.1 3.7 %shifted.5 = (f32[648,640]{1,0:T(8,128)S(1)}, f32[272,640]{1,0:T(8,128)S(1)}, f32[136,640]{1,0:T(8,128)S(1)}, f32[8,640]{1,0:T(8,128)S(1)}) custom-call(s32[1,2,4]{2,1,0:T(2,128)S(1)} %bitcast.6, s32[1,2,4]{2,1,0:T(2,128)S(1)} %bitcast.9, f32[1,512,512]{2,1,0:T(8,128)S(1)} %get-tuple-element.63.box_ref, f32[904,128]{1,0:T(8,128)S(1)} %get-tuple-element.51.refs_0_.base_ref, ...), custom_call_target="tpu_custom_call" | custom-call | flops 5628000256 | bytes 1048576 | tf_op jit(solution)/shard_map/shifted/pallas_call | solution.py:311
  45.9 0.0 collective-permute-done.7.refs_6_
  45.9 1.3 %collective-permute-start.8 = (f32[136,640]{1,0:T(8,128)S(1)}, f32[136,640]{1,0:T(8,128)S(1)}, u32[]{:S(2)}, u32[]{:S(2)}) collective-permute-start(f32[136,640]{1,0:T(8,128)S(1)} %get-tuple-element.72), channel_id=1, source_target_pairs={{0,8},{16,24},{32,40},{48,56},{64,72},{80,88},{96,104},{112,120},{... | collective-permute-start | bytes 1044488 | tf_op jit(solution)/shard_map/ppermute | solution.py:525
  47.2 0.1 collective-permute-start.10
  47.3 8.6 %collective-permute-done.10.refs_5_ = f32[136,512]{1,0:T(8,128)S(1)} collective-permute-done((f32[136,512]{1,0:T(8,128)S(1)}, f32[136,512]{1,0:T(8,128)S(1)}, u32[]{:S(2)}, u32[]{:S(2)}) %collective-permute-start.10) | collective-permute-done | bytes 278560 | tf_op jit(solution)/shard_map/ppermute | solution.py:457
  55.8 0.0 collective-permute-done.8
  55.8 0.0 collective-permute-done.9.refs_4_
  55.8 0.1 add_dynamic-update-slice_fusion
  55.9 0.0 copy-start
  55.9 0.0 copy-start.1
  55.9 0.5 collective-permute-start.11
  56.4 1.5 %edges.1 = (f32[256,384]{1,0:T(8,128)S(1)}, f32[256,128]{1,0:T(8,128)S(1)}, f32[264,384]{1,0:T(8,128)S(1)}, f32[8,256]{1,0:T(8,128)S(1)}) custom-call(f32[648,640]{1,0:T(8,128)S(1)} %get-tuple-element.61.refs_6_.refs_0_, f32[272,256]{1,0:T(8,128)S(1)} %collective-permute-done.5.refs_1_, f32[136,256]{1,0:T(8,128)S(1)} %collective-permute-done.6.refs_2_, ...), custom_call_target="tpu_custom_call" | custom-call | tf_op jit(solution)/shard_map/edges/pallas_call | solution.py:382
  57.9 1.0 %collective-permute-start.14 = (f32[264,384]{1,0:T(8,128)S(1)}, f32[264,384]{1,0:T(8,128)S(1)}, u32[]{:S(2)}, u32[]{:S(2)}) collective-permute-start(f32[264,384]{1,0:T(8,128)S(1)} %get-tuple-element.79), channel_id=1, source_target_pairs={{0,1},{1,2},{2,3},{3,4},{4,5},{5,6},{6,7},{7,0},{8,9},{9,10},{10,1... | collective-permute-start | bytes 1216520 | tf_op jit(solution)/shard_map/ppermute | solution.py:459
  58.9 2.7 %collective-permute-start.12 = (f32[136,640]{1,0:T(8,128)S(1)}, f32[136,640]{1,0:T(8,128)S(1)}, u32[]{:S(2)}, u32[]{:S(2)}) collective-permute-start(f32[136,640]{1,0:T(8,128)S(1)} %get-tuple-element.72), channel_id=1, source_target_pairs={{8,24},{24,40},{40,56},{56,72},{72,88},{88,104},{104,120},{120,136... | collective-permute-start | bytes 1044488 | tf_op jit(solution)/shard_map/ppermute | solution.py:527
  61.6 0.6 collective-permute-start.13
  62.2 5.7 %collective-permute-start.15 = (f32[8,256]{1,0:T(8,128)S(1)}, f32[8,256]{1,0:T(8,128)S(1)}, u32[]{:S(2)}, u32[]{:S(2)}) collective-permute-start(f32[8,256]{1,0:T(8,128)S(1)} %get-tuple-element.80), channel_id=1, source_target_pairs={{0,7},{1,0},{2,1},{3,2},{4,3},{5,4},{6,5},{7,6},{8,15},{9,8},{10,9... | collective-permute-start | bytes 24584 | tf_op jit(solution)/shard_map/ppermute | solution.py:459
  67.9 15.1 %collective-permute-done.13.back1 = f32[8,640]{1,0:T(8,128)S(1)} collective-permute-done((f32[8,640]{1,0:T(8,128)S(1)}, f32[8,640]{1,0:T(8,128)S(1)}, u32[]{:S(2)}, u32[]{:S(2)}) %collective-permute-start.13) | collective-permute-done | bytes 20512 | tf_op jit(solution)/shard_map/ppermute | solution.py:457
  83.0 0.0 collective-permute-done.12.far1
  83.0 0.0 collective-permute-done.15.west_ref
  83.0 0.0 collective-permute-done.14.east_ref
  83.0 0.0 collective-permute-done.11.next1
  83.1 0.0 copy-done
  83.1 0.0 copy-done.1
  83.1 2.6 %final.1 = f32[256,1024]{1,0:T(8,128)} custom-call(f32[648,640]{1,0:T(8,128)S(1)} %get-tuple-element.68.canvas1, f32[272,640]{1,0:T(8,128)S(1)} %collective-permute-done.11.next1, f32[136,640]{1,0:T(8,128)S(1)} %collective-permute-done.12.far1, f32[8,640]{1,0:T(8,128)S(1)} %collective-permute-done.13.back1, f32[256,384]{1,0:T(8,128)S(1)} %get-tuple-element.77.main_ref, ...), custom_call_target="tpu_custom_call" | custom-call | tf_op jit(solution)/shard_map/final/pallas_call | solution.py:438
Async XLA Ops:
  1.0 20.2 %collective-permute-start = (f32[128,768]{1,0:T(8,128)S(1)}, f32[128,768]{1,0:T(8,128)S(1)}, u32[]{:S(2)}, u32[]{:S(2)}) collective-permute-start(f32[128,768]{1,0:T(8,128)S(1)} %slice.22), channel_id=1, source_target_pairs={{0,248},{8,0},{16,8},{24,16},{32,24},{40,32},{48,40},{56,48},{64,5... | collective-permute-start | bytes 1179656 | tf_op jit(solution)/shard_map/ppermute | solution.py:457
  4.3 16.9 %copy-start.2 = (f32[256,1024]{1,0:T(8,128)S(1)}, f32[256,1024]{1,0:T(8,128)}, u32[]{:S(2)}) copy-start(f32[256,1024]{1,0:T(8,128)} %refs_2_.1) | copy-start | bytes 3145732
  10.4 16.2 %collective-permute-start.2 = (f32[256,256]{1,0:T(8,128)S(1)}, f32[256,256]{1,0:T(8,128)S(1)}, u32[]{:S(2)}, u32[]{:S(2)}) collective-permute-start(f32[256,256]{1,0:T(8,128)S(1)} %get-tuple-element.56), channel_id=1, source_target_pairs={{0,248},{8,0},{16,8},{24,16},{32,24},{40,32},{48,40},{56,48},{64,5... | collective-permute-start | bytes 786440 | tf_op jit(solution)/shard_map/ppermute | solution.py:457
  15.0 11.6 %collective-permute-start.1 = (f32[256,128]{1,0:T(8,128)S(1)}, f32[256,128]{1,0:T(8,128)S(1)}, u32[]{:S(2)}, u32[]{:S(2)}) collective-permute-start(f32[256,128]{1,0:T(8,128)S(1)} %get-tuple-element.55), channel_id=1, source_target_pairs={{0,7},{1,0},{2,1},{3,2},{4,3},{5,4},{6,5},{7,6},{8,15},{9,8},{10,9... | collective-permute-start | bytes 393224 | tf_op jit(solution)/shard_map/ppermute | solution.py:459
  19.8 6.8 %collective-permute-start.3 = (f32[256,128]{1,0:T(8,128)S(1)}, f32[256,128]{1,0:T(8,128)S(1)}, u32[]{:S(2)}, u32[]{:S(2)}) collective-permute-start(f32[256,128]{1,0:T(8,128)S(1)} %get-tuple-element.57), channel_id=1, source_target_pairs={{0,255},{1,248},{2,249},{3,250},{4,251},{5,252},{6,253},{7,254},{8... | collective-permute-start | bytes 393224 | tf_op jit(solution)/shard_map/ppermute | solution.py:465
  21.2 5.4 %copy-start.3 = (s32[1,4,2]{1,2,0:T(2,128)S(1)}, s32[1,4,2]{1,2,0:T(2,128)}, u32[]{:S(2)}) copy-start(s32[1,4,2]{1,2,0:T(2,128)} %param.16) | copy-start | bytes 100
  21.2 5.4 %copy-start.4 = (s32[1,4,2]{1,2,0:T(2,128)S(1)}, s32[1,4,2]{1,2,0:T(2,128)}, u32[]{:S(2)}) copy-start(s32[1,4,2]{1,2,0:T(2,128)} %param.17) | copy-start | bytes 100
  26.3 7.5 %collective-permute-start.4 = (f32[128,768]{1,0:T(8,128)S(1)}, f32[128,768]{1,0:T(8,128)S(1)}, u32[]{:S(2)}, u32[]{:S(2)}) collective-permute-start(f32[128,768]{1,0:T(8,128)S(1)} %get-tuple-element.60), channel_id=1, source_target_pairs={{0,248},{8,0},{16,8},{24,16},{32,24},{40,32},{48,40},{56,48},{64,5... | collective-permute-start | bytes 1179656 | tf_op jit(solution)/shard_map/ppermute | solution.py:457
  31.5 10.7 %collective-permute-start.5 = (f32[272,256]{1,0:T(8,128)S(1)}, f32[272,256]{1,0:T(8,128)S(1)}, u32[]{:S(2)}, u32[]{:S(2)}) collective-permute-start(f32[272,256]{1,0:T(8,128)S(1)} %get-tuple-element.65), channel_id=1, source_target_pairs={{0,8},{8,16},{16,24},{24,32},{32,40},{40,48},{48,56},{56,64},{64,7... | collective-permute-start | bytes 835592 | tf_op jit(solution)/shard_map/ppermute | solution.py:457
  33.3 8.9 %collective-permute-start.6 = (f32[136,256]{1,0:T(8,128)S(1)}, f32[136,256]{1,0:T(8,128)S(1)}, u32[]{:S(2)}, u32[]{:S(2)}) collective-permute-start(f32[136,256]{1,0:T(8,128)S(1)} %get-tuple-element.66), channel_id=1, source_target_pairs={{0,16},{8,24},{16,32},{24,40},{32,48},{40,56},{48,64},{56,72},{64,... | collective-permute-start | bytes 417800 | tf_op jit(solution)/shard_map/ppermute | solution.py:457
  39.9 15.9 %collective-permute-start.9 = (f32[272,512]{1,0:T(8,128)S(1)}, f32[272,512]{1,0:T(8,128)S(1)}, u32[]{:S(2)}, u32[]{:S(2)}) collective-permute-start(f32[272,512]{1,0:T(8,128)S(1)} %get-tuple-element.73), channel_id=1, source_target_pairs={{0,8},{8,16},{16,24},{24,32},{32,40},{40,48},{48,56},{56,64},{64,7... | collective-permute-start | bytes 1671176 | tf_op jit(solution)/shard_map/ppermute | solution.py:457
  40.0 5.9 %collective-permute-start.7 = (f32[8,768]{1,0:T(8,128)S(1)}, f32[8,768]{1,0:T(8,128)S(1)}, u32[]{:S(2)}, u32[]{:S(2)}) collective-permute-start(f32[8,768]{1,0:T(8,128)S(1)} %get-tuple-element.71), channel_id=1, source_target_pairs={{0,248},{8,0},{16,8},{24,16},{32,24},{40,32},{48,40},{56,48},{64,5... | collective-permute-start | bytes 73736 | tf_op jit(solution)/shard_map/ppermute | solution.py:457
  45.9 9.9 %collective-permute-start.8 = (f32[136,640]{1,0:T(8,128)S(1)}, f32[136,640]{1,0:T(8,128)S(1)}, u32[]{:S(2)}, u32[]{:S(2)}) collective-permute-start(f32[136,640]{1,0:T(8,128)S(1)} %get-tuple-element.72), channel_id=1, source_target_pairs={{0,8},{16,24},{32,40},{48,56},{64,72},{80,88},{96,104},{112,120},{... | collective-permute-start | bytes 1044488 | tf_op jit(solution)/shard_map/ppermute | solution.py:525
  47.2 8.6 %collective-permute-start.10 = (f32[136,512]{1,0:T(8,128)S(1)}, f32[136,512]{1,0:T(8,128)S(1)}, u32[]{:S(2)}, u32[]{:S(2)}) collective-permute-start(f32[136,512]{1,0:T(8,128)S(1)} %get-tuple-element.74), channel_id=1, source_target_pairs={{0,16},{8,24},{16,32},{24,40},{32,48},{40,56},{48,64},{56,72},{64,... | collective-permute-start | bytes 835592 | tf_op jit(solution)/shard_map/ppermute | solution.py:457
  55.9 27.1 %copy-start = (bf16[512,256]{1,0:T(8,128)(2,1)S(1)}, bf16[512,256]{1,0:T(8,128)(2,1)}, u32[]{:S(2)}) copy-start(bf16[512,256]{1,0:T(8,128)(2,1)} %constant.32.clone.high_ref) | copy-start | bytes 786436
  55.9 27.1 %copy-start.1 = (bf16[512,256]{1,0:T(8,128)(2,1)S(1)}, bf16[512,256]{1,0:T(8,128)(2,1)}, u32[]{:S(2)}) copy-start(bf16[512,256]{1,0:T(8,128)(2,1)} %constant.33.clone.low_ref) | copy-start | bytes 786436
  55.9 27.1 %collective-permute-start.11 = (f32[272,640]{1,0:T(8,128)S(1)}, f32[272,640]{1,0:T(8,128)S(1)}, u32[]{:S(2)}, u32[]{:S(2)}) collective-permute-start(f32[272,640]{1,0:T(8,128)S(1)} %add_dynamic-update-slice_fusion), channel_id=1, source_target_pairs={{0,8},{8,16},{16,24},{24,32},{32,40},{40,48},{48,56},{56,64},{64,7... | collective-permute-start | bytes 2088968 | tf_op jit(solution)/shard_map/ppermute | solution.py:457
  57.9 25.1 %collective-permute-start.14 = (f32[264,384]{1,0:T(8,128)S(1)}, f32[264,384]{1,0:T(8,128)S(1)}, u32[]{:S(2)}, u32[]{:S(2)}) collective-permute-start(f32[264,384]{1,0:T(8,128)S(1)} %get-tuple-element.79), channel_id=1, source_target_pairs={{0,1},{1,2},{2,3},{3,4},{4,5},{5,6},{6,7},{7,0},{8,9},{9,10},{10,1... | collective-permute-start | bytes 1216520 | tf_op jit(solution)/shard_map/ppermute | solution.py:459
  58.9 24.1 %collective-permute-start.12 = (f32[136,640]{1,0:T(8,128)S(1)}, f32[136,640]{1,0:T(8,128)S(1)}, u32[]{:S(2)}, u32[]{:S(2)}) collective-permute-start(f32[136,640]{1,0:T(8,128)S(1)} %get-tuple-element.72), channel_id=1, source_target_pairs={{8,24},{24,40},{40,56},{56,72},{72,88},{88,104},{104,120},{120,136... | collective-permute-start | bytes 1044488 | tf_op jit(solution)/shard_map/ppermute | solution.py:527
  61.6 21.4 %collective-permute-start.13 = (f32[8,640]{1,0:T(8,128)S(1)}, f32[8,640]{1,0:T(8,128)S(1)}, u32[]{:S(2)}, u32[]{:S(2)}) collective-permute-start(f32[8,640]{1,0:T(8,128)S(1)} %get-tuple-element.76), channel_id=1, source_target_pairs={{0,248},{8,0},{16,8},{24,16},{32,24},{40,32},{48,40},{56,48},{64,5... | collective-permute-start | bytes 61448 | tf_op jit(solution)/shard_map/ppermute | solution.py:457
  62.2 20.8 %collective-permute-start.15 = (f32[8,256]{1,0:T(8,128)S(1)}, f32[8,256]{1,0:T(8,128)S(1)}, u32[]{:S(2)}, u32[]{:S(2)}) collective-permute-start(f32[8,256]{1,0:T(8,128)S(1)} %get-tuple-element.80), channel_id=1, source_target_pairs={{0,7},{1,0},{2,1},{3,2},{4,3},{5,4},{6,5},{7,6},{8,15},{9,8},{10,9... | collective-permute-start | bytes 24584 | tf_op jit(solution)/shard_map/ppermute | solution.py:459

commit v7 on v5

--- a/solution.py
+++ b/solution.py
@@ -164,7 +164,7 @@
 
 def cost(cells, applies):
     return pl.CostEstimate(
-        flops=cells * applies * 804_000_000, bytes_accessed=cells << 20, transcendentals=0)
+        flops=cells * applies * 300_000_000, bytes_accessed=cells << 20, transcendentals=0)
 
 
 def aligned(cells, later, source, boxes, later_boxes, shifts, widths, *base):
@@ -192,7 +192,7 @@
             pltpu.SemaphoreType.DMA((len(later),)),
         ],
         compiler_params=PARAMS,
-        cost_estimate=cost(n, 5),
+        cost_estimate=cost(n, 13),
         name="aligned",
     )(shifts, widths, source, boxes, later_boxes, *base)
 
@@ -323,7 +323,7 @@
             pltpu.SemaphoreType.DMA((max(1, len(later)),)),
         ],
         compiler_params=PARAMS,
-        cost_estimate=cost(n, 7),
+        cost_estimate=cost(n, 19 if later else 7),
         name="shifted",
     )(shifts, widths, boxes, base, *arrays, *([later_boxes] if later else []))
 

time: 87.7 us -> 82.3 us (0.938)
  waiting for transfers between devices: 29.5 us -> 24.2 us
    ppermute x10, waiting for transfers between devices: 29.5 us -> 24.2 us  [moved(): lax.ppermute(array, 'row', [(i, (i + by_row) % n_row) for i in range(n_ro...]
  transfers between devices with their start and end apart: 16 -> 16, of which waited for: 5 -> 5; matrix products, arithmetic and copies ran while one was open for 0% -> 0% of each run, Pallas kernels for 31% -> 33%
where the time goes in v7:
time: 82.3 us; the launch traced here: 82 us
  Pallas kernels  29.7 us (36%)
  starting transfers between devices  26.5 us (32%)
  waiting for transfers between devices  24.2 us (29%)
  local copies, waits for them, and re-layouts  1.05 us (1%)
    ppermute x10, waiting for transfers between devices, moved(): lax.ppermute(array, 'row', [(i, (i + by_row) % n_row) for i in range(n_ro...  24.2 us
    pallas_call x3, Pallas kernels, shifted(): pl.pallas_call(functools.partial(shifted_kernel, cells, later, origin, ca...  14.7 us
    ppermute x10, starting transfers between devices, moved(): lax.ppermute(array, 'row', [(i, (i + by_row) % n_row) for i in range(n_ro...  11.9 us
    pallas_call x2, Pallas kernels, aligned(): pl.pallas_call(functools.partial(aligned_kernel, cells, later), in_specs=...  10.9 us
    ppermute x3, starting transfers between devices, moved(): lax.ppermute(array, 'col', [(i, (i + by_col) % n_col) for i in range(n_co...  10 us
    pallas_call x1, Pallas kernels, final(): pl.pallas_call(final_kernel, in_specs=[VMEM] * 10, out_specs=ANY, out_sha...  2.64 us
    ppermute x1, starting transfers between devices, on_device(): lax.ppermute(far1, 'row', [(i, (i + 2) % n_row) for i in range(1, n_row,...  1.91 us
  transfers between devices with their start and end apart: 16, of which 5 were waited for; matrix products, arithmetic and copies ran while one was open for 0% of the time, Pallas kernels for 33%

profile of v7, /device:TPU:1, one launch (start us, length us, event | category | flops | bytes accessed | tf_op | source)
XLA Modules:
  0.0 82.0 jit_solution(1551223429727836130)
XLA Ops:
  0.0 1.0 %slice.22 = f32[128,768]{1,0:T(8,128)S(1)} slice(f32[256,1024]{1,0:T(8,128)} %refs_2_.1), slice={[0:128], [0:768]} | slice | bytes 786432 | tf_op jit(solution)/shard_map/slice | solution.py:485
  1.0 3.3 %collective-permute-start = (f32[128,768]{1,0:T(8,128)S(1)}, f32[128,768]{1,0:T(8,128)S(1)}, u32[]{:S(2)}, u32[]{:S(2)}) collective-permute-start(f32[128,768]{1,0:T(8,128)S(1)} %slice.22), channel_id=1, source_target_pairs={{0,248},{8,0},{16,8},{24,16},{32,24},{40,32},{48,40},{56,48},{64,5... | collective-permute-start | bytes 1179656 | tf_op jit(solution)/shard_map/ppermute | solution.py:457
  4.3 0.0 copy-start.2
  4.3 6.0 %aligned.2 = (f32[128,256]{1,0:T(8,128)S(1)}, f32[256,256]{1,0:T(8,128)S(1)}, f32[128,512]{1,0:T(8,128)S(1)}, f32[256,128]{1,0:T(8,128)S(1)}, f32[256,128]{1,0:T...) custom-call(s32[1,2,4]{2,1,0:T(2,128)} %bitcast.10, s32[1,2,4]{2,1,0:T(2,128)} %bitcast.12, ...), custom_call_target="tpu_custom_call" | custom-call | flops 7800000000 | bytes 2097152 | tf_op jit(solution)/shard_map/aligned/pallas_call | solution.py:183
  10.4 4.7 %collective-permute-start.2 = (f32[256,256]{1,0:T(8,128)S(1)}, f32[256,256]{1,0:T(8,128)S(1)}, u32[]{:S(2)}, u32[]{:S(2)}) collective-permute-start(f32[256,256]{1,0:T(8,128)S(1)} %get-tuple-element.56), channel_id=1, source_target_pairs={{0,248},{8,0},{16,8},{24,16},{32,24},{40,32},{48,40},{56,48},{64,5... | collective-permute-start | bytes 786440 | tf_op jit(solution)/shard_map/ppermute | solution.py:457
  15.0 4.8 %collective-permute-start.1 = (f32[256,128]{1,0:T(8,128)S(1)}, f32[256,128]{1,0:T(8,128)S(1)}, u32[]{:S(2)}, u32[]{:S(2)}) collective-permute-start(f32[256,128]{1,0:T(8,128)S(1)} %get-tuple-element.55), channel_id=1, source_target_pairs={{0,7},{1,0},{2,1},{3,2},{4,3},{5,4},{6,5},{7,6},{8,15},{9,8},{10,9... | collective-permute-start | bytes 393224 | tf_op jit(solution)/shard_map/ppermute | solution.py:459
  19.8 1.4 %collective-permute-start.3 = (f32[256,128]{1,0:T(8,128)S(1)}, f32[256,128]{1,0:T(8,128)S(1)}, u32[]{:S(2)}, u32[]{:S(2)}) collective-permute-start(f32[256,128]{1,0:T(8,128)S(1)} %get-tuple-element.57), channel_id=1, source_target_pairs={{0,255},{1,248},{2,249},{3,250},{4,251},{5,252},{6,253},{7,254},{8... | collective-permute-start | bytes 393224 | tf_op jit(solution)/shard_map/ppermute | solution.py:465
  21.2 0.0 collective-permute-done.refs_4_.refs_3_
  21.2 0.0 copy-done.2
  21.2 0.0 copy-start.3
  21.2 0.0 copy-start.4
  21.2 4.9 %aligned.3 = (f32[128,768]{1,0:T(8,128)S(1)}, f32[128,512]{1,0:T(8,128)S(1)}, f32[1,512,512]{2,1,0:T(8,128)S(1)}) custom-call(s32[1,2,4]{2,1,0:T(2,128)} %bitcast.11, s32[1,2,4]{2,1,0:T(2,128)} %bitcast.13, f32[256,1024]{1,0:T(8,128)S(1)} %copy-done.2, f32[2,512,512]{2,1,0:T(8,128)S(1)} %get-tuple-element.49.boxes, f32[1,4,512,512]{3,2,1,0:T(8,128)} %refs_8_.1, ...), custom_call_target="tpu_custom_call" | custom-call | flops 7800000000 | bytes 2097152 | tf_op jit(solution)/shard_map/aligned/pallas_call | solution.py:183
  26.2 0.3 collective-permute-start.4
  26.4 0.0 collective-permute-done.1.refs_1_
  26.5 0.0 collective-permute-done.3.refs_3_
  26.5 0.0 collective-permute-done.2.refs_2_.refs_5_
  26.5 0.0 copy-done.3
  26.5 0.0 copy-done.4
  26.5 4.8 %shifted.3 = (f32[648,640]{1,0:T(8,128)S(1)}, f32[272,256]{1,0:T(8,128)S(1)}, f32[136,256]{1,0:T(8,128)S(1)}, f32[8,256]{1,0:T(8,128)S(1)}, f32[2,512,512]{2,1,0:T(8,128)S(1)}) custom-call(s32[1,2,4]{2,1,0:T(2,128)S(1)} %bitcast.4, s32[1,2,4]{2,1,0:T(2,128)S(1)} %bitcast.7, f32[1,512,512]{2,1,0:T(8,128)S(1)} %get-tuple-element.53.box_ref, ...), custom_call_target="tpu_custom_call" | custom-call | flops 5699999744 | bytes 1048576 | tf_op jit(solution)/shard_map/shifted/pallas_call | solution.py:311
  31.3 1.8 %collective-permute-start.5 = (f32[272,256]{1,0:T(8,128)S(1)}, f32[272,256]{1,0:T(8,128)S(1)}, u32[]{:S(2)}, u32[]{:S(2)}) collective-permute-start(f32[272,256]{1,0:T(8,128)S(1)} %get-tuple-element.65), channel_id=1, source_target_pairs={{0,8},{8,16},{16,24},{24,32},{32,40},{40,48},{48,56},{56,64},{64,7... | collective-permute-start | bytes 835592 | tf_op jit(solution)/shard_map/ppermute | solution.py:457
  33.1 0.0 collective-permute-start.6
  33.1 0.5 collective-permute-done.4.refs_2_.refs_1_
  33.6 6.1 %shifted.4 = (f32[648,1152]{1,0:T(8,128)S(1)}, f32[272,512]{1,0:T(8,128)S(1)}, f32[136,512]{1,0:T(8,128)S(1)}, f32[8,768]{1,0:T(8,128)S(1)}, f32[1,512,512]{2,1,0:T(8,128)S(1)}) custom-call(s32[1,2,4]{2,1,0:T(2,128)S(1)} %bitcast.5, s32[1,2,4]{2,1,0:T(2,128)S(1)} %bitcast.8, f32[2,512,512]{2,1,0:T(8,128)S(1)} %get-tuple-element.58.box_ref, ...), custom_call_target="tpu_custom_call" | custom-call | flops 11399999488 | bytes 2097152 | tf_op jit(solution)/shard_map/shifted/pallas_call | solution.py:311
  39.7 0.1 collective-permute-start.7
  39.8 0.3 collective-permute-start.9
  40.1 1.9 %collective-permute-done.6.refs_2_ = f32[136,256]{1,0:T(8,128)S(1)} collective-permute-done((f32[136,256]{1,0:T(8,128)S(1)}, f32[136,256]{1,0:T(8,128)S(1)}, u32[]{:S(2)}, u32[]{:S(2)}) %collective-permute-start.6) | collective-permute-done | bytes 139296 | tf_op jit(solution)/shard_map/ppermute | solution.py:457
  42.0 0.0 collective-permute-done.5.refs_1_
  42.0 3.8 %shifted.5 = (f32[648,640]{1,0:T(8,128)S(1)}, f32[272,640]{1,0:T(8,128)S(1)}, f32[136,640]{1,0:T(8,128)S(1)}, f32[8,640]{1,0:T(8,128)S(1)}) custom-call(s32[1,2,4]{2,1,0:T(2,128)S(1)} %bitcast.6, s32[1,2,4]{2,1,0:T(2,128)S(1)} %bitcast.9, f32[1,512,512]{2,1,0:T(8,128)S(1)} %get-tuple-element.63.box_ref, f32[904,128]{1,0:T(8,128)S(1)} %get-tuple-element.51.refs_0_.base_ref, ...), custom_call_target="tpu_custom_call" | custom-call | flops 2100000000 | bytes 1048576 | tf_op jit(solution)/shard_map/shifted/pallas_call | solution.py:311
  45.8 4.4 %collective-permute-done.7.refs_5_ = f32[136,512]{1,0:T(8,128)S(1)} collective-permute-done((f32[136,512]{1,0:T(8,128)S(1)}, f32[136,512]{1,0:T(8,128)S(1)}, u32[]{:S(2)}, u32[]{:S(2)}) %collective-permute-start.7) | collective-permute-done | bytes 278560 | tf_op jit(solution)/shard_map/ppermute | solution.py:457
  50.2 1.3 %collective-permute-start.8 = (f32[136,640]{1,0:T(8,128)S(1)}, f32[136,640]{1,0:T(8,128)S(1)}, u32[]{:S(2)}, u32[]{:S(2)}) collective-permute-start(f32[136,640]{1,0:T(8,128)S(1)} %get-tuple-element.72), channel_id=1, source_target_pairs={{0,8},{16,24},{32,40},{48,56},{64,72},{80,88},{96,104},{112,120},{... | collective-permute-start | bytes 1044488 | tf_op jit(solution)/shard_map/ppermute | solution.py:525
  51.5 1.3 %collective-permute-start.10 = (f32[8,768]{1,0:T(8,128)S(1)}, f32[8,768]{1,0:T(8,128)S(1)}, u32[]{:S(2)}, u32[]{:S(2)}) collective-permute-start(f32[8,768]{1,0:T(8,128)S(1)} %get-tuple-element.74), channel_id=1, source_target_pairs={{0,248},{8,0},{16,8},{24,16},{32,24},{40,32},{48,40},{56,48},{64,5... | collective-permute-start | bytes 73736 | tf_op jit(solution)/shard_map/ppermute | solution.py:457
  52.8 3.8 %collective-permute-done.10.refs_6_ = f32[8,768]{1,0:T(8,128)S(1)} collective-permute-done((f32[8,768]{1,0:T(8,128)S(1)}, f32[8,768]{1,0:T(8,128)S(1)}, u32[]{:S(2)}, u32[]{:S(2)}) %collective-permute-start.10) | collective-permute-done | bytes 24608 | tf_op jit(solution)/shard_map/ppermute | solution.py:457
  56.6 0.0 collective-permute-done.9.refs_4_
  56.6 0.0 collective-permute-done.8
  56.6 0.1 add_dynamic-update-slice_fusion
  56.6 0.0 copy-start
  56.7 0.0 copy-start.1
  56.7 0.1 collective-permute-start.11
  56.8 1.5 %edges.1 = (f32[256,384]{1,0:T(8,128)S(1)}, f32[256,128]{1,0:T(8,128)S(1)}, f32[264,384]{1,0:T(8,128)S(1)}, f32[8,256]{1,0:T(8,128)S(1)}) custom-call(f32[648,640]{1,0:T(8,128)S(1)} %get-tuple-element.61.refs_6_.refs_0_, f32[272,256]{1,0:T(8,128)S(1)} %collective-permute-done.5.refs_1_, f32[136,256]{1,0:T(8,128)S(1)} %collective-permute-done.6.refs_2_, ...), custom_call_target="tpu_custom_call" | custom-call | tf_op jit(solution)/shard_map/edges/pallas_call | solution.py:382
  58.3 1.0 %collective-permute-start.14 = (f32[264,384]{1,0:T(8,128)S(1)}, f32[264,384]{1,0:T(8,128)S(1)}, u32[]{:S(2)}, u32[]{:S(2)}) collective-permute-start(f32[264,384]{1,0:T(8,128)S(1)} %get-tuple-element.79), channel_id=1, source_target_pairs={{0,1},{1,2},{2,3},{3,4},{4,5},{5,6},{6,7},{7,0},{8,9},{9,10},{10,1... | collective-permute-start | bytes 1216520 | tf_op jit(solution)/shard_map/ppermute | solution.py:459
  59.3 1.9 %collective-permute-start.12 = (f32[136,640]{1,0:T(8,128)S(1)}, f32[136,640]{1,0:T(8,128)S(1)}, u32[]{:S(2)}, u32[]{:S(2)}) collective-permute-start(f32[136,640]{1,0:T(8,128)S(1)} %get-tuple-element.72), channel_id=1, source_target_pairs={{8,24},{24,40},{40,56},{56,72},{72,88},{88,104},{104,120},{120,136... | collective-permute-start | bytes 1044488 | tf_op jit(solution)/shard_map/ppermute | solution.py:527
  61.2 0.1 collective-permute-start.13
  61.3 4.2 %collective-permute-start.15 = (f32[8,256]{1,0:T(8,128)S(1)}, f32[8,256]{1,0:T(8,128)S(1)}, u32[]{:S(2)}, u32[]{:S(2)}) collective-permute-start(f32[8,256]{1,0:T(8,128)S(1)} %get-tuple-element.80), channel_id=1, source_target_pairs={{0,7},{1,0},{2,1},{3,2},{4,3},{5,4},{6,5},{7,6},{8,15},{9,8},{10,9... | collective-permute-start | bytes 24584 | tf_op jit(solution)/shard_map/ppermute | solution.py:459
  65.5 13.6 %collective-permute-done.13.back1 = f32[8,640]{1,0:T(8,128)S(1)} collective-permute-done((f32[8,640]{1,0:T(8,128)S(1)}, f32[8,640]{1,0:T(8,128)S(1)}, u32[]{:S(2)}, u32[]{:S(2)}) %collective-permute-start.13) | collective-permute-done | bytes 20512 | tf_op jit(solution)/shard_map/ppermute | solution.py:457
  79.1 0.0 collective-permute-done.12.far1
  79.1 0.0 collective-permute-done.15.west_ref
  79.1 0.0 collective-permute-done.14.east_ref
  79.1 0.0 collective-permute-done.11.next1
  79.1 0.0 copy-done
  79.2 0.0 copy-done.1
  79.2 2.6 %final.1 = f32[256,1024]{1,0:T(8,128)} custom-call(f32[648,640]{1,0:T(8,128)S(1)} %get-tuple-element.68.canvas1, f32[272,640]{1,0:T(8,128)S(1)} %collective-permute-done.11.next1, f32[136,640]{1,0:T(8,128)S(1)} %collective-permute-done.12.far1, f32[8,640]{1,0:T(8,128)S(1)} %collective-permute-done.13.back1, f32[256,384]{1,0:T(8,128)S(1)} %get-tuple-element.77.main_ref, ...), custom_call_target="tpu_custom_call" | custom-call | tf_op jit(solution)/shard_map/final/pallas_call | solution.py:438
Async XLA Ops:
  1.0 20.2 %collective-permute-start = (f32[128,768]{1,0:T(8,128)S(1)}, f32[128,768]{1,0:T(8,128)S(1)}, u32[]{:S(2)}, u32[]{:S(2)}) collective-permute-start(f32[128,768]{1,0:T(8,128)S(1)} %slice.22), channel_id=1, source_target_pairs={{0,248},{8,0},{16,8},{24,16},{32,24},{40,32},{48,40},{56,48},{64,5... | collective-permute-start | bytes 1179656 | tf_op jit(solution)/shard_map/ppermute | solution.py:457
  4.3 16.9 %copy-start.2 = (f32[256,1024]{1,0:T(8,128)S(1)}, f32[256,1024]{1,0:T(8,128)}, u32[]{:S(2)}) copy-start(f32[256,1024]{1,0:T(8,128)} %refs_2_.1) | copy-start | bytes 3145732
  10.4 16.1 %collective-permute-start.2 = (f32[256,256]{1,0:T(8,128)S(1)}, f32[256,256]{1,0:T(8,128)S(1)}, u32[]{:S(2)}, u32[]{:S(2)}) collective-permute-start(f32[256,256]{1,0:T(8,128)S(1)} %get-tuple-element.56), channel_id=1, source_target_pairs={{0,248},{8,0},{16,8},{24,16},{32,24},{40,32},{48,40},{56,48},{64,5... | collective-permute-start | bytes 786440 | tf_op jit(solution)/shard_map/ppermute | solution.py:457
  15.0 11.4 %collective-permute-start.1 = (f32[256,128]{1,0:T(8,128)S(1)}, f32[256,128]{1,0:T(8,128)S(1)}, u32[]{:S(2)}, u32[]{:S(2)}) collective-permute-start(f32[256,128]{1,0:T(8,128)S(1)} %get-tuple-element.55), channel_id=1, source_target_pairs={{0,7},{1,0},{2,1},{3,2},{4,3},{5,4},{6,5},{7,6},{8,15},{9,8},{10,9... | collective-permute-start | bytes 393224 | tf_op jit(solution)/shard_map/ppermute | solution.py:459
  19.8 6.6 %collective-permute-start.3 = (f32[256,128]{1,0:T(8,128)S(1)}, f32[256,128]{1,0:T(8,128)S(1)}, u32[]{:S(2)}, u32[]{:S(2)}) collective-permute-start(f32[256,128]{1,0:T(8,128)S(1)} %get-tuple-element.57), channel_id=1, source_target_pairs={{0,255},{1,248},{2,249},{3,250},{4,251},{5,252},{6,253},{7,254},{8... | collective-permute-start | bytes 393224 | tf_op jit(solution)/shard_map/ppermute | solution.py:465
  21.2 5.3 %copy-start.3 = (s32[1,4,2]{1,2,0:T(2,128)S(1)}, s32[1,4,2]{1,2,0:T(2,128)}, u32[]{:S(2)}) copy-start(s32[1,4,2]{1,2,0:T(2,128)} %param.16) | copy-start | bytes 100
  21.2 5.3 %copy-start.4 = (s32[1,4,2]{1,2,0:T(2,128)S(1)}, s32[1,4,2]{1,2,0:T(2,128)}, u32[]{:S(2)}) copy-start(s32[1,4,2]{1,2,0:T(2,128)} %param.17) | copy-start | bytes 100
  26.2 7.5 %collective-permute-start.4 = (f32[128,768]{1,0:T(8,128)S(1)}, f32[128,768]{1,0:T(8,128)S(1)}, u32[]{:S(2)}, u32[]{:S(2)}) collective-permute-start(f32[128,768]{1,0:T(8,128)S(1)} %get-tuple-element.60), channel_id=1, source_target_pairs={{0,248},{8,0},{16,8},{24,16},{32,24},{40,32},{48,40},{56,48},{64,5... | collective-permute-start | bytes 1179656 | tf_op jit(solution)/shard_map/ppermute | solution.py:457
  31.3 10.7 %collective-permute-start.5 = (f32[272,256]{1,0:T(8,128)S(1)}, f32[272,256]{1,0:T(8,128)S(1)}, u32[]{:S(2)}, u32[]{:S(2)}) collective-permute-start(f32[272,256]{1,0:T(8,128)S(1)} %get-tuple-element.65), channel_id=1, source_target_pairs={{0,8},{8,16},{16,24},{24,32},{32,40},{40,48},{48,56},{56,64},{64,7... | collective-permute-start | bytes 835592 | tf_op jit(solution)/shard_map/ppermute | solution.py:457
  33.1 8.9 %collective-permute-start.6 = (f32[136,256]{1,0:T(8,128)S(1)}, f32[136,256]{1,0:T(8,128)S(1)}, u32[]{:S(2)}, u32[]{:S(2)}) collective-permute-start(f32[136,256]{1,0:T(8,128)S(1)} %get-tuple-element.66), channel_id=1, source_target_pairs={{0,16},{8,24},{16,32},{24,40},{32,48},{40,56},{48,64},{56,72},{64,... | collective-permute-start | bytes 417800 | tf_op jit(solution)/shard_map/ppermute | solution.py:457
  39.7 10.5 %collective-permute-start.7 = (f32[136,512]{1,0:T(8,128)S(1)}, f32[136,512]{1,0:T(8,128)S(1)}, u32[]{:S(2)}, u32[]{:S(2)}) collective-permute-start(f32[136,512]{1,0:T(8,128)S(1)} %get-tuple-element.71), channel_id=1, source_target_pairs={{0,16},{8,24},{16,32},{24,40},{32,48},{40,56},{48,64},{56,72},{64,... | collective-permute-start | bytes 835592 | tf_op jit(solution)/shard_map/ppermute | solution.py:457
  39.8 16.7 %collective-permute-start.9 = (f32[272,512]{1,0:T(8,128)S(1)}, f32[272,512]{1,0:T(8,128)S(1)}, u32[]{:S(2)}, u32[]{:S(2)}) collective-permute-start(f32[272,512]{1,0:T(8,128)S(1)} %get-tuple-element.73), channel_id=1, source_target_pairs={{0,8},{8,16},{16,24},{24,32},{32,40},{40,48},{48,56},{56,64},{64,7... | collective-permute-start | bytes 1671176 | tf_op jit(solution)/shard_map/ppermute | solution.py:457
  50.2 6.4 %collective-permute-start.8 = (f32[136,640]{1,0:T(8,128)S(1)}, f32[136,640]{1,0:T(8,128)S(1)}, u32[]{:S(2)}, u32[]{:S(2)}) collective-permute-start(f32[136,640]{1,0:T(8,128)S(1)} %get-tuple-element.72), channel_id=1, source_target_pairs={{0,8},{16,24},{32,40},{48,56},{64,72},{80,88},{96,104},{112,120},{... | collective-permute-start | bytes 1044488 | tf_op jit(solution)/shard_map/ppermute | solution.py:525
  51.5 5.1 %collective-permute-start.10 = (f32[8,768]{1,0:T(8,128)S(1)}, f32[8,768]{1,0:T(8,128)S(1)}, u32[]{:S(2)}, u32[]{:S(2)}) collective-permute-start(f32[8,768]{1,0:T(8,128)S(1)} %get-tuple-element.74), channel_id=1, source_target_pairs={{0,248},{8,0},{16,8},{24,16},{32,24},{40,32},{48,40},{56,48},{64,5... | collective-permute-start | bytes 73736 | tf_op jit(solution)/shard_map/ppermute | solution.py:457
  56.6 22.5 %copy-start = (bf16[512,256]{1,0:T(8,128)(2,1)S(1)}, bf16[512,256]{1,0:T(8,128)(2,1)}, u32[]{:S(2)}) copy-start(bf16[512,256]{1,0:T(8,128)(2,1)} %constant.32.clone.high_ref) | copy-start | bytes 786436
  56.7 22.5 %copy-start.1 = (bf16[512,256]{1,0:T(8,128)(2,1)S(1)}, bf16[512,256]{1,0:T(8,128)(2,1)}, u32[]{:S(2)}) copy-start(bf16[512,256]{1,0:T(8,128)(2,1)} %constant.33.clone.low_ref) | copy-start | bytes 786436
  56.7 22.5 %collective-permute-start.11 = (f32[272,640]{1,0:T(8,128)S(1)}, f32[272,640]{1,0:T(8,128)S(1)}, u32[]{:S(2)}, u32[]{:S(2)}) collective-permute-start(f32[272,640]{1,0:T(8,128)S(1)} %add_dynamic-update-slice_fusion), channel_id=1, source_target_pairs={{0,8},{8,16},{16,24},{24,32},{32,40},{40,48},{48,56},{56,64},{64,7... | collective-permute-start | bytes 2088968 | tf_op jit(solution)/shard_map/ppermute | solution.py:457
  58.3 20.9 %collective-permute-start.14 = (f32[264,384]{1,0:T(8,128)S(1)}, f32[264,384]{1,0:T(8,128)S(1)}, u32[]{:S(2)}, u32[]{:S(2)}) collective-permute-start(f32[264,384]{1,0:T(8,128)S(1)} %get-tuple-element.79), channel_id=1, source_target_pairs={{0,1},{1,2},{2,3},{3,4},{4,5},{5,6},{6,7},{7,0},{8,9},{9,10},{10,1... | collective-permute-start | bytes 1216520 | tf_op jit(solution)/shard_map/ppermute | solution.py:459
  59.3 19.9 %collective-permute-start.12 = (f32[136,640]{1,0:T(8,128)S(1)}, f32[136,640]{1,0:T(8,128)S(1)}, u32[]{:S(2)}, u32[]{:S(2)}) collective-permute-start(f32[136,640]{1,0:T(8,128)S(1)} %get-tuple-element.72), channel_id=1, source_target_pairs={{8,24},{24,40},{40,56},{56,72},{72,88},{88,104},{104,120},{120,136... | collective-permute-start | bytes 1044488 | tf_op jit(solution)/shard_map/ppermute | solution.py:527
  61.2 17.9 %collective-permute-start.13 = (f32[8,640]{1,0:T(8,128)S(1)}, f32[8,640]{1,0:T(8,128)S(1)}, u32[]{:S(2)}, u32[]{:S(2)}) collective-permute-start(f32[8,640]{1,0:T(8,128)S(1)} %get-tuple-element.76), channel_id=1, source_target_pairs={{0,248},{8,0},{16,8},{24,16},{32,24},{40,32},{48,40},{56,48},{64,5... | collective-permute-start | bytes 61448 | tf_op jit(solution)/shard_map/ppermute | solution.py:457
  61.3 17.9 %collective-permute-start.15 = (f32[8,256]{1,0:T(8,128)S(1)}, f32[8,256]{1,0:T(8,128)S(1)}, u32[]{:S(2)}, u32[]{:S(2)}) collective-permute-start(f32[8,256]{1,0:T(8,128)S(1)} %get-tuple-element.80), channel_id=1, source_target_pairs={{0,7},{1,0},{2,1},{3,2},{4,3},{5,4},{6,5},{7,6},{8,15},{9,8},{10,9... | collective-permute-start | bytes 24584 | tf_op jit(solution)/shard_map/ppermute | solution.py:459
